TPU v7x, 32 devices: a whole 2x2x4 slice. The times are simulated.
32 devices in a mesh: grp: 2 (over y), gx: 16 (over z, x, core).
Axes of the slice: x: 2, y: 2, z: 4, core: 2. Of those that a mesh axis runs over, the one named last changes fastest.
Arguments:
- voltages: bfloat16 [2, 512, 2, 1, 2, 16384], P('grp', 'gx'), may hold values from -6 to 6
- tile_of: int32 [2, 32768], P(None, 'gx'), may hold values from -1 to 1, as said below
- cell_of: int32 [2, 32768], P(None, 'gx'), may hold values from 0 to 511
Outputs:
- image: float32 [2, 2, 4096, 4096], P('grp', None, 'gx')
Inputs may be any that keep to these rules, and one draw needn't show every extreme that they name: `tile_of`: among the 2048 blocks of one coarse channel and one gx index, no tile is named more than 256 times, and one tile exactly 256 times; -1 marks blocks that no tile takes.
All inputs are finite; a program needn't handle non-finite values.
Results may differ from a plain program's by a relative error of at most 0.006.
Values may be sent and summed in bfloat16 or wider, within the bound.
No kernel may reach another device: no remote copies, remote signals or barrier semaphores. Data moves between devices by JAX's collectives and lax.ppermute only.
A program may use at most 128 MiB of HBM per device.

v0:
```python
import functools
import math

import jax
import jax.numpy as jnp
import numpy as np
from jax import lax
from jax.experimental import pallas as pl
from jax.experimental.pallas import tpu as pltpu
from jax.sharding import PartitionSpec as P

FRADIX = 128
AVG = 256
BR = 16
BC = 128
TRADIX = 64
TILE = 4096
SUB = 8
PACK = 16
F32 = jnp.float32
BF16 = jnp.bfloat16


def halves(matrix):
    high = matrix.astype(np.float32).astype(BF16)
    low = (matrix - high.astype(np.float64)).astype(np.float32).astype(BF16)
    return high, low


def complex_table(angle, scale):
    cos, sin = scale * np.cos(angle), scale * np.sin(angle)
    return np.stack([np.stack([cos, -sin]), np.stack([sin, cos])])


def turn(product, period, sign):
    return sign * 2.0 * np.pi / period * (product % period)


def spectra_tables(n_gx, out_dev):
    index = np.arange(FRADIX)
    first = complex_table(turn(np.outer(index, index), FRADIX, -1.0), 1.0 / FRADIX)
    first = first.transpose(0, 2, 3, 1).reshape(2 * FRADIX, 2 * FRADIX)
    high, low = halves(first)
    first = np.concatenate([high, low], axis=1)
    angle = turn(np.outer(index, index), FRADIX * FRADIX, -1.0)
    twist = np.stack([np.cos(angle), np.sin(angle)]).astype(np.float32)
    second = complex_table(turn(np.outer(index, index), FRADIX, -1.0), 1.0)
    low_count = FRADIX // (n_gx * out_dev)
    second = second.reshape(2, 2, n_gx, out_dev, low_count, FRADIX)
    second = second.transpose(3, 2, 0, 4, 1, 5).reshape(2 * FRADIX, 2 * FRADIX)
    high, low = halves(second)
    second = np.concatenate([high, low, high], axis=1)
    return first, twist, second


def row_tables(n_gx):
    cols = TILE // BC
    k1, w = np.arange(cols), np.arange(BC)
    angle = turn(np.outer(k1, w), TILE, 1.0)
    twist = np.stack([np.cos(angle), np.sin(angle)]).astype(np.float32)
    second = complex_table(turn(np.outer(w, w), BC, 1.0), 1.0 / math.sqrt(TILE))
    second = second.transpose(2, 0, 1, 3).reshape(2 * BC, 2 * BC)
    high, low = halves(second)
    return twist, np.concatenate([high, low, high], axis=1)


def column_tables(n_gx):
    count = TILE // BR
    blocks = count // n_gx
    index = np.arange(count)
    first = complex_table(turn(np.outer(index, index), count, 1.0), 1.0 / math.sqrt(TILE))
    first = first.reshape(2, 2, n_gx, blocks, count)
    first = first.transpose(2, 1, 3, 0, 4).reshape(2 * count, 2 * count)
    high, low = halves(first)
    angle = turn(np.outer(np.arange(BR), index), TILE, 1.0)
    twist = np.stack([np.cos(angle), np.sin(angle)]).astype(np.float32)
    return np.concatenate([high, low], axis=0), twist


def times(value, factor):
    re, im = value
    c, s = factor
    return (re * c - im * s, re * s + im * c)


def fixed_turn(value, step, count, sign):
    re, im = value
    step = step % count
    if step == 0:
        return value
    if 4 * step == count:
        return (-im, re) if sign > 0 else (im, -re)
    angle = sign * 2.0 * math.pi * step / count
    c, s = math.cos(angle), math.sin(angle)
    if 8 * step == count:
        return ((re - im) * c, (re + im) * c) if sign > 0 else ((re + im) * c, (im - re) * c)
    if 8 * step == 3 * count:
        h = abs(c)
        return ((-re - im) * h, (re - im) * h) if sign > 0 else ((im - re) * h, (-re - im) * h)
    return (re * c - im * s, re * s + im * c)


def butterflies(values, sign):
    count = len(values)
    if count == 1:
        return values
    even = butterflies(values[0::2], sign)
    odd = butterflies(values[1::2], sign)
    out = [None] * count
    for k in range(count // 2):
        turned = fixed_turn(odd[k], k, count, sign)
        out[k] = (even[k][0] + turned[0], even[k][1] + turned[1])
        out[k + count // 2] = (even[k][0] - turned[0], even[k][1] - turned[1])
    return out


def split_value(value):
    high = value.astype(BF16)
    return high, (value - high.astype(F32)).astype(BF16)


def dot_nt(left, right):
    return lax.dot_general(left, right, (((1,), (1,)), ((), ())), preferred_element_type=F32)


def dot_tn(left, right):
    return lax.dot_general(left, right, (((0,), (0,)), ((), ())), preferred_element_type=F32)


def spectra_kernel(n_gx, out_dev, v_ref, first_ref, twist_ref, second_ref, *rest):
    out_refs, scratch = rest[:out_dev], rest[out_dev]
    rows = 2 * FRADIX

    def one(i, carry):
        v = v_ref[i]
        y = jnp.dot(first_ref[...], jnp.concatenate([v, v], axis=0), preferred_element_type=F32)
        re, im = times((y[:FRADIX], y[FRADIX:]), (twist_ref[0], twist_ref[1]))
        high, low = split_value(jnp.concatenate([re, im], axis=1))
        z = dot_nt(second_ref[...], jnp.concatenate([high, high, low], axis=1))
        scratch[pl.ds(pl.multiple_of(i * rows, rows), rows), :] = z
        return carry

    lax.fori_loop(0, PACK, one, 0, unroll=2)
    per = rows // (out_dev * n_gx)
    for o in range(out_dev):
        for d in range(n_gx):
            for t in range(per):
                row = (o * n_gx + d) * per + t
                piece = scratch[pl.ds(row, PACK, stride=rows), :]
                out_refs[o][d, :, t * FRADIX : (t + 1) * FRADIX] = piece.astype(BF16)


def spectra_call(volts, n_gx, out_dev):
    inputs = volts.shape[0]
    first, twist, second = spectra_tables(n_gx, out_dev)
    depth = 2 * AVG
    whole = lambda x: pl.BlockSpec(x.shape, lambda i: (0,) * x.ndim)
    return pl.pallas_call(
        functools.partial(spectra_kernel, n_gx, out_dev),
        grid=(inputs // PACK,),
        in_specs=[
            pl.BlockSpec((PACK, 2 * FRADIX, FRADIX), lambda i: (i, 0, 0)),
            whole(first),
            whole(twist),
            whole(second),
        ],
        out_specs=[pl.BlockSpec((n_gx, PACK, depth), lambda i: (0, i, 0))] * out_dev,
        out_shape=[jax.ShapeDtypeStruct((n_gx, inputs, depth), BF16)] * out_dev,
        scratch_shapes=[pltpu.VMEM((PACK * 2 * FRADIX, FRADIX), F32)],
        name="spectra",
    )(volts, first, twist, second)


def gram_kernel(first_call, cells, factor, count_ref, list_ref, *rest):
    if first_call:
        mine_ref, other_ref, out_ref, vis, grid, sem = rest
    else:
        mine_ref, other_ref, in_ref, out_ref, vis, grid, sem = rest
    nin, depth = mine_ref.shape
    half = depth // 2
    if first_call:
        def clear(i, carry):
            grid[:, pl.ds(i * SUB, SUB)] = jnp.zeros((2, SUB, BR, BC), F32)
            return carry

        lax.fori_loop(0, cells // SUB, clear, 0)
    else:
        load = pltpu.make_async_copy(in_ref, grid, sem)
        load.start()
    panel = 2 * BC
    for which, x_ref in enumerate((mine_ref, other_ref)):
        def one(p, carry):
            base = pl.multiple_of(p * panel, panel)
            x = x_ref[pl.ds(base, panel), :]
            swapped = jnp.concatenate([x[:, half:], -x[:, :half]], axis=1)
            left = jnp.concatenate([x, swapped], axis=0)
            gram = (dot_nt(left, x_ref[...]) * factor).astype(BF16)
            for e in range(nin // BC):
                vis[0, e, pl.ds(base, panel), :] = gram[:panel, e * BC : (e + 1) * BC]
                vis[1, e, pl.ds(base, panel), :] = gram[panel:, e * BC : (e + 1) * BC]
            return carry

        lax.fori_loop(0, nin // panel, one, 0)
        if which == 0 and not first_call:
            load.wait()

        def place(s, carry):
            code = list_ref[which, s]
            cell = lax.rem(code, cells)
            block = lax.div(code, cells)
            e = lax.rem(block, nin // BC)
            row = pl.multiple_of(lax.div(block, nin // BC) * BR, BR)
            for part in range(2):
                grid[part, cell] += vis[part, e, pl.ds(row, BR), :].astype(F32)
            return carry

        lax.fori_loop(0, count_ref[which], place, 0)
    store = pltpu.make_async_copy(grid, out_ref, sem)
    store.start()
    store.wait()


def gram_call(counts, lists, mine, other, grid, cells, factor):
    first_call = grid is None
    shape = (2, cells, BR, BC)
    nin, depth = mine.shape
    any_spec = pl.BlockSpec(memory_space=pl.ANY)
    vmem = pl.BlockSpec(memory_space=pltpu.VMEM)
    smem = pl.BlockSpec(memory_space=pltpu.SMEM)
    args = (counts, lists, mine, other) + (() if first_call else (grid,))
    flops = 2 * 2 * 2 * nin * nin * depth
    return pl.pallas_call(
        functools.partial(gram_kernel, first_call, cells, factor),
        in_specs=[smem, smem, vmem, vmem] + ([] if first_call else [any_spec]),
        out_specs=any_spec,
        out_shape=jax.ShapeDtypeStruct(shape, F32),
        scratch_shapes=[
            pltpu.VMEM((2, nin // BC, nin, BC), BF16),
            pltpu.VMEM(shape, F32),
            pltpu.SemaphoreType.DMA,
        ],
        input_output_aliases={} if first_call else {4: 0},
        cost_estimate=pl.CostEstimate(flops=flops, transcendentals=0, bytes_accessed=2**24),
        name="gram",
    )(*args)


def row_first_kernel(grid_ref, twist_ref, high_ref, low_ref, scratch):
    cols = TILE // BC
    for h in range(BR // SUB):
        rows = slice(h * SUB, (h + 1) * SUB)
        values = [(grid_ref[0, 0, c, rows], grid_ref[1, 0, c, rows]) for c in range(cols)]
        values = butterflies(values, 1.0)
        for k in range(cols):
            factor = (twist_ref[0, k : k + 1, :], twist_ref[1, k : k + 1, :])
            re, im = times(values[k], factor)
            at = slice(k * BR + h * SUB, k * BR + (h + 1) * SUB)
            scratch[at, :BC] = re
            scratch[at, BC:] = im
    high, low = split_value(scratch[...])
    high_ref[0] = high
    low_ref[0] = low


def row_first_call(grid, twist):
    _, blocks, cols, _, _ = grid.shape
    shape = jax.ShapeDtypeStruct((blocks, cols * BR, 2 * BC), BF16)
    out = pl.BlockSpec((1, cols * BR, 2 * BC), lambda i: (i, 0, 0))
    return pl.pallas_call(
        row_first_kernel,
        grid=(blocks,),
        in_specs=[
            pl.BlockSpec((2, 1, cols, BR, BC), lambda i: (0, i, 0, 0, 0)),
            pl.BlockSpec(twist.shape, lambda i: (0, 0, 0)),
        ],
        out_specs=[out, out],
        out_shape=[shape, shape],
        scratch_shapes=[pltpu.VMEM((cols * BR, 2 * BC), F32)],
        name="row_first",
    )(grid, twist)


def row_second_kernel(high_ref, low_ref, second_ref, out_ref, scratch):
    blocks, lanes, _ = high_ref.shape
    rows = 2 * BC

    def one(b, carry):
        for u in range(2):
            high, low = high_ref[2 * b + u], low_ref[2 * b + u]
            z = dot_nt(second_ref[...], jnp.concatenate([high, high, low], axis=1))
            scratch[pl.ds(pl.multiple_of((2 * b + u) * rows, rows), rows), :] = z
        return carry

    lax.fori_loop(0, blocks // 2, one, 0)
    n_gx, lows, _, _ = out_ref.shape
    for d in range(n_gx):
        for k in range(lows):
            for part in range(2):
                row = (d * lows + k) * 2 + part
                piece = scratch[pl.ds(row, blocks, stride=rows), :]
                out_ref[d, k, part * blocks : (part + 1) * blocks, :] = piece.astype(BF16)


def row_second_call(high, low, second, n_gx, chunk):
    blocks = high.shape[0]
    lanes = SUB * BR
    lows = BC // n_gx
    take = pl.BlockSpec((blocks, lanes, 2 * BC), lambda i: (0, chunk, 0))
    return pl.pallas_call(
        row_second_kernel,
        grid=(1,),
        in_specs=[take, take, pl.BlockSpec(second.shape, lambda i: (0, 0))],
        out_specs=pl.BlockSpec((n_gx, lows, 2 * blocks, lanes), lambda i: (0, 0, 0, 0)),
        out_shape=jax.ShapeDtypeStruct((n_gx, lows, 2 * blocks, lanes), BF16),
        scratch_shapes=[pltpu.VMEM((blocks * 2 * BC, lanes), F32)],
        cost_estimate=pl.CostEstimate(flops=2**31, transcendentals=0, bytes_accessed=2**22),
        name="row_second",
    )(high, low, second)


def column_kernel(alias, data_ref, first_ref, twist_ref, *rest):
    out_ref, scratch = rest[-2], rest[-1]
    n_gx, _, rows, lanes = data_ref.shape
    data = data_ref[:, 0].reshape(n_gx * rows, lanes)
    mixed = dot_tn(jnp.concatenate([data, data], axis=0), first_ref[...])
    count = TILE // BR
    for b in range(2 * count // BC):
        scratch[b * lanes : (b + 1) * lanes, :] = mixed[:, b * BC : (b + 1) * BC]
    for b in range(count // BC):
        values = []
        for r in range(BR):
            value = (
                scratch[pl.ds(b * lanes + r, SUB, stride=BR), :],
                scratch[pl.ds((count // BC + b) * lanes + r, SUB, stride=BR), :],
            )
            lane = slice(b * BC, (b + 1) * BC)
            values.append(times(value, (twist_ref[0, r : r + 1, lane], twist_ref[1, r : r + 1, lane])))
        values = butterflies(values, 1.0)
        for k in range(BR):
            lane = slice(k * count + b * BC, k * count + (b + 1) * BC)
            out_ref[0, 0, 0, :, lane] = values[k][0]
            out_ref[1, 0, 0, :, lane] = values[k][1]


def column_call(data, first, twist, image, chunk, chunks):
    n_gx, lows, rows, lanes = data.shape
    alias = image is not None
    shape = (2, lows, chunks, SUB, TILE)
    return pl.pallas_call(
        functools.partial(column_kernel, alias),
        grid=(lows,),
        in_specs=[
            pl.BlockSpec((n_gx, 1, rows, lanes), lambda i: (0, i, 0, 0)),
            pl.BlockSpec(first.shape, lambda i: (0, 0)),
            pl.BlockSpec(twist.shape, lambda i: (0, 0, 0)),
        ]
        + ([pl.BlockSpec(memory_space=pl.ANY)] if alias else []),
        out_specs=pl.BlockSpec((2, 1, 1, SUB, TILE), lambda i: (0, i, chunk, 0, 0)),
        out_shape=jax.ShapeDtypeStruct(shape, F32),
        scratch_shapes=[pltpu.VMEM((2 * (TILE // BR) // BC * lanes, BC), F32)],
        input_output_aliases={3: 0} if alias else {},
        cost_estimate=pl.CostEstimate(flops=2**30, transcendentals=0, bytes_accessed=2**22),
        name="column",
    )(data, first, twist, *((image,) if alias else ()))


def work_lists(tile_of, cell_of, me, out_dev, cells):
    groups, blocks = tile_of.shape
    per = blocks // out_dev
    taken = (tile_of == me).reshape(groups, out_dev, per)
    number = taken.astype(jnp.int32)
    rank = jnp.cumsum(number, axis=2) - number
    slot = jnp.where(taken, rank, -1)
    code = jnp.arange(per, dtype=jnp.int32) * cells + cell_of.reshape(groups, out_dev, per)
    hit = jnp.arange(per, dtype=jnp.int32)[:, None] == slot[:, :, None, :]
    lists = jnp.sum(jnp.where(hit, code[:, :, None, :], 0), axis=3)
    return jnp.sum(number, axis=2), lists


def pair_plan(voltages, tile_of, cell_of):
    n_gx = lax.axis_size("gx")
    _, st_dev, pols, spectra, parts, fine = voltages.shape
    inputs = st_dev * pols
    out_dev = fine // (n_gx * AVG)
    cells = (TILE // n_gx // BR) * (TILE // BC)
    blocks = TILE // n_gx // BR
    cols = TILE // BC
    me = lax.axis_index("grp")
    counts, lists = work_lists(tile_of, cell_of, me, out_dev, cells)
    swap = jnp.where(me == 0, jnp.arange(2), jnp.arange(2)[::-1])
    counts, lists = jnp.take(counts, swap, axis=0), jnp.take(lists, swap, axis=0)

    volts = voltages.reshape(inputs, 2, FRADIX, FRADIX).transpose(0, 2, 1, 3)
    volts = volts.reshape(inputs, 2 * FRADIX, FRADIX)
    spec = spectra_call(volts, n_gx, out_dev)
    grid = None
    for o in range(out_dev):
        mine = lax.all_to_all(spec[o], "gx", split_axis=0, concat_axis=0, tiled=True)
        mine = mine.reshape(n_gx * inputs, 2 * AVG)
        other = lax.ppermute(mine, "grp", [(0, 1), (1, 0)])
        factor = 1.0 / math.sqrt(spectra * AVG)
        grid = gram_call(counts[:, o], lists[:, o], mine, other, grid, cells, factor)
    twist, second = row_tables(n_gx)
    high, low = row_first_call(grid.reshape(2, blocks, cols, BR, BC), twist)
    first, turned = column_tables(n_gx)
    image = None
    chunks = cols // SUB
    for chunk in range(chunks):
        rows = row_second_call(high, low, second, n_gx, chunk)
        data = lax.all_to_all(rows, "gx", split_axis=0, concat_axis=0, tiled=True)
        image = column_call(data, first, turned, image, chunk, chunks)
    return image.reshape(1, 2, TILE // n_gx, TILE)


def base_table(radix, sign):
    index = jnp.arange(radix, dtype=jnp.int32)
    product = index[:, None] * index[None, :] % radix
    angle = sign * 2.0 * math.pi / radix * product.astype(jnp.float32)
    return (jnp.cos(angle), jnp.sin(angle))


def twist_table(radix, sign):
    index = jnp.arange(radix, dtype=jnp.int32)
    product = index[:, None] * index[None, :]
    angle = sign * 2.0 * math.pi / (radix * radix) * product.astype(jnp.float32)
    return (jnp.cos(angle), jnp.sin(angle))


def complex_einsum(form, table, real_part, imag_part):
    cos_part, sin_part = table

    def product(left, right):
        return jnp.einsum(form, left, right, precision=lax.Precision.HIGH)

    new_real = product(cos_part, real_part) - product(sin_part, imag_part)
    new_imag = product(cos_part, imag_part) + product(sin_part, real_part)
    return (new_real, new_imag)


def fourier(real_part, imag_part, radix, sign, to_front):
    count = real_part.shape[0]
    real_part = real_part.reshape(count, radix, radix)
    imag_part = imag_part.reshape(count, radix, radix)
    table = base_table(radix, sign)
    real_part, imag_part = complex_einsum("ak,rab->rkb", table, real_part, imag_part)
    twist_cos, twist_sin = twist_table(radix, sign)
    twist_cos = twist_cos.T
    twist_sin = twist_sin.T
    turned_real = real_part * twist_cos - imag_part * twist_sin
    turned_imag = real_part * twist_sin + imag_part * twist_cos
    if to_front:
        form = "bj,rkb->jkr"
        shape = (radix * radix, count)
    else:
        form = "bj,rkb->rjk"
        shape = (count, radix * radix)
    out_real, out_imag = complex_einsum(form, table, turned_real, turned_imag)
    return (out_real.reshape(shape) / radix, out_imag.reshape(shape) / radix)


def operands(local):
    stations, pols, spectra, parts, channels = local.shape
    inputs = stations * pols
    nout = channels // AVG
    grouped = local.reshape(inputs, spectra, 2, nout, AVG).transpose(3, 0, 1, 2, 4)
    swapped = jnp.stack([grouped[:, :, :, 1], -grouped[:, :, :, 0]], axis=3)
    left = jnp.stack([grouped, swapped], axis=1).reshape(nout, 2 * inputs, spectra, 2 * AVG)
    right = grouped.reshape(nout, inputs, spectra, 2 * AVG)
    return (left, right)


def gram_all(local):
    left, right = operands(local)
    nout, rows_two, spectra, depth = left.shape
    left = left.reshape(nout, rows_two, spectra * depth)
    right = right.reshape(nout, rows_two // 2, spectra * depth)
    return jnp.einsum("oyk,ork->oyr", left, right, preferred_element_type=jnp.float32)


def pair_fits(gx_count, shape):
    lead, st_dev, pols, spectra, parts, fine = shape
    return (
        lead == 1
        and spectra == 1
        and fine == FRADIX * FRADIX
        and (st_dev * pols) % PACK == 0
        and fine % (gx_count * AVG) == 0
        and TILE // gx_count // BR == PACK
    )


def on_device(voltages, tile_of, cell_of):
    grp_count = lax.axis_size("grp")
    gx_count = lax.axis_size("gx")
    lead, st_dev, pols, spectra, parts, fine = voltages.shape
    if grp_count == 2 and pair_fits(gx_count, voltages.shape):
        return pair_plan(voltages, tile_of, cell_of)
    volts = voltages.reshape(st_dev * pols * spectra, 2, fine).astype(jnp.float32)
    spec_re, spec_im = fourier(volts[:, 0], volts[:, 1], FRADIX, -1.0, False)
    spec = jnp.stack([spec_re, spec_im], axis=1).astype(jnp.bfloat16)
    spec = spec.reshape(st_dev, pols, spectra, 2, fine)
    local = lax.all_to_all(spec, "gx", split_axis=4, concat_axis=0, tiled=True)
    gram = gram_all(local)
    factor = 1.0 / math.sqrt(spectra * AVG)
    out_dev = gram.shape[0]
    inputs = gram.shape[2]
    vis = (gram * factor).astype(jnp.bfloat16).reshape(out_dev, 2, inputs, inputs)
    width = 2 * BR * BC
    shaped = vis.reshape(out_dev, 2, inputs // BR, BR, inputs // BC, BC)
    blocks = shaped.transpose(0, 2, 4, 1, 3, 5).reshape(-1, width)
    count_blocks = blocks.shape[0]
    capacity = max(2, count_blocks // (4 * grp_count))
    slots = grp_count * capacity
    me = lax.axis_index("grp")
    groups = tile_of.shape[0]
    marked = (tile_of[:, None, :] == jnp.arange(grp_count, dtype=jnp.int32)[None, :, None]).astype(
        jnp.int32
    )
    rank_all = jnp.sum((jnp.cumsum(marked, axis=2) - marked) * marked, axis=1)
    my_tiles = lax.dynamic_index_in_dim(tile_of, me, 0, keepdims=False)
    my_rank = lax.dynamic_index_in_dim(rank_all, me, 0, keepdims=False)
    slot_id = jnp.where(my_tiles < 0, -1, my_tiles * capacity + my_rank)
    hits = jnp.arange(slots, dtype=jnp.int32)[:, None] == slot_id[None, :]
    filled = jnp.any(hits, axis=1)
    source = jnp.where(filled, jnp.argmax(hits, axis=1), count_blocks)
    padded = jnp.concatenate([blocks, jnp.zeros((1, width), jnp.bfloat16)], axis=0)
    outgoing = jnp.take(padded, source, axis=0)
    outgoing = outgoing.reshape(grp_count, capacity, width)
    arrived = lax.all_to_all(outgoing, "grp", split_axis=0, concat_axis=0, tiled=True)
    slab = TILE // gx_count
    row_blocks = slab // BR
    col_blocks = TILE // BC
    cells_count = row_blocks * col_blocks
    source_group = jnp.arange(groups, dtype=jnp.int32)[:, None]
    slot_flat = jnp.where(tile_of == me, source_group * capacity + rank_all, -1).reshape(-1)
    cell_flat = cell_of.reshape(-1)
    cell_hit = (jnp.arange(cells_count, dtype=jnp.int32)[:, None] == cell_flat[None, :]).astype(
        jnp.bfloat16
    )
    slot_hit = (jnp.arange(slots, dtype=jnp.int32)[:, None] == slot_flat[None, :]).astype(
        jnp.bfloat16
    )
    place = lax.dot_general(
        cell_hit, slot_hit, (((1,), (1,)), ((), ())), preferred_element_type=jnp.float32
    )
    place = place.astype(jnp.bfloat16)
    grid = jnp.dot(place, arrived.reshape(slots, width), preferred_element_type=jnp.float32)
    grid = (
        grid.reshape(row_blocks, col_blocks, 2, BR, BC)
        .transpose(2, 0, 3, 1, 4)
        .reshape(2, slab, TILE)
    )
    rows_re, rows_im = fourier(grid[0], grid[1], TRADIX, 1.0, True)
    rows = jnp.stack([rows_re, rows_im], axis=0).astype(jnp.bfloat16)
    columns = lax.all_to_all(rows, "gx", split_axis=1, concat_axis=2, tiled=True)
    kx_local = columns.shape[1]
    image_re, image_im = fourier(
        columns[0].astype(jnp.float32), columns[1].astype(jnp.float32), TRADIX, 1.0, False
    )
    image = jnp.stack([image_re, image_im], axis=0).reshape(1, 2, kx_local, TILE)
    return image


def solution(mesh):
    in_specs = (P("grp", "gx", None, None, None, None), P(None, "gx"), P(None, "gx"))
    out_specs = P("grp", None, "gx", None)
    return jax.shard_map(
        on_device, mesh=mesh, in_specs=in_specs, out_specs=out_specs, check_vma=False
    )
```

profile of v0, /device:TPU:13, one launch (start us, length us, event | category | flops | bytes accessed | tf_op | source)
XLA Modules:
  0.0 380.4 jit_solution(17480771449209036259)
XLA Ops:
  0.0 27.7 %spectra.1 = (bf16[16,64,512]{2,1,0:T(8,128)(2,1)}, bf16[16,64,512]{2,1,0:T(8,128)(2,1)}, bf16[16,64,512]{2,1,0:T(8,128)(2,1)}, bf16[16,64,512]{2,1,0:T(8,128)(2,1)}) custom-call(bf16[64,256,128]{2,1,0:T(8,128)(2,1)} %bitcast.27, bf16[256,512]{1,0:T(8,128)(2,1)} %constant.56.clone.first_ref, f32[2,128,128]{2,1,0:T(8,128)} %constant.57.clone.twist_ref, ...), custom_call_target="tpu_custom_call" | custom-call | tf_op jit(solution)/shard_map/spectra/pallas_call | solution.py:158
  27.7 31.9 %all_to_all.40 = bf16[16,64,512]{2,1,0:T(8,128)(2,1)S(1)} all-to-all(bf16[16,64,512]{2,1,0:T(8,128)(2,1)} %get-tuple-element.12), channel_id=1, replica_groups=mesh['grp'=2,'gx'=16] {'gx'}, dimensions={0} | all-to-all | bytes 2097152 | tf_op jit(solution)/shard_map/all_to_all | solution.py:398
  59.6 29.7 %all_to_all.41 = bf16[16,64,512]{2,1,0:T(8,128)(2,1)S(1)} all-to-all(bf16[16,64,512]{2,1,0:T(8,128)(2,1)} %get-tuple-element.13), channel_id=1, replica_groups=mesh['grp'=2,'gx'=16] {'gx'}, dimensions={0} | all-to-all | bytes 2097152 | tf_op jit(solution)/shard_map/all_to_all | solution.py:398
  89.3 4.4 %all-to-all-start.3 = ((bf16[16,64,512]{2,1,0:T(8,128)(2,1)}), bf16[16,64,512]{2,1,0:T(8,128)(2,1)S(1)}, u32[]{:S(2)}, u32[]{:S(2)}) async-start(bf16[16,64,512]{2,1,0:T(8,128)(2,1)} %get-tuple-element.14), calls=%async_computation.3 | async-start | bytes 2097152 | tf_op jit(solution)/shard_map/all_to_all | solution.py:398
  93.7 0.1 rev.3
  93.8 2.4 reduce-window.6
  96.3 0.3 slice_reduce_fusion
  96.6 0.4 reduce-window.9
  96.9 21.6 %all-to-all-done.3 = bf16[16,64,512]{2,1,0:T(8,128)(2,1)S(1)} async-done(((bf16[16,64,512]{2,1,0:T(8,128)(2,1)}), bf16[16,64,512]{2,1,0:T(8,128)(2,1)S(1)}, u32[]{:S(2)}, u32[]{:S(2)}) %all-to-all-start.3) | async-done | bytes 1048608 | tf_op jit(solution)/shard_map/all_to_all | solution.py:398
  118.6 1.0 copy-done.7
  119.6 4.8 %all-to-all-start = ((bf16[16,64,512]{2,1,0:T(8,128)(2,1)}), bf16[16,64,512]{2,1,0:T(8,128)(2,1)S(1)}, u32[]{:S(2)}, u32[]{:S(2)}) async-start(bf16[16,64,512]{2,1,0:T(8,128)(2,1)} %get-tuple-element.11), calls=%async_computation | async-start | bytes 2097152 | tf_op jit(solution)/shard_map/all_to_all | solution.py:398
  124.5 0.1 fusion
  124.6 0.6 gather_fusion
  125.2 0.3 collective-permute-start.3
  125.5 1.1 select_reduce_fusion
  126.6 1.3 collective-permute-start.2
  128.0 0.6 gather_fusion.1
  128.6 0.2 collective-permute-start.1
  128.8 0.8 slice_reduce_fusion.1
  129.6 0.6 slice_bitcast_fusion
  130.2 19.0 %all-to-all-done = bf16[16,64,512]{2,1,0:T(8,128)(2,1)S(1)} async-done(((bf16[16,64,512]{2,1,0:T(8,128)(2,1)}), bf16[16,64,512]{2,1,0:T(8,128)(2,1)S(1)}, u32[]{:S(2)}, u32[]{:S(2)}) %all-to-all-start) | async-done | bytes 1048608 | tf_op jit(solution)/shard_map/all_to_all | solution.py:398
  149.3 0.2 collective-permute-start
  149.5 0.4 collective-permute-done.3.rest_1_
  149.9 12.8 %gram.4.rest_2_ = f32[2,512,16,128]{3,2,1,0:T(8,128)} custom-call(s32[2]{0:T(128)} %get-tuple-element.17.count_ref, s32[2,512]{1,0:T(2,128)} %get-tuple-element.25.list_ref, bf16[1024,512]{1,0:T(8,128)(2,1)} %bitcast.29, bf16[1024,512]{1,0:T(8,128)(2,1)} %collective-permute-done.3.rest_1_), custom_call_target="tpu_custom_call" | custom-call | flops 4294967296 | bytes 16777216 | tf_op jit(solution)/shard_map/gram/pallas_call | solution.py:232
  162.7 9.7 %collective-permute-done.2.rest_1_ = bf16[1024,512]{1,0:T(8,128)(2,1)} collective-permute-done((bf16[1024,512]{1,0:T(8,128)(2,1)S(1)}, bf16[1024,512]{1,0:T(8,128)(2,1)}, u32[]{:S(2)}, u32[]{:S(2)}) %collective-permute-start.2) | collective-permute-done | bytes 1048608 | tf_op jit(solution)/shard_map/ppermute | solution.py:400
  172.4 12.7 %gram.5.rest_2_ = f32[2,512,16,128]{3,2,1,0:T(8,128)} custom-call(s32[2]{0:T(128)} %get-tuple-element.18.count_ref, s32[2,512]{1,0:T(2,128)} %get-tuple-element.26.list_ref, bf16[1024,512]{1,0:T(8,128)(2,1)} %bitcast.24, bf16[1024,512]{1,0:T(8,128)(2,1)} %collective-permute-done.2.rest_1_, ...), custom_call_target="tpu_custom_call", output_to_operand_aliasing={{}: (4, {})} | custom-call | flops 4294967296 | bytes 16777216 | tf_op jit(solution)/shard_map/gram/pallas_call | solution.py:232
  185.1 9.8 %collective-permute-done.1.rest_1_ = bf16[1024,512]{1,0:T(8,128)(2,1)} collective-permute-done((bf16[1024,512]{1,0:T(8,128)(2,1)S(1)}, bf16[1024,512]{1,0:T(8,128)(2,1)}, u32[]{:S(2)}, u32[]{:S(2)}) %collective-permute-start.1) | collective-permute-done | bytes 1048608 | tf_op jit(solution)/shard_map/ppermute | solution.py:400
  194.9 12.6 %gram.6.rest_2_ = f32[2,512,16,128]{3,2,1,0:T(8,128)} custom-call(s32[2]{0:T(128)} %get-tuple-element.19.count_ref, s32[2,512]{1,0:T(2,128)} %get-tuple-element.27.list_ref, bf16[1024,512]{1,0:T(8,128)(2,1)} %bitcast.22, bf16[1024,512]{1,0:T(8,128)(2,1)} %collective-permute-done.1.rest_1_, ...), custom_call_target="tpu_custom_call", output_to_operand_aliasing={{}: (4, {})} | custom-call | flops 4294967296 | bytes 16777216 | tf_op jit(solution)/shard_map/gram/pallas_call | solution.py:232
  207.4 9.9 %collective-permute-done.rest_1_ = bf16[1024,512]{1,0:T(8,128)(2,1)} collective-permute-done((bf16[1024,512]{1,0:T(8,128)(2,1)S(1)}, bf16[1024,512]{1,0:T(8,128)(2,1)}, u32[]{:S(2)}, u32[]{:S(2)}) %collective-permute-start) | collective-permute-done | bytes 1048608 | tf_op jit(solution)/shard_map/ppermute | solution.py:400
  217.3 12.2 %gram.7 = f32[2,512,16,128]{3,2,1,0:T(8,128)} custom-call(s32[2]{0:T(128)} %get-tuple-element.20.count_ref, s32[2,512]{1,0:T(2,128)} %get-tuple-element.28.list_ref, bf16[1024,512]{1,0:T(8,128)(2,1)} %bitcast.26, bf16[1024,512]{1,0:T(8,128)(2,1)} %collective-permute-done.rest_1_, f32[2,512,16,128]{3,2,1,0:T(8,128)} %gram.6.rest_2_), custom_call_target="tpu_custom_call", output_to_operand_aliasing={{}: (4, {})} | custom-call | flops 4294967296 | bytes 16777216 | tf_op jit(solution)/shard_map/gram/pallas_call | solution.py:232
  229.5 13.5 %row_first.1 = (bf16[16,512,256]{2,1,0:T(8,128)(2,1)}, bf16[16,512,256]{2,1,0:T(8,128)(2,1)}) custom-call(f32[2,16,32,16,128]{4,3,2,1,0:T(8,128)} %bitcast.20, f32[2,32,128]{2,1,0:T(8,128)} %constant.59.clone.twist_ref), custom_call_target="tpu_custom_call" | custom-call | tf_op jit(solution)/shard_map/row_first/pallas_call | solution.py:269
  243.0 6.7 %row_second.7 = bf16[16,8,32,128]{3,2,1,0:T(8,128)(2,1)} custom-call(bf16[16,512,256]{2,1,0:T(8,128)(2,1)} %get-tuple-element.15.high_ref, bf16[16,512,256]{2,1,0:T(8,128)(2,1)} %get-tuple-element.16.low_ref, bf16[256,768]{1,0:T(8,128)(2,1)} %constant.60.clone.second_ref), custom_call_target="tpu_custom_call" | custom-call | flops 2147483648 | bytes 4194304 | tf_op jit(solution)/shard_map/row_second/pallas_call | solution.py:309
  249.7 8.2 %all-to-all-start.7 = ((bf16[16,8,32,128]{3,2,1,0:T(8,128)(2,1)}), bf16[16,8,32,128]{3,2,1,0:T(8,128)(2,1)S(1)}, u32[]{:S(2)}, u32[]{:S(2)}) async-start(bf16[16,8,32,128]{3,2,1,0:T(8,128)(2,1)} %row_second.7), calls=%async_computation.7 | async-start | bytes 2097152 | tf_op jit(solution)/shard_map/all_to_all | solution.py:410
  257.8 6.8 %row_second.6 = bf16[16,8,32,128]{3,2,1,0:T(8,128)(2,1)} custom-call(bf16[16,512,256]{2,1,0:T(8,128)(2,1)} %get-tuple-element.15.high_ref, bf16[16,512,256]{2,1,0:T(8,128)(2,1)} %get-tuple-element.16.low_ref, bf16[256,768]{1,0:T(8,128)(2,1)} %constant.60.clone.second_ref), custom_call_target="tpu_custom_call" | custom-call | flops 2147483648 | bytes 4194304 | tf_op jit(solution)/shard_map/row_second/pallas_call | solution.py:309
  264.6 18.2 %all-to-all-done.7.data_ref = bf16[16,8,32,128]{3,2,1,0:T(8,128)(2,1)S(1)} async-done(((bf16[16,8,32,128]{3,2,1,0:T(8,128)(2,1)}), bf16[16,8,32,128]{3,2,1,0:T(8,128)(2,1)S(1)}, u32[]{:S(2)}, u32[]{:S(2)}) %all-to-all-start.7) | async-done | bytes 1048608 | tf_op jit(solution)/shard_map/all_to_all | solution.py:410
  282.8 4.8 %all-to-all-start.6 = ((bf16[16,8,32,128]{3,2,1,0:T(8,128)(2,1)}), bf16[16,8,32,128]{3,2,1,0:T(8,128)(2,1)S(1)}, u32[]{:S(2)}, u32[]{:S(2)}) async-start(bf16[16,8,32,128]{3,2,1,0:T(8,128)(2,1)} %row_second.6), calls=%async_computation.6 | async-start | bytes 2097152 | tf_op jit(solution)/shard_map/all_to_all | solution.py:410
  287.5 6.7 %row_second.5 = bf16[16,8,32,128]{3,2,1,0:T(8,128)(2,1)} custom-call(bf16[16,512,256]{2,1,0:T(8,128)(2,1)} %get-tuple-element.15.high_ref, bf16[16,512,256]{2,1,0:T(8,128)(2,1)} %get-tuple-element.16.low_ref, bf16[256,768]{1,0:T(8,128)(2,1)} %constant.60.clone.second_ref), custom_call_target="tpu_custom_call" | custom-call | flops 2147483648 | bytes 4194304 | tf_op jit(solution)/shard_map/row_second/pallas_call | solution.py:309
  294.2 18.3 %all-to-all-done.6.data_ref = bf16[16,8,32,128]{3,2,1,0:T(8,128)(2,1)S(1)} async-done(((bf16[16,8,32,128]{3,2,1,0:T(8,128)(2,1)}), bf16[16,8,32,128]{3,2,1,0:T(8,128)(2,1)S(1)}, u32[]{:S(2)}, u32[]{:S(2)}) %all-to-all-start.6) | async-done | bytes 1048608 | tf_op jit(solution)/shard_map/all_to_all | solution.py:410
  312.5 4.8 %all-to-all-start.5 = ((bf16[16,8,32,128]{3,2,1,0:T(8,128)(2,1)}), bf16[16,8,32,128]{3,2,1,0:T(8,128)(2,1)S(1)}, u32[]{:S(2)}, u32[]{:S(2)}) async-start(bf16[16,8,32,128]{3,2,1,0:T(8,128)(2,1)} %row_second.5), calls=%async_computation.5 | async-start | bytes 2097152 | tf_op jit(solution)/shard_map/all_to_all | solution.py:410
  317.2 6.8 %row_second.4 = bf16[16,8,32,128]{3,2,1,0:T(8,128)(2,1)} custom-call(bf16[16,512,256]{2,1,0:T(8,128)(2,1)} %get-tuple-element.15.high_ref, bf16[16,512,256]{2,1,0:T(8,128)(2,1)} %get-tuple-element.16.low_ref, bf16[256,768]{1,0:T(8,128)(2,1)} %constant.60.clone.second_ref), custom_call_target="tpu_custom_call" | custom-call | flops 2147483648 | bytes 4194304 | tf_op jit(solution)/shard_map/row_second/pallas_call | solution.py:309
  324.0 18.2 %all-to-all-done.5.data_ref = bf16[16,8,32,128]{3,2,1,0:T(8,128)(2,1)S(1)} async-done(((bf16[16,8,32,128]{3,2,1,0:T(8,128)(2,1)}), bf16[16,8,32,128]{3,2,1,0:T(8,128)(2,1)S(1)}, u32[]{:S(2)}, u32[]{:S(2)}) %all-to-all-start.5) | async-done | bytes 1048608 | tf_op jit(solution)/shard_map/all_to_all | solution.py:410
  342.1 4.8 %all-to-all-start.4 = ((bf16[16,8,32,128]{3,2,1,0:T(8,128)(2,1)}), bf16[16,8,32,128]{3,2,1,0:T(8,128)(2,1)S(1)}, u32[]{:S(2)}, u32[]{:S(2)}) async-start(bf16[16,8,32,128]{3,2,1,0:T(8,128)(2,1)} %row_second.4), calls=%async_computation.4 | async-start | bytes 2097152 | tf_op jit(solution)/shard_map/all_to_all | solution.py:410
  346.9 7.6 %column.4.rest_0_ = f32[2,8,4,8,4096]{4,3,2,1,0:T(8,128)} custom-call(bf16[16,8,32,128]{3,2,1,0:T(8,128)(2,1)} %copy-done.3, bf16[1024,512]{1,0:T(8,128)(2,1)} %constant.61.clone.first_ref, f32[2,16,256]{2,1,0:T(8,128)} %constant.62.clone.twist_ref), custom_call_target="tpu_custom_call" | custom-call | flops 1073741824 | bytes 4194304 | tf_op jit(solution)/shard_map/column/pallas_call | solution.py:349
  354.5 7.6 %column.5.rest_0_ = f32[2,8,4,8,4096]{4,3,2,1,0:T(8,128)} custom-call(bf16[16,8,32,128]{3,2,1,0:T(8,128)(2,1)} %copy-done.4, bf16[1024,512]{1,0:T(8,128)(2,1)} %constant.61.clone.first_ref, f32[2,16,256]{2,1,0:T(8,128)} %constant.62.clone.twist_ref, f32[2,8,4,8,4096]{4,3,2,1,0:T(8,128)} %column.4.rest_0_), custom_call_target="tpu_custom_call", output_to_operand_aliasing={{}: (3, {})} | custom-call | flops 1073741824 | bytes 4194304 | tf_op jit(solution)/shard_map/column/pallas_call | solution.py:349
  362.2 7.6 %column.6.rest_0_ = f32[2,8,4,8,4096]{4,3,2,1,0:T(8,128)} custom-call(bf16[16,8,32,128]{3,2,1,0:T(8,128)(2,1)} %copy-done.5, bf16[1024,512]{1,0:T(8,128)(2,1)} %constant.61.clone.first_ref, f32[2,16,256]{2,1,0:T(8,128)} %constant.62.clone.twist_ref, f32[2,8,4,8,4096]{4,3,2,1,0:T(8,128)} %column.5.rest_0_), custom_call_target="tpu_custom_call", output_to_operand_aliasing={{}: (3, {})} | custom-call | flops 1073741824 | bytes 4194304 | tf_op jit(solution)/shard_map/column/pallas_call | solution.py:349
  369.8 2.0 all-to-all-done.4.data_ref
  371.8 1.0 copy-done.6
  372.8 7.6 %column.7 = f32[2,8,4,8,4096]{4,3,2,1,0:T(8,128)} custom-call(bf16[16,8,32,128]{3,2,1,0:T(8,128)(2,1)} %copy-done.6, bf16[1024,512]{1,0:T(8,128)(2,1)} %constant.61.clone.first_ref, f32[2,16,256]{2,1,0:T(8,128)} %constant.62.clone.twist_ref, f32[2,8,4,8,4096]{4,3,2,1,0:T(8,128)} %column.6.rest_0_), custom_call_target="tpu_custom_call", output_to_operand_aliasing={{}: (3, {})} | custom-call | flops 1073741824 | bytes 4194304 | tf_op jit(solution)/shard_map/column/pallas_call | solution.py:349
  (30 shorter events, 0.4 us)
Async XLA Ops:
  0.0 93.8 %copy-start.8 = (s32[2,2048]{1,0:T(2,128)S(1)}, s32[2,2048]{1,0:T(2,128)}, u32[]{:S(2)}) copy-start(s32[2,2048]{1,0:T(2,128)} %param.12) | copy-start | bytes 49156
  0.0 93.8 %copy-start.9 = (s32[2,2048]{1,0:T(2,128)S(1)}, s32[2,2048]{1,0:T(2,128)}, u32[]{:S(2)}) copy-start(s32[2,2048]{1,0:T(2,128)} %param.11) | copy-start | bytes 49156
  59.6 103.1 %copy-start = (bf16[16,64,512]{2,1,0:T(8,128)(2,1)}, bf16[16,64,512]{2,1,0:T(8,128)(2,1)S(1)}, u32[]{:S(2)}) copy-start(bf16[16,64,512]{2,1,0:T(8,128)(2,1)S(1)} %all_to_all.40) | copy-start | bytes 3145732
  89.3 73.4 %copy-start.1 = (bf16[16,64,512]{2,1,0:T(8,128)(2,1)}, bf16[16,64,512]{2,1,0:T(8,128)(2,1)S(1)}, u32[]{:S(2)}) copy-start(bf16[16,64,512]{2,1,0:T(8,128)(2,1)S(1)} %all_to_all.41) | copy-start | bytes 3145732
  89.3 29.3 %all-to-all-start.3 = ((bf16[16,64,512]{2,1,0:T(8,128)(2,1)}), bf16[16,64,512]{2,1,0:T(8,128)(2,1)S(1)}, u32[]{:S(2)}, u32[]{:S(2)}) async-start(bf16[16,64,512]{2,1,0:T(8,128)(2,1)} %get-tuple-element.14), calls=%async_computation.3 | async-start | bytes 2097152 | tf_op jit(solution)/shard_map/all_to_all | solution.py:398
  118.6 1.0 copy-start.7
  119.6 29.7 %all-to-all-start = ((bf16[16,64,512]{2,1,0:T(8,128)(2,1)}), bf16[16,64,512]{2,1,0:T(8,128)(2,1)S(1)}, u32[]{:S(2)}, u32[]{:S(2)}) async-start(bf16[16,64,512]{2,1,0:T(8,128)(2,1)} %get-tuple-element.11), calls=%async_computation | async-start | bytes 2097152 | tf_op jit(solution)/shard_map/all_to_all | solution.py:398
  125.2 24.7 %collective-permute-start.3 = (bf16[1024,512]{1,0:T(8,128)(2,1)}, bf16[1024,512]{1,0:T(8,128)(2,1)}, u32[]{:S(2)}, u32[]{:S(2)}) collective-permute-start(bf16[1024,512]{1,0:T(8,128)(2,1)} %bitcast.28), channel_id=1, source_target_pairs={{0,16},{16,0},{1,17},{17,1},{2,18},{18,2},{3,19},{19,3},{4,20},{20... | collective-permute-start | bytes 3145736 | tf_op jit(solution)/shard_map/ppermute | solution.py:400
  126.6 45.8 %collective-permute-start.2 = (bf16[1024,512]{1,0:T(8,128)(2,1)S(1)}, bf16[1024,512]{1,0:T(8,128)(2,1)}, u32[]{:S(2)}, u32[]{:S(2)}) collective-permute-start(bf16[1024,512]{1,0:T(8,128)(2,1)S(1)} %bitcast.23), channel_id=1, source_target_pairs={{0,16},{16,0},{1,17},{17,1},{2,18},{18,2},{3,19},{19,3},{4,20},{20... | collective-permute-start | bytes 3145736 | tf_op jit(solution)/shard_map/ppermute | solution.py:400
  128.6 66.3 %collective-permute-start.1 = (bf16[1024,512]{1,0:T(8,128)(2,1)S(1)}, bf16[1024,512]{1,0:T(8,128)(2,1)}, u32[]{:S(2)}, u32[]{:S(2)}) collective-permute-start(bf16[1024,512]{1,0:T(8,128)(2,1)S(1)} %bitcast.21), channel_id=1, source_target_pairs={{0,16},{16,0},{1,17},{17,1},{2,18},{18,2},{3,19},{19,3},{4,20},{20... | collective-permute-start | bytes 3145736 | tf_op jit(solution)/shard_map/ppermute | solution.py:400
  149.3 35.8 %copy-start.2 = (bf16[16,64,512]{2,1,0:T(8,128)(2,1)}, bf16[16,64,512]{2,1,0:T(8,128)(2,1)S(1)}, u32[]{:S(2)}) copy-start(bf16[16,64,512]{2,1,0:T(8,128)(2,1)S(1)} %all-to-all-done) | copy-start | bytes 3145732
  149.3 68.1 %collective-permute-start = (bf16[1024,512]{1,0:T(8,128)(2,1)S(1)}, bf16[1024,512]{1,0:T(8,128)(2,1)}, u32[]{:S(2)}, u32[]{:S(2)}) collective-permute-start(bf16[1024,512]{1,0:T(8,128)(2,1)S(1)} %bitcast.25), channel_id=1, source_target_pairs={{0,16},{16,0},{1,17},{17,1},{2,18},{18,2},{3,19},{19,3},{4,20},{20... | collective-permute-start | bytes 3145736 | tf_op jit(solution)/shard_map/ppermute | solution.py:400
  249.7 33.1 %all-to-all-start.7 = ((bf16[16,8,32,128]{3,2,1,0:T(8,128)(2,1)}), bf16[16,8,32,128]{3,2,1,0:T(8,128)(2,1)S(1)}, u32[]{:S(2)}, u32[]{:S(2)}) async-start(bf16[16,8,32,128]{3,2,1,0:T(8,128)(2,1)} %row_second.7), calls=%async_computation.7 | async-start | bytes 2097152 | tf_op jit(solution)/shard_map/all_to_all | solution.py:410
  282.8 41.2 %copy-start.3 = (bf16[16,8,32,128]{3,2,1,0:T(8,128)(2,1)}, bf16[16,8,32,128]{3,2,1,0:T(8,128)(2,1)S(1)}, u32[]{:S(2)}) copy-start(bf16[16,8,32,128]{3,2,1,0:T(8,128)(2,1)S(1)} %all-to-all-done.7.data_ref) | copy-start | bytes 3145732
  282.8 29.7 %all-to-all-start.6 = ((bf16[16,8,32,128]{3,2,1,0:T(8,128)(2,1)}), bf16[16,8,32,128]{3,2,1,0:T(8,128)(2,1)S(1)}, u32[]{:S(2)}, u32[]{:S(2)}) async-start(bf16[16,8,32,128]{3,2,1,0:T(8,128)(2,1)} %row_second.6), calls=%async_computation.6 | async-start | bytes 2097152 | tf_op jit(solution)/shard_map/all_to_all | solution.py:410
  312.5 42.1 %copy-start.4 = (bf16[16,8,32,128]{3,2,1,0:T(8,128)(2,1)}, bf16[16,8,32,128]{3,2,1,0:T(8,128)(2,1)S(1)}, u32[]{:S(2)}) copy-start(bf16[16,8,32,128]{3,2,1,0:T(8,128)(2,1)S(1)} %all-to-all-done.6.data_ref) | copy-start | bytes 3145732
  312.5 29.7 %all-to-all-start.5 = ((bf16[16,8,32,128]{3,2,1,0:T(8,128)(2,1)}), bf16[16,8,32,128]{3,2,1,0:T(8,128)(2,1)S(1)}, u32[]{:S(2)}, u32[]{:S(2)}) async-start(bf16[16,8,32,128]{3,2,1,0:T(8,128)(2,1)} %row_second.5), calls=%async_computation.5 | async-start | bytes 2097152 | tf_op jit(solution)/shard_map/all_to_all | solution.py:410
  342.1 20.0 %copy-start.5 = (bf16[16,8,32,128]{3,2,1,0:T(8,128)(2,1)}, bf16[16,8,32,128]{3,2,1,0:T(8,128)(2,1)S(1)}, u32[]{:S(2)}) copy-start(bf16[16,8,32,128]{3,2,1,0:T(8,128)(2,1)S(1)} %all-to-all-done.5.data_ref) | copy-start | bytes 3145732
  342.1 29.7 %all-to-all-start.4 = ((bf16[16,8,32,128]{3,2,1,0:T(8,128)(2,1)}), bf16[16,8,32,128]{3,2,1,0:T(8,128)(2,1)S(1)}, u32[]{:S(2)}, u32[]{:S(2)}) async-start(bf16[16,8,32,128]{3,2,1,0:T(8,128)(2,1)} %row_second.4), calls=%async_computation.4 | async-start | bytes 2097152 | tf_op jit(solution)/shard_map/all_to_all | solution.py:410
  371.8 1.0 copy-start.6
where the time goes:
time: 382 us; the launch traced here: 380 us
  Pallas kernels  149 us (39%)
  waiting for transfers between devices  127 us (33%)
  blocking collectives  61.6 us (16%)
  starting transfers between devices  33.6 us (9%)
  local copies, waits for them, and re-layouts  5.01 us (1%)
  other arithmetic  4.29 us (1%)
    all_to_all x2, blocking collectives, pair_plan(): lax.all_to_all(spec[o], 'gx', split_axis=0, concat_axis=0, tiled=True)  61.6 us
    all_to_all x4, waiting for transfers between devices, pair_plan(): data = lax.all_to_all(rows, 'gx', split_axis=0, concat_axis=0, tiled=True)  56.6 us
    pallas_call x4, Pallas kernels, gram_call(): pl.pallas_call(functools.partial(gram_kernel, first_call, cells, factor),...  50.2 us
    all_to_all x2, waiting for transfers between devices, pair_plan(): lax.all_to_all(spec[o], 'gx', split_axis=0, concat_axis=0, tiled=True)  40.7 us
    pallas_call x4, Pallas kernels, column_call(): pl.pallas_call(functools.partial(column_kernel, alias), grid=(lows,), in_...  30.5 us
    ppermute x4, waiting for transfers between devices, pair_plan(): other = lax.ppermute(mine, 'grp', [(0, 1), (1, 0)])  29.8 us
    pallas_call x1, Pallas kernels, spectra_call(): pl.pallas_call(functools.partial(spectra_kernel, n_gx, out_dev), grid=(in...  27.7 us
    pallas_call x4, Pallas kernels, row_second_call(): pl.pallas_call(row_second_kernel, grid=(1,), in_specs=[take, take, pl.Blo...  26.8 us
  transfers between devices with their start and end apart: 10, of which 10 were waited for; matrix products, arithmetic and copies ran while one was open for 2% of the time, Pallas kernels for 21%

commit v1 on v0

--- a/solution.py
+++ b/solution.py
@@ -8,6 +8,7 @@
 from jax.experimental import pallas as pl
 from jax.experimental.pallas import tpu as pltpu
 from jax.sharding import PartitionSpec as P
+
 
 FRADIX = 128
 AVG = 256
@@ -53,15 +54,14 @@
     return first, twist, second
 
 
-def row_tables(n_gx):
+def row_tables():
     cols = TILE // BC
     k1, w = np.arange(cols), np.arange(BC)
     angle = turn(np.outer(k1, w), TILE, 1.0)
     twist = np.stack([np.cos(angle), np.sin(angle)]).astype(np.float32)
     second = complex_table(turn(np.outer(w, w), BC, 1.0), 1.0 / math.sqrt(TILE))
     second = second.transpose(2, 0, 1, 3).reshape(2 * BC, 2 * BC)
-    high, low = halves(second)
-    return twist, np.concatenate([high, low, high], axis=1)
+    return twist, halves(second)[0]
 
 
 def column_tables(n_gx):
@@ -71,10 +71,9 @@
     first = complex_table(turn(np.outer(index, index), count, 1.0), 1.0 / math.sqrt(TILE))
     first = first.reshape(2, 2, n_gx, blocks, count)
     first = first.transpose(2, 1, 3, 0, 4).reshape(2 * count, 2 * count)
-    high, low = halves(first)
     angle = turn(np.outer(np.arange(BR), index), TILE, 1.0)
     twist = np.stack([np.cos(angle), np.sin(angle)]).astype(np.float32)
-    return np.concatenate([high, low], axis=0), twist
+    return halves(first)[0], twist
 
 
 def times(value, factor):
@@ -127,36 +126,62 @@
     return lax.dot_general(left, right, (((0,), (0,)), ((), ())), preferred_element_type=F32)
 
 
-def spectra_kernel(n_gx, out_dev, v_ref, first_ref, twist_ref, second_ref, *rest):
-    out_refs, scratch = rest[:out_dev], rest[out_dev]
-    rows = 2 * FRADIX
-
-    def one(i, carry):
-        v = v_ref[i]
+def channel_rows(n_gx, scratch, out_ref):
+    stride = scratch.shape[0] // PACK
+    per = out_ref.shape[2] // FRADIX
+    for d in range(n_gx):
+        for t in range(per):
+            piece = scratch[pl.ds(d * per + t, PACK, stride=stride), :]
+            out_ref[d, :, t * FRADIX : (t + 1) * FRADIX] = piece.astype(BF16)
+
+
+def second_stage(pair, high_ref, low_ref, second_ref, scratch):
+    rows = second_ref.shape[0]
+    stride = scratch.shape[0] // PACK
+    two = 2 * FRADIX
+    high = high_ref[2 * pair : 2 * pair + 2].reshape(two, two)
+    low = low_ref[2 * pair : 2 * pair + 2].reshape(two, two)
+    z = dot_nt(second_ref[...], jnp.concatenate([high, high, low], axis=1))
+    scratch[2 * pair * stride : 2 * pair * stride + rows, :] = z[:, :FRADIX]
+    scratch[(2 * pair + 1) * stride : (2 * pair + 1) * stride + rows, :] = z[:, FRADIX:]
+
+
+def spectra_first_kernel(n_gx, v_ref, first_ref, twist_ref, second_ref, high_ref, low_ref, out_ref, scratch):
+    for pair in range(PACK // 2):
+        v = jnp.concatenate([v_ref[2 * pair], v_ref[2 * pair + 1]], axis=1)
         y = jnp.dot(first_ref[...], jnp.concatenate([v, v], axis=0), preferred_element_type=F32)
-        re, im = times((y[:FRADIX], y[FRADIX:]), (twist_ref[0], twist_ref[1]))
-        high, low = split_value(jnp.concatenate([re, im], axis=1))
-        z = dot_nt(second_ref[...], jnp.concatenate([high, high, low], axis=1))
-        scratch[pl.ds(pl.multiple_of(i * rows, rows), rows), :] = z
-        return carry
-
-    lax.fori_loop(0, PACK, one, 0, unroll=2)
-    per = rows // (out_dev * n_gx)
-    for o in range(out_dev):
-        for d in range(n_gx):
-            for t in range(per):
-                row = (o * n_gx + d) * per + t
-                piece = scratch[pl.ds(row, PACK, stride=rows), :]
-                out_refs[o][d, :, t * FRADIX : (t + 1) * FRADIX] = piece.astype(BF16)
-
-
-def spectra_call(volts, n_gx, out_dev):
+        for u in range(2):
+            lane = slice(u * FRADIX, (u + 1) * FRADIX)
+            re, im = times((y[:FRADIX, lane], y[FRADIX:, lane]), (twist_ref[0], twist_ref[1]))
+            for part, value in enumerate((re, im)):
+                high, low = split_value(value)
+                high_ref[2 * pair + u, :, part * FRADIX : (part + 1) * FRADIX] = high
+                low_ref[2 * pair + u, :, part * FRADIX : (part + 1) * FRADIX] = low
+    for pair in range(PACK // 2):
+        second_stage(pair, high_ref, low_ref, second_ref, scratch)
+    channel_rows(n_gx, scratch, out_ref)
+
+
+def spectra_second_kernel(n_gx, high_ref, low_ref, second_ref, out_ref, scratch):
+    for pair in range(PACK // 2):
+        second_stage(pair, high_ref, low_ref, second_ref, scratch)
+    channel_rows(n_gx, scratch, out_ref)
+
+
+def whole(x):
+    return pl.BlockSpec(x.shape, lambda *i: (0,) * x.ndim)
+
+
+def spectra_first_call(volts, n_gx, out_dev):
     inputs = volts.shape[0]
     first, twist, second = spectra_tables(n_gx, out_dev)
+    rows = 2 * FRADIX // out_dev
+    second = second[:rows]
     depth = 2 * AVG
-    whole = lambda x: pl.BlockSpec(x.shape, lambda i: (0,) * x.ndim)
+    turned = jax.ShapeDtypeStruct((inputs, FRADIX, 2 * FRADIX), BF16)
+    turned_spec = pl.BlockSpec((PACK, FRADIX, 2 * FRADIX), lambda i: (i, 0, 0))
     return pl.pallas_call(
-        functools.partial(spectra_kernel, n_gx, out_dev),
+        functools.partial(spectra_first_kernel, n_gx),
         grid=(inputs // PACK,),
         in_specs=[
             pl.BlockSpec((PACK, 2 * FRADIX, FRADIX), lambda i: (i, 0, 0)),
@@ -164,20 +189,70 @@
             whole(twist),
             whole(second),
         ],
-        out_specs=[pl.BlockSpec((n_gx, PACK, depth), lambda i: (0, i, 0))] * out_dev,
-        out_shape=[jax.ShapeDtypeStruct((n_gx, inputs, depth), BF16)] * out_dev,
-        scratch_shapes=[pltpu.VMEM((PACK * 2 * FRADIX, FRADIX), F32)],
-        name="spectra",
+        out_specs=[turned_spec, turned_spec, pl.BlockSpec((n_gx, PACK, depth), lambda i: (0, i, 0))],
+        out_shape=[turned, turned, jax.ShapeDtypeStruct((n_gx, inputs, depth), BF16)],
+        scratch_shapes=[pltpu.VMEM((PACK * (rows + SUB), FRADIX), F32)],
+        name="spectra_first",
     )(volts, first, twist, second)
 
 
-def gram_kernel(first_call, cells, factor, count_ref, list_ref, *rest):
-    if first_call:
-        mine_ref, other_ref, out_ref, vis, grid, sem = rest
-    else:
-        mine_ref, other_ref, in_ref, out_ref, vis, grid, sem = rest
-    nin, depth = mine_ref.shape
+def spectra_second_call(high, low, n_gx, out_dev, o):
+    inputs = high.shape[0]
+    rows = 2 * FRADIX // out_dev
+    second = spectra_tables(n_gx, out_dev)[2][o * rows : (o + 1) * rows]
+    depth = 2 * AVG
+    turned_spec = pl.BlockSpec((PACK, FRADIX, 2 * FRADIX), lambda i: (i, 0, 0))
+    return pl.pallas_call(
+        functools.partial(spectra_second_kernel, n_gx),
+        grid=(inputs // PACK,),
+        in_specs=[turned_spec, turned_spec, whole(second)],
+        out_specs=pl.BlockSpec((n_gx, PACK, depth), lambda i: (0, i, 0)),
+        out_shape=jax.ShapeDtypeStruct((n_gx, inputs, depth), BF16),
+        scratch_shapes=[pltpu.VMEM((PACK * (rows + SUB), FRADIX), F32)],
+        name="spectra_second",
+    )(high, low, second)
+
+
+def correlate(x_ref, vis, factor):
+    nin, depth = x_ref.shape
     half = depth // 2
+    panel = 2 * BC
+
+    def one(p, carry):
+        base = pl.multiple_of(p * panel, panel)
+        x = x_ref[pl.ds(base, panel), :]
+        swapped = jnp.concatenate([x[:, half:], -x[:, :half]], axis=1)
+        left = jnp.concatenate([x, swapped], axis=0)
+        gram = (dot_nt(left, x_ref[...]) * factor).astype(BF16)
+        for e in range(nin // BC):
+            vis[0, e, pl.ds(base, panel), :] = gram[:panel, e * BC : (e + 1) * BC]
+            vis[1, e, pl.ds(base, panel), :] = gram[panel:, e * BC : (e + 1) * BC]
+        return carry
+
+    lax.fori_loop(0, nin // panel, one, 0)
+
+
+def place_blocks(which, count_ref, list_ref, vis, grid):
+    cells = grid.shape[1]
+    wide = vis.shape[1]
+
+    def place(s, carry):
+        code = list_ref[which, s]
+        cell = lax.rem(code, cells)
+        block = lax.div(code, cells)
+        e = lax.rem(block, wide)
+        row = pl.multiple_of(lax.div(block, wide) * BR, BR)
+        for part in range(2):
+            grid[part, cell] += vis[part, e, pl.ds(row, BR), :].astype(F32)
+        return carry
+
+    lax.fori_loop(0, count_ref[which], place, 0)
+
+
+def gram_kernel(streams, first_call, factor, count_ref, list_ref, *rest):
+    x_refs, rest = rest[:streams], rest[streams:]
+    out_ref, vis, grid, sem = rest[-4:]
+    cells = grid.shape[1]
     if first_call:
         def clear(i, carry):
             grid[:, pl.ds(i * SUB, SUB)] = jnp.zeros((2, SUB, BR, BC), F32)
@@ -185,53 +260,30 @@
 
         lax.fori_loop(0, cells // SUB, clear, 0)
     else:
-        load = pltpu.make_async_copy(in_ref, grid, sem)
+        load = pltpu.make_async_copy(rest[0], grid, sem)
         load.start()
-    panel = 2 * BC
-    for which, x_ref in enumerate((mine_ref, other_ref)):
-        def one(p, carry):
-            base = pl.multiple_of(p * panel, panel)
-            x = x_ref[pl.ds(base, panel), :]
-            swapped = jnp.concatenate([x[:, half:], -x[:, :half]], axis=1)
-            left = jnp.concatenate([x, swapped], axis=0)
-            gram = (dot_nt(left, x_ref[...]) * factor).astype(BF16)
-            for e in range(nin // BC):
-                vis[0, e, pl.ds(base, panel), :] = gram[:panel, e * BC : (e + 1) * BC]
-                vis[1, e, pl.ds(base, panel), :] = gram[panel:, e * BC : (e + 1) * BC]
-            return carry
-
-        lax.fori_loop(0, nin // panel, one, 0)
+    for which, x_ref in enumerate(x_refs):
+        correlate(x_ref, vis, factor)
         if which == 0 and not first_call:
             load.wait()
-
-        def place(s, carry):
-            code = list_ref[which, s]
-            cell = lax.rem(code, cells)
-            block = lax.div(code, cells)
-            e = lax.rem(block, nin // BC)
-            row = pl.multiple_of(lax.div(block, nin // BC) * BR, BR)
-            for part in range(2):
-                grid[part, cell] += vis[part, e, pl.ds(row, BR), :].astype(F32)
-            return carry
-
-        lax.fori_loop(0, count_ref[which], place, 0)
+        place_blocks(which, count_ref, list_ref, vis, grid)
     store = pltpu.make_async_copy(grid, out_ref, sem)
     store.start()
     store.wait()
 
 
-def gram_call(counts, lists, mine, other, grid, cells, factor):
+def gram_call(counts, lists, streams, grid, cells, factor):
     first_call = grid is None
     shape = (2, cells, BR, BC)
-    nin, depth = mine.shape
+    nin, depth = streams[0].shape
     any_spec = pl.BlockSpec(memory_space=pl.ANY)
     vmem = pl.BlockSpec(memory_space=pltpu.VMEM)
     smem = pl.BlockSpec(memory_space=pltpu.SMEM)
-    args = (counts, lists, mine, other) + (() if first_call else (grid,))
-    flops = 2 * 2 * 2 * nin * nin * depth
+    args = (counts, lists) + tuple(streams) + (() if first_call else (grid,))
+    flops = len(streams) * 4 * nin * nin * depth
     return pl.pallas_call(
-        functools.partial(gram_kernel, first_call, cells, factor),
-        in_specs=[smem, smem, vmem, vmem] + ([] if first_call else [any_spec]),
+        functools.partial(gram_kernel, len(streams), first_call, factor),
+        in_specs=[smem, smem] + [vmem] * len(streams) + ([] if first_call else [any_spec]),
         out_specs=any_spec,
         out_shape=jax.ShapeDtypeStruct(shape, F32),
         scratch_shapes=[
@@ -239,125 +291,151 @@
             pltpu.VMEM(shape, F32),
             pltpu.SemaphoreType.DMA,
         ],
-        input_output_aliases={} if first_call else {4: 0},
+        input_output_aliases={} if first_call else {2 + len(streams): 0},
         cost_estimate=pl.CostEstimate(flops=flops, transcendentals=0, bytes_accessed=2**24),
         name="gram",
     )(*args)
 
 
-def row_first_kernel(grid_ref, twist_ref, high_ref, low_ref, scratch):
+def gram_row_kernel(factor, count_ref, list_ref, x_ref, grid_ref, twist_ref, out_ref, vis, grid, scratch, sem):
     cols = TILE // BC
+    step = pl.program_id(0)
+
+    @pl.when(step == 0)
+    def _():
+        load = pltpu.make_async_copy(grid_ref, grid, sem)
+        load.start()
+        correlate(x_ref, vis, factor)
+        load.wait()
+        place_blocks(0, count_ref, list_ref, vis, grid)
+
     for h in range(BR // SUB):
         rows = slice(h * SUB, (h + 1) * SUB)
-        values = [(grid_ref[0, 0, c, rows], grid_ref[1, 0, c, rows]) for c in range(cols)]
+        values = [(grid[0, step * cols + c, rows], grid[1, step * cols + c, rows]) for c in range(cols)]
         values = butterflies(values, 1.0)
         for k in range(cols):
-            factor = (twist_ref[0, k : k + 1, :], twist_ref[1, k : k + 1, :])
-            re, im = times(values[k], factor)
+            factor_k = (twist_ref[0, k : k + 1, :], twist_ref[1, k : k + 1, :])
+            re, im = times(values[k], factor_k)
             at = slice(k * BR + h * SUB, k * BR + (h + 1) * SUB)
             scratch[at, :BC] = re
             scratch[at, BC:] = im
-    high, low = split_value(scratch[...])
-    high_ref[0] = high
-    low_ref[0] = low
-
-
-def row_first_call(grid, twist):
-    _, blocks, cols, _, _ = grid.shape
-    shape = jax.ShapeDtypeStruct((blocks, cols * BR, 2 * BC), BF16)
-    out = pl.BlockSpec((1, cols * BR, 2 * BC), lambda i: (i, 0, 0))
+    out_ref[0] = scratch[...].astype(BF16)
+
+
+def gram_row_call(counts, lists, stream, grid, cells, factor, twist):
+    nin, _ = stream.shape
+    cols = TILE // BC
+    blocks = cells // cols
+    smem = pl.BlockSpec(memory_space=pltpu.SMEM)
     return pl.pallas_call(
-        row_first_kernel,
+        functools.partial(gram_row_kernel, factor),
         grid=(blocks,),
         in_specs=[
-            pl.BlockSpec((2, 1, cols, BR, BC), lambda i: (0, i, 0, 0, 0)),
-            pl.BlockSpec(twist.shape, lambda i: (0, 0, 0)),
+            smem,
+            smem,
+            pl.BlockSpec(memory_space=pltpu.VMEM),
+            pl.BlockSpec(memory_space=pl.ANY),
+            whole(twist),
         ],
-        out_specs=[out, out],
-        out_shape=[shape, shape],
-        scratch_shapes=[pltpu.VMEM((cols * BR, 2 * BC), F32)],
-        name="row_first",
-    )(grid, twist)
-
-
-def row_second_kernel(high_ref, low_ref, second_ref, out_ref, scratch):
-    blocks, lanes, _ = high_ref.shape
+        out_specs=pl.BlockSpec((1, cols * BR, 2 * BC), lambda i: (i, 0, 0)),
+        out_shape=jax.ShapeDtypeStruct((blocks, cols * BR, 2 * BC), BF16),
+        scratch_shapes=[
+            pltpu.VMEM((2, nin // BC, nin, BC), BF16),
+            pltpu.VMEM((2, cells, BR, BC), F32),
+            pltpu.VMEM((cols * BR, 2 * BC), F32),
+            pltpu.SemaphoreType.DMA,
+        ],
+        name="gram_row",
+    )(counts, lists, stream, grid, twist)
+
+
+def row_second_kernel(data_ref, second_ref, out_ref, scratch):
+    blocks = data_ref.shape[0]
+    lanes = SUB * BR
     rows = 2 * BC
-
-    def one(b, carry):
+    stride = scratch.shape[0] // blocks
+    for b in range(blocks // 2):
+        data = data_ref[2 * b : 2 * b + 2].reshape(2 * lanes, rows)
+        z = dot_nt(second_ref[...], data)
         for u in range(2):
-            high, low = high_ref[2 * b + u], low_ref[2 * b + u]
-            z = dot_nt(second_ref[...], jnp.concatenate([high, high, low], axis=1))
-            scratch[pl.ds(pl.multiple_of((2 * b + u) * rows, rows), rows), :] = z
-        return carry
-
-    lax.fori_loop(0, blocks // 2, one, 0)
+            at = (2 * b + u) * stride
+            scratch[at : at + rows, :] = z[:, u * lanes : (u + 1) * lanes]
     n_gx, lows, _, _ = out_ref.shape
     for d in range(n_gx):
         for k in range(lows):
             for part in range(2):
                 row = (d * lows + k) * 2 + part
-                piece = scratch[pl.ds(row, blocks, stride=rows), :]
+                piece = scratch[pl.ds(row, blocks, stride=stride), :]
                 out_ref[d, k, part * blocks : (part + 1) * blocks, :] = piece.astype(BF16)
 
 
-def row_second_call(high, low, second, n_gx, chunk):
-    blocks = high.shape[0]
+def row_second_call(data, second, n_gx, start, count):
+    blocks = data.shape[0]
     lanes = SUB * BR
     lows = BC // n_gx
-    take = pl.BlockSpec((blocks, lanes, 2 * BC), lambda i: (0, chunk, 0))
     return pl.pallas_call(
         row_second_kernel,
-        grid=(1,),
-        in_specs=[take, take, pl.BlockSpec(second.shape, lambda i: (0, 0))],
-        out_specs=pl.BlockSpec((n_gx, lows, 2 * blocks, lanes), lambda i: (0, 0, 0, 0)),
-        out_shape=jax.ShapeDtypeStruct((n_gx, lows, 2 * blocks, lanes), BF16),
-        scratch_shapes=[pltpu.VMEM((blocks * 2 * BC, lanes), F32)],
+        grid=(count,),
+        in_specs=[
+            pl.BlockSpec((blocks, lanes, 2 * BC), lambda i: (0, start + i, 0)),
+            whole(second),
+        ],
+        out_specs=pl.BlockSpec((n_gx, lows, 2 * blocks, lanes), lambda i: (0, 0, 0, i)),
+        out_shape=jax.ShapeDtypeStruct((n_gx, lows, 2 * blocks, count * lanes), BF16),
+        scratch_shapes=[pltpu.VMEM((blocks * (2 * BC + SUB), lanes), F32)],
         cost_estimate=pl.CostEstimate(flops=2**31, transcendentals=0, bytes_accessed=2**22),
         name="row_second",
-    )(high, low, second)
-
-
-def column_kernel(alias, data_ref, first_ref, twist_ref, *rest):
+    )(data, second)
+
+
+COLUMN_STEP = 2
+
+
+def column_kernel(data_ref, first_ref, twist_ref, *rest):
     out_ref, scratch = rest[-2], rest[-1]
     n_gx, _, rows, lanes = data_ref.shape
-    data = data_ref[:, 0].reshape(n_gx * rows, lanes)
-    mixed = dot_tn(jnp.concatenate([data, data], axis=0), first_ref[...])
     count = TILE // BR
-    for b in range(2 * count // BC):
-        scratch[b * lanes : (b + 1) * lanes, :] = mixed[:, b * BC : (b + 1) * BC]
-    for b in range(count // BC):
-        values = []
-        for r in range(BR):
-            value = (
-                scratch[pl.ds(b * lanes + r, SUB, stride=BR), :],
-                scratch[pl.ds((count // BC + b) * lanes + r, SUB, stride=BR), :],
-            )
+    span = scratch.shape[0] // COLUMN_STEP
+    for q in range(COLUMN_STEP):
+        data = data_ref[:, q].reshape(n_gx * rows, lanes)
+        mixed = dot_tn(data, first_ref[...])
+        for b in range(2 * count // BC):
+            scratch[q * span + b * lanes : q * span + (b + 1) * lanes, :] = mixed[:, b * BC : (b + 1) * BC]
+    for q in range(COLUMN_STEP):
+        for b in range(count // BC):
             lane = slice(b * BC, (b + 1) * BC)
-            values.append(times(value, (twist_ref[0, r : r + 1, lane], twist_ref[1, r : r + 1, lane])))
-        values = butterflies(values, 1.0)
-        for k in range(BR):
-            lane = slice(k * count + b * BC, k * count + (b + 1) * BC)
-            out_ref[0, 0, 0, :, lane] = values[k][0]
-            out_ref[1, 0, 0, :, lane] = values[k][1]
-
-
-def column_call(data, first, twist, image, chunk, chunks):
-    n_gx, lows, rows, lanes = data.shape
+            values = []
+            for r in range(BR):
+                value = (
+                    scratch[pl.ds(q * span + b * lanes + r, SUB, stride=BR), :],
+                    scratch[pl.ds(q * span + (count // BC + b) * lanes + r, SUB, stride=BR), :],
+                )
+                factor = (twist_ref[0, r : r + 1, lane], twist_ref[1, r : r + 1, lane])
+                values.append(times(value, factor) if r else value)
+            values = butterflies(values, 1.0)
+            for k in range(BR):
+                at = slice(k * count + b * BC, k * count + (b + 1) * BC)
+                out_ref[0, q, 0, :, at] = values[k][0]
+                out_ref[1, q, 0, :, at] = values[k][1]
+
+
+def column_call(data, first, twist, image, part, chunk, chunks):
+    n_gx, lows, rows, _ = data.shape
+    lanes = SUB * BR
     alias = image is not None
     shape = (2, lows, chunks, SUB, TILE)
     return pl.pallas_call(
-        functools.partial(column_kernel, alias),
-        grid=(lows,),
+        column_kernel,
+        grid=(lows // COLUMN_STEP,),
         in_specs=[
-            pl.BlockSpec((n_gx, 1, rows, lanes), lambda i: (0, i, 0, 0)),
-            pl.BlockSpec(first.shape, lambda i: (0, 0)),
-            pl.BlockSpec(twist.shape, lambda i: (0, 0, 0)),
+            pl.BlockSpec((n_gx, COLUMN_STEP, rows, lanes), lambda i: (0, i, 0, part)),
+            whole(first),
+            whole(twist),
         ]
         + ([pl.BlockSpec(memory_space=pl.ANY)] if alias else []),
-        out_specs=pl.BlockSpec((2, 1, 1, SUB, TILE), lambda i: (0, i, chunk, 0, 0)),
+        out_specs=pl.BlockSpec((2, COLUMN_STEP, 1, SUB, TILE), lambda i: (0, i, chunk, 0, 0)),
         out_shape=jax.ShapeDtypeStruct(shape, F32),
-        scratch_shapes=[pltpu.VMEM((2 * (TILE // BR) // BC * lanes, BC), F32)],
+        scratch_shapes=[pltpu.VMEM((COLUMN_STEP * 2 * (TILE // BR) // BC * lanes, BC), F32)],
         input_output_aliases={3: 0} if alias else {},
         cost_estimate=pl.CostEstimate(flops=2**30, transcendentals=0, bytes_accessed=2**22),
         name="column",
@@ -377,13 +455,16 @@
     return jnp.sum(number, axis=2), lists
 
 
+def row_chunks(groups):
+    return (1,) * groups
+
+
 def pair_plan(voltages, tile_of, cell_of):
     n_gx = lax.axis_size("gx")
-    _, st_dev, pols, spectra, parts, fine = voltages.shape
+    _, st_dev, pols, spectra, _, fine = voltages.shape
     inputs = st_dev * pols
     out_dev = fine // (n_gx * AVG)
     cells = (TILE // n_gx // BR) * (TILE // BC)
-    blocks = TILE // n_gx // BR
     cols = TILE // BC
     me = lax.axis_index("grp")
     counts, lists = work_lists(tile_of, cell_of, me, out_dev, cells)
@@ -392,23 +473,34 @@
 
     volts = voltages.reshape(inputs, 2, FRADIX, FRADIX).transpose(0, 2, 1, 3)
     volts = volts.reshape(inputs, 2 * FRADIX, FRADIX)
-    spec = spectra_call(volts, n_gx, out_dev)
+    factor = 1.0 / math.sqrt(spectra * AVG)
+    high, low, spec = spectra_first_call(volts, n_gx, out_dev)
     grid = None
     for o in range(out_dev):
-        mine = lax.all_to_all(spec[o], "gx", split_axis=0, concat_axis=0, tiled=True)
+        if o:
+            spec = spectra_second_call(high, low, n_gx, out_dev, o)
+        mine = lax.all_to_all(spec, "gx", split_axis=0, concat_axis=0, tiled=True)
         mine = mine.reshape(n_gx * inputs, 2 * AVG)
+        number, list_of = counts[0, o : o + 1], lists[0, o : o + 1]
+        if o:
+            number = jnp.concatenate([number, counts[1, o - 1 : o]])
+            list_of = jnp.concatenate([list_of, lists[1, o - 1 : o]])
+        streams = (mine, other) if o else (mine,)
+        grid = gram_call(number, list_of, streams, grid, cells, factor)
         other = lax.ppermute(mine, "grp", [(0, 1), (1, 0)])
-        factor = 1.0 / math.sqrt(spectra * AVG)
-        grid = gram_call(counts[:, o], lists[:, o], mine, other, grid, cells, factor)
-    twist, second = row_tables(n_gx)
-    high, low = row_first_call(grid.reshape(2, blocks, cols, BR, BC), twist)
+    twist, second = row_tables()
+    last = out_dev - 1
+    mixed = gram_row_call(counts[1, last:], lists[1, last:], other, grid, cells, factor, twist)
     first, turned = column_tables(n_gx)
     image = None
-    chunks = cols // SUB
-    for chunk in range(chunks):
-        rows = row_second_call(high, low, second, n_gx, chunk)
+    start = 0
+    groups = cols // SUB
+    for size in row_chunks(groups):
+        rows = row_second_call(mixed, second, n_gx, start, size)
         data = lax.all_to_all(rows, "gx", split_axis=0, concat_axis=0, tiled=True)
-        image = column_call(data, first, turned, image, chunk, chunks)
+        for part in range(size):
+            image = column_call(data, first, turned, image, part, start + part, groups)
+        start += size
     return image.reshape(1, 2, TILE // n_gx, TILE)
 
 
@@ -459,7 +551,7 @@
 
 
 def operands(local):
-    stations, pols, spectra, parts, channels = local.shape
+    stations, pols, spectra, _, channels = local.shape
     inputs = stations * pols
     nout = channels // AVG
     grouped = local.reshape(inputs, spectra, 2, nout, AVG).transpose(3, 0, 1, 2, 4)
@@ -478,7 +570,7 @@
 
 
 def pair_fits(gx_count, shape):
-    lead, st_dev, pols, spectra, parts, fine = shape
+    lead, st_dev, pols, spectra, _, fine = shape
     return (
         lead == 1
         and spectra == 1
@@ -492,7 +584,7 @@
 def on_device(voltages, tile_of, cell_of):
     grp_count = lax.axis_size("grp")
     gx_count = lax.axis_size("gx")
-    lead, st_dev, pols, spectra, parts, fine = voltages.shape
+    _, st_dev, pols, spectra, _, fine = voltages.shape
     if grp_count == 2 and pair_fits(gx_count, voltages.shape):
         return pair_plan(voltages, tile_of, cell_of)
     volts = voltages.reshape(st_dev * pols * spectra, 2, fine).astype(jnp.float32)

time: 382 us -> 346 us (0.906)
  blocking collectives: 61.6 us -> 0 us
  waiting for transfers between devices: 127 us -> 157 us
  Pallas kernels: 149 us -> 127 us
  starting transfers between devices: 33.6 us -> 42.9 us
  other arithmetic: 4.29 us -> 11.6 us
    all_to_all x2 -> x0, blocking collectives: 61.6 us -> none  [pair_plan(): lax.all_to_all(spec[o], 'gx', split_axis=0, concat_axis=0, tiled=True)]
    pallas_call x14 -> x17, Pallas kernels: 149 us -> 127 us  [the longest x4 50 us: gram_call(): pl.pallas_call(functools.partial(gram_kernel, len(streams), first_call, f...]
    all_to_all x2 -> x4, waiting for transfers between devices: 40.7 us -> 61.1 us  [pair_plan(): mine = lax.all_to_all(spec, 'gx', split_axis=0, concat_axis=0, tiled=True)]
    all_to_all x4, waiting for transfers between devices: 56.6 us -> 76.2 us  [pair_plan(): data = lax.all_to_all(rows, 'gx', split_axis=0, concat_axis=0, tiled=True)]
    all_to_all x2 -> x4, starting transfers between devices: 9.12 us -> 20.8 us  [pair_plan(): mine = lax.all_to_all(spec, 'gx', split_axis=0, concat_axis=0, tiled=True)]
    ppermute x4, waiting for transfers between devices: 29.8 us -> 20.1 us  [pair_plan(): other = lax.ppermute(mine, 'grp', [(0, 1), (1, 0)])]
    concatenate x0 -> x6, other arithmetic: none -> 7.29 us  [the longest x3 5.49 us: pair_plan(): number = jnp.concatenate([number, counts[1, o - 1:o]])]
  transfers between devices with their start and end apart: 10 -> 12, of which waited for: 10 -> 11; matrix products, arithmetic and copies ran while one was open for 2% -> 4% of each run, Pallas kernels for 21% -> 28%
where the time goes in v1:
time: 346 us; the launch traced here: 344 us
  waiting for transfers between devices  157 us (45%)
  Pallas kernels  127 us (37%)
  starting transfers between devices  42.9 us (12%)
  other arithmetic  11.6 us (3%)
  local copies, waits for them, and re-layouts  4.9 us (1%)
    all_to_all x4, waiting for transfers between devices, pair_plan(): data = lax.all_to_all(rows, 'gx', split_axis=0, concat_axis=0, tiled=True)  76.2 us
    all_to_all x4, waiting for transfers between devices, pair_plan(): mine = lax.all_to_all(spec, 'gx', split_axis=0, concat_axis=0, tiled=True)  61.1 us
    pallas_call x4, Pallas kernels, gram_call(): pl.pallas_call(functools.partial(gram_kernel, len(streams), first_call, f...  50 us
    pallas_call x3, Pallas kernels, spectra_second_call(): pl.pallas_call(functools.partial(spectra_second_kernel, n_gx), grid=(inpu...  22.4 us
    all_to_all x4, starting transfers between devices, pair_plan(): mine = lax.all_to_all(spec, 'gx', split_axis=0, concat_axis=0, tiled=True)  20.8 us
    all_to_all x4, starting transfers between devices, pair_plan(): data = lax.all_to_all(rows, 'gx', split_axis=0, concat_axis=0, tiled=True)  20.2 us
    ppermute x4, waiting for transfers between devices, pair_plan(): other = lax.ppermute(mine, 'grp', [(0, 1), (1, 0)])  20.1 us
    pallas_call x4, Pallas kernels, column_call(): pl.pallas_call(column_kernel, grid=(lows // COLUMN_STEP,), in_specs=[pl.B...  19.4 us
  transfers between devices with their start and end apart: 12, of which 11 were waited for; matrix products, arithmetic and copies ran while one was open for 4% of the time, Pallas kernels for 28%

profile of v1, /device:TPU:13, one launch (start us, length us, event | category | flops | bytes accessed | tf_op | source)
XLA Modules:
  0.0 343.9 jit_solution(14700097452127532250)
XLA Ops:
  0.0 9.1 %spectra_first.1 = (bf16[64,128,256]{2,1,0:T(8,128)(2,1)}, bf16[64,128,256]{2,1,0:T(8,128)(2,1)}, bf16[16,64,512]{2,1,0:T(8,128)(2,1)}) custom-call(bf16[64,256,128]{2,1,0:T(8,128)(2,1)} %bitcast.41, bf16[256,512]{1,0:T(8,128)(2,1)} %constant.62.clone.first_ref, f32[2,128,128]{2,1,0:T(8,128)} %constant.63.clone.twist_ref, ...), custom_call_target="tpu_custom_call" | custom-call | tf_op jit(solution)/shard_map/spectra_first/pallas_call | solution.py:183
  9.1 6.5 %all-to-all-start.3 = ((bf16[16,64,512]{2,1,0:T(8,128)(2,1)}), bf16[16,64,512]{2,1,0:T(8,128)(2,1)S(1)}, u32[]{:S(2)}, u32[]{:S(2)}) async-start(bf16[16,64,512]{2,1,0:T(8,128)(2,1)} %get-tuple-element.10), calls=%async_computation.3 | async-start | bytes 2097152 | tf_op jit(solution)/shard_map/all_to_all | solution.py:482
  15.6 7.5 %spectra_second.5 = bf16[16,64,512]{2,1,0:T(8,128)(2,1)} custom-call(bf16[64,128,256]{2,1,0:T(8,128)(2,1)} %get-tuple-element.8.high_ref, bf16[64,128,256]{2,1,0:T(8,128)(2,1)} %get-tuple-element.9.low_ref, bf16[64,768]{1,0:T(8,128)(2,1)} %constant.65.clone.second_ref), custom_call_target="tpu_custom_call" | custom-call | tf_op jit(solution)/shard_map/spectra_second/pallas_call | solution.py:205
  23.1 17.4 %all-to-all-done.3 = bf16[16,64,512]{2,1,0:T(8,128)(2,1)S(1)} async-done(((bf16[16,64,512]{2,1,0:T(8,128)(2,1)}), bf16[16,64,512]{2,1,0:T(8,128)(2,1)S(1)}, u32[]{:S(2)}, u32[]{:S(2)}) %all-to-all-start.3) | async-done | bytes 1048608 | tf_op jit(solution)/shard_map/all_to_all | solution.py:482
  40.6 1.0 copy-done.7
  41.5 4.8 %all-to-all-start.2 = ((bf16[16,64,512]{2,1,0:T(8,128)(2,1)}), bf16[16,64,512]{2,1,0:T(8,128)(2,1)S(1)}, u32[]{:S(2)}, u32[]{:S(2)}) async-start(bf16[16,64,512]{2,1,0:T(8,128)(2,1)} %spectra_second.5), calls=%async_computation.2 | async-start | bytes 2097152 | tf_op jit(solution)/shard_map/all_to_all | solution.py:482
  46.3 7.5 %spectra_second.4 = bf16[16,64,512]{2,1,0:T(8,128)(2,1)} custom-call(bf16[64,128,256]{2,1,0:T(8,128)(2,1)} %get-tuple-element.8.high_ref, bf16[64,128,256]{2,1,0:T(8,128)(2,1)} %get-tuple-element.9.low_ref, bf16[64,768]{1,0:T(8,128)(2,1)} %constant.66.clone.second_ref), custom_call_target="tpu_custom_call" | custom-call | tf_op jit(solution)/shard_map/spectra_second/pallas_call | solution.py:205
  53.8 17.5 %all-to-all-done.2 = bf16[16,64,512]{2,1,0:T(8,128)(2,1)S(1)} async-done(((bf16[16,64,512]{2,1,0:T(8,128)(2,1)}), bf16[16,64,512]{2,1,0:T(8,128)(2,1)S(1)}, u32[]{:S(2)}, u32[]{:S(2)}) %all-to-all-start.2) | async-done | bytes 1048608 | tf_op jit(solution)/shard_map/all_to_all | solution.py:482
  71.2 4.8 %all-to-all-start.1 = ((bf16[16,64,512]{2,1,0:T(8,128)(2,1)}), bf16[16,64,512]{2,1,0:T(8,128)(2,1)S(1)}, u32[]{:S(2)}, u32[]{:S(2)}) async-start(bf16[16,64,512]{2,1,0:T(8,128)(2,1)} %spectra_second.4), calls=%async_computation.1 | async-start | bytes 2097152 | tf_op jit(solution)/shard_map/all_to_all | solution.py:482
  76.2 2.4 reduce-window.6
  79.4 7.5 %spectra_second.3 = bf16[16,64,512]{2,1,0:T(8,128)(2,1)} custom-call(bf16[64,128,256]{2,1,0:T(8,128)(2,1)} %get-tuple-element.8.high_ref, bf16[64,128,256]{2,1,0:T(8,128)(2,1)} %get-tuple-element.9.low_ref, bf16[64,768]{1,0:T(8,128)(2,1)} %constant.67.clone.second_ref), custom_call_target="tpu_custom_call" | custom-call | tf_op jit(solution)/shard_map/spectra_second/pallas_call | solution.py:205
  86.9 14.0 %all-to-all-done.1 = bf16[16,64,512]{2,1,0:T(8,128)(2,1)S(1)} async-done(((bf16[16,64,512]{2,1,0:T(8,128)(2,1)}), bf16[16,64,512]{2,1,0:T(8,128)(2,1)S(1)}, u32[]{:S(2)}, u32[]{:S(2)}) %all-to-all-start.1) | async-done | bytes 1048608 | tf_op jit(solution)/shard_map/all_to_all | solution.py:482
  100.9 4.8 %all-to-all-start = ((bf16[16,64,512]{2,1,0:T(8,128)(2,1)}), bf16[16,64,512]{2,1,0:T(8,128)(2,1)S(1)}, u32[]{:S(2)}, u32[]{:S(2)}) async-start(bf16[16,64,512]{2,1,0:T(8,128)(2,1)} %spectra_second.3), calls=%async_computation | async-start | bytes 2097152 | tf_op jit(solution)/shard_map/all_to_all | solution.py:482
  105.8 1.1 select_reduce_fusion
  108.1 0.7 fusion.2
  109.1 1.9 pad_add_fusion.5.count_ref
  111.0 0.6 slice_bitcast_fusion
  111.6 0.6 pad_add_fusion.2.list_ref
  112.2 1.2 collective-permute-start.2
  113.4 1.9 pad_add_fusion.4.count_ref
  115.9 0.6 pad_add_fusion.list_ref
  116.7 1.8 pad_add_fusion.3.count_ref
  118.5 12.1 %all-to-all-done = bf16[16,64,512]{2,1,0:T(8,128)(2,1)S(1)} async-done(((bf16[16,64,512]{2,1,0:T(8,128)(2,1)}), bf16[16,64,512]{2,1,0:T(8,128)(2,1)S(1)}, u32[]{:S(2)}, u32[]{:S(2)}) %all-to-all-start) | async-done | bytes 1048608 | tf_op jit(solution)/shard_map/all_to_all | solution.py:482
  130.8 9.8 %gram.4.rest_2_ = f32[2,512,16,128]{3,2,1,0:T(8,128)} custom-call(s32[1]{0:T(128)} %bitcast.21.count_ref, s32[1,512]{1,0:T(1,128)} %get-tuple-element.15.list_ref, bf16[1024,512]{1,0:T(8,128)(2,1)} %bitcast.43), custom_call_target="tpu_custom_call" | custom-call | flops 2147483648 | bytes 16777216 | tf_op jit(solution)/shard_map/gram/pallas_call | solution.py:284
  140.7 13.7 %gram.5.rest_2_ = f32[2,512,16,128]{3,2,1,0:T(8,128)} custom-call(s32[2]{0:T(128)} %pad_add_fusion.5.count_ref, s32[2,512]{1,0:T(2,128)} %pad_add_fusion.2.list_ref, bf16[1024,512]{1,0:T(8,128)(2,1)} %bitcast.36, bf16[1024,512]{1,0:T(8,128)(2,1)} %collective-permute-done.3.rest_1_, f32[2,512,16,128]{3,2,1,0:T(8,128)} %gram.4.rest_2_), custom_call_target="tpu_custom_call", output_to_operand_aliasing={{}: (4, {})} | custom-call | flops 4294967296 | bytes 16777216 | tf_op jit(solution)/shard_map/gram/pallas_call | solution.py:284
  154.4 1.6 collective-permute-done.2.rest_1_
  156.0 13.2 %gram.6.rest_2_ = f32[2,512,16,128]{3,2,1,0:T(8,128)} custom-call(s32[2]{0:T(128)} %pad_add_fusion.4.count_ref, s32[2,512]{1,0:T(2,128)} %pad_add_fusion.1.list_ref, bf16[1024,512]{1,0:T(8,128)(2,1)} %bitcast.38, bf16[1024,512]{1,0:T(8,128)(2,1)} %collective-permute-done.2.rest_1_, f32[2,512,16,128]{3,2,1,0:T(8,128)} %gram.5.rest_2_), custom_call_target="tpu_custom_call", output_to_operand_aliasing={{}: (4, {})} | custom-call | flops 4294967296 | bytes 16777216 | tf_op jit(solution)/shard_map/gram/pallas_call | solution.py:284
  169.2 9.3 %collective-permute-done.1.rest_1_ = bf16[1024,512]{1,0:T(8,128)(2,1)} collective-permute-done((bf16[1024,512]{1,0:T(8,128)(2,1)S(1)}, bf16[1024,512]{1,0:T(8,128)(2,1)}, u32[]{:S(2)}, u32[]{:S(2)}) %collective-permute-start.1) | collective-permute-done | bytes 1048608 | tf_op jit(solution)/shard_map/ppermute | solution.py:490
  178.5 13.3 %gram.7.grid_ref = f32[2,512,16,128]{3,2,1,0:T(8,128)} custom-call(s32[2]{0:T(128)} %pad_add_fusion.3.count_ref, s32[2,512]{1,0:T(2,128)} %pad_add_fusion.list_ref, bf16[1024,512]{1,0:T(8,128)(2,1)} %bitcast.40, bf16[1024,512]{1,0:T(8,128)(2,1)} %collective-permute-done.1.rest_1_, f32[2,512,16,128]{3,2,1,0:T(8,128)} %gram.6.rest_2_), custom_call_target="tpu_custom_call", output_to_operand_aliasing={{}: (4, {})} | custom-call | flops 4294967296 | bytes 16777216 | tf_op jit(solution)/shard_map/gram/pallas_call | solution.py:284
  191.7 9.2 %collective-permute-done.x_ref = bf16[1024,512]{1,0:T(8,128)(2,1)} collective-permute-done((bf16[1024,512]{1,0:T(8,128)(2,1)S(1)}, bf16[1024,512]{1,0:T(8,128)(2,1)}, u32[]{:S(2)}, u32[]{:S(2)}) %collective-permute-start) | collective-permute-done | bytes 1048608 | tf_op jit(solution)/shard_map/ppermute | solution.py:490
  200.9 14.3 %gram_row.1.data_ref = bf16[16,512,256]{2,1,0:T(8,128)(2,1)} custom-call(s32[1]{0:T(128)} %bitcast.count_ref, s32[1,512]{1,0:T(1,128)} %get-tuple-element.22.list_ref, bf16[1024,512]{1,0:T(8,128)(2,1)} %collective-permute-done.x_ref, f32[2,512,16,128]{3,2,1,0:T(8,128)} %gram.7.grid_ref, f32[2,32,128]{2,1,0:T(8,128)} %constant.68.clone.twist_ref), custom_call_target="tpu_custom_call" | custom-call | tf_op jit(solution)/shard_map/gram_row/pallas_call | solution.py:330
  215.2 3.0 row_second.7
  218.2 5.9 %all-to-all-start.7 = ((bf16[16,8,32,128]{3,2,1,0:T(8,128)(2,1)}), bf16[16,8,32,128]{3,2,1,0:T(8,128)(2,1)S(1)}, u32[]{:S(2)}, u32[]{:S(2)}) async-start(bf16[16,8,32,128]{3,2,1,0:T(8,128)(2,1)} %row_second.7), calls=%async_computation.7 | async-start | bytes 2097152 | tf_op jit(solution)/shard_map/all_to_all | solution.py:500
  224.1 3.0 row_second.6
  227.0 21.9 %all-to-all-done.7.data_ref = bf16[16,8,32,128]{3,2,1,0:T(8,128)(2,1)S(1)} async-done(((bf16[16,8,32,128]{3,2,1,0:T(8,128)(2,1)}), bf16[16,8,32,128]{3,2,1,0:T(8,128)(2,1)S(1)}, u32[]{:S(2)}, u32[]{:S(2)}) %all-to-all-start.7) | async-done | bytes 1048608 | tf_op jit(solution)/shard_map/all_to_all | solution.py:500
  249.0 4.8 %all-to-all-start.6 = ((bf16[16,8,32,128]{3,2,1,0:T(8,128)(2,1)}), bf16[16,8,32,128]{3,2,1,0:T(8,128)(2,1)S(1)}, u32[]{:S(2)}, u32[]{:S(2)}) async-start(bf16[16,8,32,128]{3,2,1,0:T(8,128)(2,1)} %row_second.6), calls=%async_computation.6 | async-start | bytes 2097152 | tf_op jit(solution)/shard_map/all_to_all | solution.py:500
  253.8 3.0 row_second.5
  256.7 22.0 %all-to-all-done.6.data_ref = bf16[16,8,32,128]{3,2,1,0:T(8,128)(2,1)S(1)} async-done(((bf16[16,8,32,128]{3,2,1,0:T(8,128)(2,1)}), bf16[16,8,32,128]{3,2,1,0:T(8,128)(2,1)S(1)}, u32[]{:S(2)}, u32[]{:S(2)}) %all-to-all-start.6) | async-done | bytes 1048608 | tf_op jit(solution)/shard_map/all_to_all | solution.py:500
  278.7 4.8 %all-to-all-start.5 = ((bf16[16,8,32,128]{3,2,1,0:T(8,128)(2,1)}), bf16[16,8,32,128]{3,2,1,0:T(8,128)(2,1)S(1)}, u32[]{:S(2)}, u32[]{:S(2)}) async-start(bf16[16,8,32,128]{3,2,1,0:T(8,128)(2,1)} %row_second.5), calls=%async_computation.5 | async-start | bytes 2097152 | tf_op jit(solution)/shard_map/all_to_all | solution.py:500
  283.4 3.0 row_second.4
  286.4 21.9 %all-to-all-done.5.data_ref = bf16[16,8,32,128]{3,2,1,0:T(8,128)(2,1)S(1)} async-done(((bf16[16,8,32,128]{3,2,1,0:T(8,128)(2,1)}), bf16[16,8,32,128]{3,2,1,0:T(8,128)(2,1)S(1)}, u32[]{:S(2)}, u32[]{:S(2)}) %all-to-all-start.5) | async-done | bytes 1048608 | tf_op jit(solution)/shard_map/all_to_all | solution.py:500
  308.4 4.8 %all-to-all-start.4 = ((bf16[16,8,32,128]{3,2,1,0:T(8,128)(2,1)}), bf16[16,8,32,128]{3,2,1,0:T(8,128)(2,1)S(1)}, u32[]{:S(2)}, u32[]{:S(2)}) async-start(bf16[16,8,32,128]{3,2,1,0:T(8,128)(2,1)} %row_second.4), calls=%async_computation.4 | async-start | bytes 2097152 | tf_op jit(solution)/shard_map/all_to_all | solution.py:500
  313.1 4.8 %column.4.rest_0_ = f32[2,8,4,8,4096]{4,3,2,1,0:T(8,128)} custom-call(bf16[16,8,32,128]{3,2,1,0:T(8,128)(2,1)} %copy-done.3, bf16[512,512]{1,0:T(8,128)(2,1)} %constant.70.clone.first_ref, f32[2,16,256]{2,1,0:T(8,128)} %constant.71.clone.twist_ref), custom_call_target="tpu_custom_call" | custom-call | flops 1073741824 | bytes 4194304 | tf_op jit(solution)/shard_map/column/pallas_call | solution.py:427
  318.0 4.8 %column.5.rest_0_ = f32[2,8,4,8,4096]{4,3,2,1,0:T(8,128)} custom-call(bf16[16,8,32,128]{3,2,1,0:T(8,128)(2,1)} %copy-done.4, bf16[512,512]{1,0:T(8,128)(2,1)} %constant.70.clone.first_ref, f32[2,16,256]{2,1,0:T(8,128)} %constant.71.clone.twist_ref, f32[2,8,4,8,4096]{4,3,2,1,0:T(8,128)} %column.4.rest_0_), custom_call_target="tpu_custom_call", output_to_operand_aliasing={{}: (3, {})} | custom-call | flops 1073741824 | bytes 4194304 | tf_op jit(solution)/shard_map/column/pallas_call | solution.py:427
  322.8 4.8 %column.6.rest_0_ = f32[2,8,4,8,4096]{4,3,2,1,0:T(8,128)} custom-call(bf16[16,8,32,128]{3,2,1,0:T(8,128)(2,1)} %copy-done.5, bf16[512,512]{1,0:T(8,128)(2,1)} %constant.70.clone.first_ref, f32[2,16,256]{2,1,0:T(8,128)} %constant.71.clone.twist_ref, f32[2,8,4,8,4096]{4,3,2,1,0:T(8,128)} %column.5.rest_0_), custom_call_target="tpu_custom_call", output_to_operand_aliasing={{}: (3, {})} | custom-call | flops 1073741824 | bytes 4194304 | tf_op jit(solution)/shard_map/column/pallas_call | solution.py:427
  327.7 10.4 %all-to-all-done.4.data_ref = bf16[16,8,32,128]{3,2,1,0:T(8,128)(2,1)S(1)} async-done(((bf16[16,8,32,128]{3,2,1,0:T(8,128)(2,1)}), bf16[16,8,32,128]{3,2,1,0:T(8,128)(2,1)S(1)}, u32[]{:S(2)}, u32[]{:S(2)}) %all-to-all-start.4) | async-done | bytes 1048608 | tf_op jit(solution)/shard_map/all_to_all | solution.py:500
  338.1 1.0 copy-done.6
  339.0 4.8 %column.7 = f32[2,8,4,8,4096]{4,3,2,1,0:T(8,128)} custom-call(bf16[16,8,32,128]{3,2,1,0:T(8,128)(2,1)} %copy-done.6, bf16[512,512]{1,0:T(8,128)(2,1)} %constant.70.clone.first_ref, f32[2,16,256]{2,1,0:T(8,128)} %constant.71.clone.twist_ref, f32[2,8,4,8,4096]{4,3,2,1,0:T(8,128)} %column.6.rest_0_), custom_call_target="tpu_custom_call", output_to_operand_aliasing={{}: (3, {})} | custom-call | flops 1073741824 | bytes 4194304 | tf_op jit(solution)/shard_map/column/pallas_call | solution.py:427
  (41 shorter events, 3.7 us)
Async XLA Ops:
  9.1 31.5 %all-to-all-start.3 = ((bf16[16,64,512]{2,1,0:T(8,128)(2,1)}), bf16[16,64,512]{2,1,0:T(8,128)(2,1)S(1)}, u32[]{:S(2)}, u32[]{:S(2)}) async-start(bf16[16,64,512]{2,1,0:T(8,128)(2,1)} %get-tuple-element.10), calls=%async_computation.3 | async-start | bytes 2097152 | tf_op jit(solution)/shard_map/all_to_all | solution.py:482
  23.1 53.0 %copy-start.8 = (s32[2,2048]{1,0:T(2,128)S(1)}, s32[2,2048]{1,0:T(2,128)}, u32[]{:S(2)}) copy-start(s32[2,2048]{1,0:T(2,128)} %param.15) | copy-start | bytes 49156
  23.1 53.0 %copy-start.9 = (s32[2,2048]{1,0:T(2,128)S(1)}, s32[2,2048]{1,0:T(2,128)}, u32[]{:S(2)}) copy-start(s32[2,2048]{1,0:T(2,128)} %param.14) | copy-start | bytes 49156
  40.6 1.0 copy-start.7
  41.5 29.7 %all-to-all-start.2 = ((bf16[16,64,512]{2,1,0:T(8,128)(2,1)}), bf16[16,64,512]{2,1,0:T(8,128)(2,1)S(1)}, u32[]{:S(2)}, u32[]{:S(2)}) async-start(bf16[16,64,512]{2,1,0:T(8,128)(2,1)} %spectra_second.5), calls=%async_computation.2 | async-start | bytes 2097152 | tf_op jit(solution)/shard_map/all_to_all | solution.py:482
  71.2 69.4 %copy-start = (bf16[16,64,512]{2,1,0:T(8,128)(2,1)}, bf16[16,64,512]{2,1,0:T(8,128)(2,1)S(1)}, u32[]{:S(2)}) copy-start(bf16[16,64,512]{2,1,0:T(8,128)(2,1)S(1)} %all-to-all-done.2) | copy-start | bytes 3145732
  71.2 29.7 %all-to-all-start.1 = ((bf16[16,64,512]{2,1,0:T(8,128)(2,1)}), bf16[16,64,512]{2,1,0:T(8,128)(2,1)S(1)}, u32[]{:S(2)}, u32[]{:S(2)}) async-start(bf16[16,64,512]{2,1,0:T(8,128)(2,1)} %spectra_second.4), calls=%async_computation.1 | async-start | bytes 2097152 | tf_op jit(solution)/shard_map/all_to_all | solution.py:482
  100.9 53.5 %copy-start.1 = (bf16[16,64,512]{2,1,0:T(8,128)(2,1)}, bf16[16,64,512]{2,1,0:T(8,128)(2,1)S(1)}, u32[]{:S(2)}) copy-start(bf16[16,64,512]{2,1,0:T(8,128)(2,1)S(1)} %all-to-all-done.1) | copy-start | bytes 3145732
  100.9 29.7 %all-to-all-start = ((bf16[16,64,512]{2,1,0:T(8,128)(2,1)}), bf16[16,64,512]{2,1,0:T(8,128)(2,1)S(1)}, u32[]{:S(2)}, u32[]{:S(2)}) async-start(bf16[16,64,512]{2,1,0:T(8,128)(2,1)} %spectra_second.3), calls=%async_computation | async-start | bytes 2097152 | tf_op jit(solution)/shard_map/all_to_all | solution.py:482
  108.9 31.8 %collective-permute-start.3 = (bf16[1024,512]{1,0:T(8,128)(2,1)}, bf16[1024,512]{1,0:T(8,128)(2,1)}, u32[]{:S(2)}, u32[]{:S(2)}) collective-permute-start(bf16[1024,512]{1,0:T(8,128)(2,1)} %bitcast.42), channel_id=1, source_target_pairs={{0,16},{16,0},{1,17},{17,1},{2,18},{18,2},{3,19},{19,3},{4,20},{20... | collective-permute-start | bytes 3145736 | tf_op jit(solution)/shard_map/ppermute | solution.py:490
  112.2 43.8 %collective-permute-start.2 = (bf16[1024,512]{1,0:T(8,128)(2,1)S(1)}, bf16[1024,512]{1,0:T(8,128)(2,1)}, u32[]{:S(2)}, u32[]{:S(2)}) collective-permute-start(bf16[1024,512]{1,0:T(8,128)(2,1)S(1)} %bitcast.35), channel_id=1, source_target_pairs={{0,16},{16,0},{1,17},{17,1},{2,18},{18,2},{3,19},{19,3},{4,20},{20... | collective-permute-start | bytes 3145736 | tf_op jit(solution)/shard_map/ppermute | solution.py:490
  116.5 62.0 %collective-permute-start.1 = (bf16[1024,512]{1,0:T(8,128)(2,1)S(1)}, bf16[1024,512]{1,0:T(8,128)(2,1)}, u32[]{:S(2)}, u32[]{:S(2)}) collective-permute-start(bf16[1024,512]{1,0:T(8,128)(2,1)S(1)} %bitcast.37), channel_id=1, source_target_pairs={{0,16},{16,0},{1,17},{17,1},{2,18},{18,2},{3,19},{19,3},{4,20},{20... | collective-permute-start | bytes 3145736 | tf_op jit(solution)/shard_map/ppermute | solution.py:490
  130.6 23.8 %copy-start.2 = (bf16[16,64,512]{2,1,0:T(8,128)(2,1)}, bf16[16,64,512]{2,1,0:T(8,128)(2,1)S(1)}, u32[]{:S(2)}) copy-start(bf16[16,64,512]{2,1,0:T(8,128)(2,1)S(1)} %all-to-all-done) | copy-start | bytes 3145732
  130.6 70.3 %collective-permute-start = (bf16[1024,512]{1,0:T(8,128)(2,1)S(1)}, bf16[1024,512]{1,0:T(8,128)(2,1)}, u32[]{:S(2)}, u32[]{:S(2)}) collective-permute-start(bf16[1024,512]{1,0:T(8,128)(2,1)S(1)} %bitcast.39), channel_id=1, source_target_pairs={{0,16},{16,0},{1,17},{17,1},{2,18},{18,2},{3,19},{19,3},{4,20},{20... | collective-permute-start | bytes 3145736 | tf_op jit(solution)/shard_map/ppermute | solution.py:490
  218.2 30.8 %all-to-all-start.7 = ((bf16[16,8,32,128]{3,2,1,0:T(8,128)(2,1)}), bf16[16,8,32,128]{3,2,1,0:T(8,128)(2,1)S(1)}, u32[]{:S(2)}, u32[]{:S(2)}) async-start(bf16[16,8,32,128]{3,2,1,0:T(8,128)(2,1)} %row_second.7), calls=%async_computation.7 | async-start | bytes 2097152 | tf_op jit(solution)/shard_map/all_to_all | solution.py:500
  249.0 37.4 %copy-start.3 = (bf16[16,8,32,128]{3,2,1,0:T(8,128)(2,1)}, bf16[16,8,32,128]{3,2,1,0:T(8,128)(2,1)S(1)}, u32[]{:S(2)}) copy-start(bf16[16,8,32,128]{3,2,1,0:T(8,128)(2,1)S(1)} %all-to-all-done.7.data_ref) | copy-start | bytes 3145732
  249.0 29.7 %all-to-all-start.6 = ((bf16[16,8,32,128]{3,2,1,0:T(8,128)(2,1)}), bf16[16,8,32,128]{3,2,1,0:T(8,128)(2,1)S(1)}, u32[]{:S(2)}, u32[]{:S(2)}) async-start(bf16[16,8,32,128]{3,2,1,0:T(8,128)(2,1)} %row_second.6), calls=%async_computation.6 | async-start | bytes 2097152 | tf_op jit(solution)/shard_map/all_to_all | solution.py:500
  278.7 39.3 %copy-start.4 = (bf16[16,8,32,128]{3,2,1,0:T(8,128)(2,1)}, bf16[16,8,32,128]{3,2,1,0:T(8,128)(2,1)S(1)}, u32[]{:S(2)}) copy-start(bf16[16,8,32,128]{3,2,1,0:T(8,128)(2,1)S(1)} %all-to-all-done.6.data_ref) | copy-start | bytes 3145732
  278.7 29.7 %all-to-all-start.5 = ((bf16[16,8,32,128]{3,2,1,0:T(8,128)(2,1)}), bf16[16,8,32,128]{3,2,1,0:T(8,128)(2,1)S(1)}, u32[]{:S(2)}, u32[]{:S(2)}) async-start(bf16[16,8,32,128]{3,2,1,0:T(8,128)(2,1)} %row_second.5), calls=%async_computation.5 | async-start | bytes 2097152 | tf_op jit(solution)/shard_map/all_to_all | solution.py:500
  308.4 14.5 %copy-start.5 = (bf16[16,8,32,128]{3,2,1,0:T(8,128)(2,1)}, bf16[16,8,32,128]{3,2,1,0:T(8,128)(2,1)S(1)}, u32[]{:S(2)}) copy-start(bf16[16,8,32,128]{3,2,1,0:T(8,128)(2,1)S(1)} %all-to-all-done.5.data_ref) | copy-start | bytes 3145732
  308.4 29.7 %all-to-all-start.4 = ((bf16[16,8,32,128]{3,2,1,0:T(8,128)(2,1)}), bf16[16,8,32,128]{3,2,1,0:T(8,128)(2,1)S(1)}, u32[]{:S(2)}, u32[]{:S(2)}) async-start(bf16[16,8,32,128]{3,2,1,0:T(8,128)(2,1)} %row_second.4), calls=%async_computation.4 | async-start | bytes 2097152 | tf_op jit(solution)/shard_map/all_to_all | solution.py:500
  338.0 1.0 copy-start.6

commit v2 on v1

--- a/solution.py
+++ b/solution.py
@@ -71,9 +71,14 @@
     first = complex_table(turn(np.outer(index, index), count, 1.0), 1.0 / math.sqrt(TILE))
     first = first.reshape(2, 2, n_gx, blocks, count)
     first = first.transpose(2, 1, 3, 0, 4).reshape(2 * count, 2 * count)
-    angle = turn(np.outer(np.arange(BR), index), TILE, 1.0)
-    twist = np.stack([np.cos(angle), np.sin(angle)]).astype(np.float32)
-    return halves(first)[0], twist
+    return halves(first)[0]
+
+
+def column_twist():
+    shape = (BR, TILE // BR)
+    product = lax.broadcasted_iota(jnp.int32, shape, 0) * lax.broadcasted_iota(jnp.int32, shape, 1)
+    angle = 2.0 * math.pi / TILE * product.astype(F32)
+    return jnp.cos(angle), jnp.sin(angle)
 
 
 def times(value, factor):
@@ -128,11 +133,13 @@
 
 def channel_rows(n_gx, scratch, out_ref):
     stride = scratch.shape[0] // PACK
-    per = out_ref.shape[2] // FRADIX
-    for d in range(n_gx):
-        for t in range(per):
-            piece = scratch[pl.ds(d * per + t, PACK, stride=stride), :]
-            out_ref[d, :, t * FRADIX : (t + 1) * FRADIX] = piece.astype(BF16)
+    channels = out_ref.shape[1]
+    per = out_ref.shape[3] // FRADIX
+    for o in range(channels):
+        for d in range(n_gx):
+            for t in range(per):
+                piece = scratch[pl.ds((o * n_gx + d) * per + t, PACK, stride=stride), :]
+                out_ref[d, o, :, t * FRADIX : (t + 1) * FRADIX] = piece.astype(BF16)
 
 
 def second_stage(pair, high_ref, low_ref, second_ref, scratch):
@@ -172,64 +179,65 @@
     return pl.BlockSpec(x.shape, lambda *i: (0,) * x.ndim)
 
 
-def spectra_first_call(volts, n_gx, out_dev):
-    inputs = volts.shape[0]
-    first, twist, second = spectra_tables(n_gx, out_dev)
-    rows = 2 * FRADIX // out_dev
-    second = second[:rows]
+def spectra_call(volts, turned, tables, n_gx, out_dev, start, stop):
+    first, twist, second = tables
+    per = 2 * FRADIX // out_dev
+    second = second[start * per : stop * per]
     depth = 2 * AVG
-    turned = jax.ShapeDtypeStruct((inputs, FRADIX, 2 * FRADIX), BF16)
+    channels = stop - start
+    lead = volts if turned is None else turned[0]
+    inputs = lead.shape[0]
+    turned_shape = jax.ShapeDtypeStruct((inputs, FRADIX, 2 * FRADIX), BF16)
     turned_spec = pl.BlockSpec((PACK, FRADIX, 2 * FRADIX), lambda i: (i, 0, 0))
-    return pl.pallas_call(
-        functools.partial(spectra_first_kernel, n_gx),
-        grid=(inputs // PACK,),
-        in_specs=[
-            pl.BlockSpec((PACK, 2 * FRADIX, FRADIX), lambda i: (i, 0, 0)),
-            whole(first),
-            whole(twist),
-            whole(second),
-        ],
-        out_specs=[turned_spec, turned_spec, pl.BlockSpec((n_gx, PACK, depth), lambda i: (0, i, 0))],
-        out_shape=[turned, turned, jax.ShapeDtypeStruct((n_gx, inputs, depth), BF16)],
-        scratch_shapes=[pltpu.VMEM((PACK * (rows + SUB), FRADIX), F32)],
-        name="spectra_first",
-    )(volts, first, twist, second)
-
-
-def spectra_second_call(high, low, n_gx, out_dev, o):
-    inputs = high.shape[0]
-    rows = 2 * FRADIX // out_dev
-    second = spectra_tables(n_gx, out_dev)[2][o * rows : (o + 1) * rows]
-    depth = 2 * AVG
-    turned_spec = pl.BlockSpec((PACK, FRADIX, 2 * FRADIX), lambda i: (i, 0, 0))
+    out_spec = pl.BlockSpec((n_gx, channels, PACK, depth), lambda i: (0, 0, i, 0))
+    out_shape = jax.ShapeDtypeStruct((n_gx, channels, inputs, depth), BF16)
+    scratch = [pltpu.VMEM((PACK * (channels * per + SUB), FRADIX), F32)]
+    if turned is None:
+        return pl.pallas_call(
+            functools.partial(spectra_first_kernel, n_gx),
+            grid=(inputs // PACK,),
+            in_specs=[
+                pl.BlockSpec((PACK, 2 * FRADIX, FRADIX), lambda i: (i, 0, 0)),
+                whole(first),
+                whole(twist),
+                whole(second),
+            ],
+            out_specs=[turned_spec, turned_spec, out_spec],
+            out_shape=[turned_shape, turned_shape, out_shape],
+            scratch_shapes=scratch,
+            name="spectra_first",
+        )(volts, first, twist, second)
     return pl.pallas_call(
         functools.partial(spectra_second_kernel, n_gx),
         grid=(inputs // PACK,),
         in_specs=[turned_spec, turned_spec, whole(second)],
-        out_specs=pl.BlockSpec((n_gx, PACK, depth), lambda i: (0, i, 0)),
-        out_shape=jax.ShapeDtypeStruct((n_gx, inputs, depth), BF16),
-        scratch_shapes=[pltpu.VMEM((PACK * (rows + SUB), FRADIX), F32)],
+        out_specs=out_spec,
+        out_shape=out_shape,
+        scratch_shapes=scratch,
         name="spectra_second",
-    )(high, low, second)
-
-
-def correlate(x_ref, vis, factor):
-    nin, depth = x_ref.shape
+    )(*turned, second)
+
+
+def correlate(x_ref, slot, vis, factor):
+    sources, _, inputs, depth = x_ref.shape
+    nin = sources * inputs
     half = depth // 2
-    panel = 2 * BC
+    group = sources // 4
+    panel = group * inputs
 
     def one(p, carry):
         base = pl.multiple_of(p * panel, panel)
-        x = x_ref[pl.ds(base, panel), :]
+        x = x_ref[pl.ds(p * group, group), slot].reshape(panel, depth)
         swapped = jnp.concatenate([x[:, half:], -x[:, :half]], axis=1)
         left = jnp.concatenate([x, swapped], axis=0)
-        gram = (dot_nt(left, x_ref[...]) * factor).astype(BF16)
+        right = x_ref[:, slot].reshape(nin, depth)
+        gram = (dot_nt(left, right) * factor).astype(BF16)
         for e in range(nin // BC):
             vis[0, e, pl.ds(base, panel), :] = gram[:panel, e * BC : (e + 1) * BC]
             vis[1, e, pl.ds(base, panel), :] = gram[panel:, e * BC : (e + 1) * BC]
         return carry
 
-    lax.fori_loop(0, nin // panel, one, 0)
+    lax.fori_loop(0, sources // group, one, 0)
 
 
 def place_blocks(which, count_ref, list_ref, vis, grid):
@@ -249,47 +257,69 @@
     lax.fori_loop(0, count_ref[which], place, 0)
 
 
-def gram_kernel(streams, first_call, factor, count_ref, list_ref, *rest):
-    x_refs, rest = rest[:streams], rest[streams:]
-    out_ref, vis, grid, sem = rest[-4:]
+LOADS = 8
+
+
+def split_copies(source, target, sems):
+    share = target.shape[1] // LOADS
+    copies = []
+    for i in range(LOADS):
+        at = pl.ds(i * share, share)
+        copies.append(pltpu.make_async_copy(source.at[:, at], target.at[:, at], sems.at[i]))
+    return copies
+
+
+def gram_kernel(slots, first_call, factor, count_ref, list_ref, *rest):
+    x_refs, rest = rest[: len(slots)], rest[len(slots) :]
+    out_ref, vis, grid, sems = rest[-4:]
     cells = grid.shape[1]
     if first_call:
+
         def clear(i, carry):
             grid[:, pl.ds(i * SUB, SUB)] = jnp.zeros((2, SUB, BR, BC), F32)
             return carry
 
         lax.fori_loop(0, cells // SUB, clear, 0)
     else:
-        load = pltpu.make_async_copy(rest[0], grid, sem)
-        load.start()
-    for which, x_ref in enumerate(x_refs):
-        correlate(x_ref, vis, factor)
-        if which == 0 and not first_call:
-            load.wait()
-        place_blocks(which, count_ref, list_ref, vis, grid)
-    store = pltpu.make_async_copy(grid, out_ref, sem)
-    store.start()
-    store.wait()
+        loads = split_copies(rest[0], grid, sems)
+        for load in loads:
+            load.start()
+    which = 0
+    for x_ref, many in zip(x_refs, slots):
+        for slot in range(many):
+            correlate(x_ref, slot, vis, factor)
+            if which == 0 and not first_call:
+                for load in loads:
+                    load.wait()
+            place_blocks(which, count_ref, list_ref, vis, grid)
+            which += 1
+    stores = split_copies(grid, out_ref, sems)
+    for store in stores:
+        store.start()
+    for store in stores:
+        store.wait()
 
 
 def gram_call(counts, lists, streams, grid, cells, factor):
     first_call = grid is None
     shape = (2, cells, BR, BC)
-    nin, depth = streams[0].shape
+    sources, _, inputs, depth = streams[0].shape
+    nin = sources * inputs
+    slots = tuple(x.shape[1] for x in streams)
     any_spec = pl.BlockSpec(memory_space=pl.ANY)
     vmem = pl.BlockSpec(memory_space=pltpu.VMEM)
     smem = pl.BlockSpec(memory_space=pltpu.SMEM)
     args = (counts, lists) + tuple(streams) + (() if first_call else (grid,))
-    flops = len(streams) * 4 * nin * nin * depth
+    flops = sum(slots) * 4 * nin * nin * depth
     return pl.pallas_call(
-        functools.partial(gram_kernel, len(streams), first_call, factor),
+        functools.partial(gram_kernel, slots, first_call, factor),
         in_specs=[smem, smem] + [vmem] * len(streams) + ([] if first_call else [any_spec]),
         out_specs=any_spec,
         out_shape=jax.ShapeDtypeStruct(shape, F32),
         scratch_shapes=[
             pltpu.VMEM((2, nin // BC, nin, BC), BF16),
             pltpu.VMEM(shape, F32),
-            pltpu.SemaphoreType.DMA,
+            pltpu.SemaphoreType.DMA((LOADS,)),
         ],
         input_output_aliases={} if first_call else {2 + len(streams): 0},
         cost_estimate=pl.CostEstimate(flops=flops, transcendentals=0, bytes_accessed=2**24),
@@ -297,65 +327,66 @@
     )(*args)
 
 
-def gram_row_kernel(factor, count_ref, list_ref, x_ref, grid_ref, twist_ref, out_ref, vis, grid, scratch, sem):
+def row_block(block, grid, twist_ref, stage, turned):
     cols = TILE // BC
+    inner = cols // 4
+    for h in range(BR // SUB):
+        rows = slice(h * SUB, (h + 1) * SUB)
+        for q in range(4):
+            at = [block * cols + 4 * m + q for m in range(inner)]
+            values = butterflies([(grid[0, c, rows], grid[1, c, rows]) for c in at], 1.0)
+            for k in range(inner):
+                re, im = fixed_turn(values[k], q * k, cols, 1.0)
+                stage[h, 0, q * inner + k] = re
+                stage[h, 1, q * inner + k] = im
+    for k in range(inner):
+        halves_of = []
+        for h in range(BR // SUB):
+            values = [(stage[h, 0, q * inner + k], stage[h, 1, q * inner + k]) for q in range(4)]
+            values = butterflies(values, 1.0)
+            for m in range(4):
+                at = k + m * inner
+                if at:
+                    factor = (twist_ref[0, at : at + 1, :], twist_ref[1, at : at + 1, :])
+                    values[m] = times(values[m], factor)
+            halves_of.append(values)
+        for m in range(4):
+            at = slice((k + m * inner) * BR, (k + m * inner + 1) * BR)
+            for part in range(2):
+                both = jnp.concatenate([values[m][part] for values in halves_of], axis=0)
+                turned[block, at, part * BC : (part + 1) * BC] = both.astype(BF16)
+
+
+def rows_kernel(
+    factor, count_ref, list_ref, x_ref, grid_ref, twist_ref, second_ref, out_ref, vis, grid, stage, turned, scratch, sems
+):
+    blocks = turned.shape[0]
+    lanes = SUB * BR
+    rows = 2 * BC
     step = pl.program_id(0)
 
     @pl.when(step == 0)
     def _():
-        load = pltpu.make_async_copy(grid_ref, grid, sem)
-        load.start()
-        correlate(x_ref, vis, factor)
-        load.wait()
-        place_blocks(0, count_ref, list_ref, vis, grid)
-
-    for h in range(BR // SUB):
-        rows = slice(h * SUB, (h + 1) * SUB)
-        values = [(grid[0, step * cols + c, rows], grid[1, step * cols + c, rows]) for c in range(cols)]
-        values = butterflies(values, 1.0)
-        for k in range(cols):
-            factor_k = (twist_ref[0, k : k + 1, :], twist_ref[1, k : k + 1, :])
-            re, im = times(values[k], factor_k)
-            at = slice(k * BR + h * SUB, k * BR + (h + 1) * SUB)
-            scratch[at, :BC] = re
-            scratch[at, BC:] = im
-    out_ref[0] = scratch[...].astype(BF16)
-
-
-def gram_row_call(counts, lists, stream, grid, cells, factor, twist):
-    nin, _ = stream.shape
-    cols = TILE // BC
-    blocks = cells // cols
-    smem = pl.BlockSpec(memory_space=pltpu.SMEM)
-    return pl.pallas_call(
-        functools.partial(gram_row_kernel, factor),
-        grid=(blocks,),
-        in_specs=[
-            smem,
-            smem,
-            pl.BlockSpec(memory_space=pltpu.VMEM),
-            pl.BlockSpec(memory_space=pl.ANY),
-            whole(twist),
-        ],
-        out_specs=pl.BlockSpec((1, cols * BR, 2 * BC), lambda i: (i, 0, 0)),
-        out_shape=jax.ShapeDtypeStruct((blocks, cols * BR, 2 * BC), BF16),
-        scratch_shapes=[
-            pltpu.VMEM((2, nin // BC, nin, BC), BF16),
-            pltpu.VMEM((2, cells, BR, BC), F32),
-            pltpu.VMEM((cols * BR, 2 * BC), F32),
-            pltpu.SemaphoreType.DMA,
-        ],
-        name="gram_row",
-    )(counts, lists, stream, grid, twist)
-
-
-def row_second_kernel(data_ref, second_ref, out_ref, scratch):
-    blocks = data_ref.shape[0]
-    lanes = SUB * BR
-    rows = 2 * BC
+        loads = split_copies(grid_ref, grid, sems)
+        for load in loads:
+            load.start()
+        for slot in range(x_ref.shape[1]):
+            correlate(x_ref, slot, vis, factor)
+            if slot == 0:
+                for load in loads:
+                    load.wait()
+            place_blocks(slot, count_ref, list_ref, vis, grid)
+
+        def one(block, carry):
+            row_block(block, grid, twist_ref, stage, turned)
+            return carry
+
+        lax.fori_loop(0, blocks, one, 0)
+
     stride = scratch.shape[0] // blocks
+    at_lane = pl.ds(pl.multiple_of(step * lanes, lanes), lanes)
     for b in range(blocks // 2):
-        data = data_ref[2 * b : 2 * b + 2].reshape(2 * lanes, rows)
+        data = turned[2 * b : 2 * b + 2, at_lane].reshape(2 * lanes, rows)
         z = dot_nt(second_ref[...], data)
         for u in range(2):
             at = (2 * b + u) * stride
@@ -369,77 +400,81 @@
                 out_ref[d, k, part * blocks : (part + 1) * blocks, :] = piece.astype(BF16)
 
 
-def row_second_call(data, second, n_gx, start, count):
-    blocks = data.shape[0]
+def rows_call(counts, lists, stream, grid, cells, factor, twist, second, n_gx):
+    sources, _, inputs, _ = stream.shape
+    nin = sources * inputs
+    cols = TILE // BC
+    blocks = cells // cols
     lanes = SUB * BR
     lows = BC // n_gx
+    smem = pl.BlockSpec(memory_space=pltpu.SMEM)
     return pl.pallas_call(
-        row_second_kernel,
-        grid=(count,),
+        functools.partial(rows_kernel, factor),
+        grid=(cols // SUB,),
         in_specs=[
-            pl.BlockSpec((blocks, lanes, 2 * BC), lambda i: (0, start + i, 0)),
+            smem,
+            smem,
+            whole(stream),
+            pl.BlockSpec(memory_space=pl.ANY),
+            whole(twist),
             whole(second),
         ],
         out_specs=pl.BlockSpec((n_gx, lows, 2 * blocks, lanes), lambda i: (0, 0, 0, i)),
-        out_shape=jax.ShapeDtypeStruct((n_gx, lows, 2 * blocks, count * lanes), BF16),
-        scratch_shapes=[pltpu.VMEM((blocks * (2 * BC + SUB), lanes), F32)],
-        cost_estimate=pl.CostEstimate(flops=2**31, transcendentals=0, bytes_accessed=2**22),
-        name="row_second",
-    )(data, second)
-
-
-COLUMN_STEP = 2
-
-
-def column_kernel(data_ref, first_ref, twist_ref, *rest):
-    out_ref, scratch = rest[-2], rest[-1]
+        out_shape=jax.ShapeDtypeStruct((n_gx, lows, 2 * blocks, cols * BR), BF16),
+        scratch_shapes=[
+            pltpu.VMEM((2, nin // BC, nin, BC), BF16),
+            pltpu.VMEM((2, cells, BR, BC), F32),
+            pltpu.VMEM((BR // SUB, 2, cols, SUB, BC), F32),
+            pltpu.VMEM((blocks, cols * BR, 2 * BC), BF16),
+            pltpu.VMEM((blocks * (2 * BC + SUB), lanes), F32),
+            pltpu.SemaphoreType.DMA((LOADS,)),
+        ],
+        name="rows",
+    )(counts, lists, stream, grid, twist, second)
+
+
+def column_kernel(data_ref, first_ref, cos_ref, sin_ref, out_ref, scratch):
     n_gx, _, rows, lanes = data_ref.shape
     count = TILE // BR
-    span = scratch.shape[0] // COLUMN_STEP
-    for q in range(COLUMN_STEP):
-        data = data_ref[:, q].reshape(n_gx * rows, lanes)
-        mixed = dot_tn(data, first_ref[...])
-        for b in range(2 * count // BC):
-            scratch[q * span + b * lanes : q * span + (b + 1) * lanes, :] = mixed[:, b * BC : (b + 1) * BC]
-    for q in range(COLUMN_STEP):
+    mixed = dot_tn(data_ref[:, 0].reshape(n_gx * rows, lanes), first_ref[...])
+    for b in range(2 * count // BC):
+        scratch[b * lanes : (b + 1) * lanes, :] = mixed[:, b * BC : (b + 1) * BC]
+    for g in range(lanes // (SUB * BR)):
         for b in range(count // BC):
             lane = slice(b * BC, (b + 1) * BC)
             values = []
             for r in range(BR):
+                at = g * SUB * BR + r
                 value = (
-                    scratch[pl.ds(q * span + b * lanes + r, SUB, stride=BR), :],
-                    scratch[pl.ds(q * span + (count // BC + b) * lanes + r, SUB, stride=BR), :],
+                    scratch[pl.ds(b * lanes + at, SUB, stride=BR), :],
+                    scratch[pl.ds((count // BC + b) * lanes + at, SUB, stride=BR), :],
                 )
-                factor = (twist_ref[0, r : r + 1, lane], twist_ref[1, r : r + 1, lane])
+                factor = (cos_ref[r : r + 1, lane], sin_ref[r : r + 1, lane])
                 values.append(times(value, factor) if r else value)
             values = butterflies(values, 1.0)
             for k in range(BR):
                 at = slice(k * count + b * BC, k * count + (b + 1) * BC)
-                out_ref[0, q, 0, :, at] = values[k][0]
-                out_ref[1, q, 0, :, at] = values[k][1]
-
-
-def column_call(data, first, twist, image, part, chunk, chunks):
-    n_gx, lows, rows, _ = data.shape
-    lanes = SUB * BR
-    alias = image is not None
-    shape = (2, lows, chunks, SUB, TILE)
+                out_ref[0, 0, g * SUB : (g + 1) * SUB, at] = values[k][0]
+                out_ref[1, 0, g * SUB : (g + 1) * SUB, at] = values[k][1]
+
+
+def column_call(data, first, cos, sin):
+    n_gx, lows, rows, lanes = data.shape
+    cols = TILE // BC
     return pl.pallas_call(
         column_kernel,
-        grid=(lows // COLUMN_STEP,),
+        grid=(lows,),
         in_specs=[
-            pl.BlockSpec((n_gx, COLUMN_STEP, rows, lanes), lambda i: (0, i, 0, part)),
+            pl.BlockSpec((n_gx, 1, rows, lanes), lambda i: (0, i, 0, 0)),
             whole(first),
-            whole(twist),
-        ]
-        + ([pl.BlockSpec(memory_space=pl.ANY)] if alias else []),
-        out_specs=pl.BlockSpec((2, COLUMN_STEP, 1, SUB, TILE), lambda i: (0, i, chunk, 0, 0)),
-        out_shape=jax.ShapeDtypeStruct(shape, F32),
-        scratch_shapes=[pltpu.VMEM((COLUMN_STEP * 2 * (TILE // BR) // BC * lanes, BC), F32)],
-        input_output_aliases={3: 0} if alias else {},
-        cost_estimate=pl.CostEstimate(flops=2**30, transcendentals=0, bytes_accessed=2**22),
+            whole(cos),
+            whole(sin),
+        ],
+        out_specs=pl.BlockSpec((2, 1, cols, TILE), lambda i: (0, i, 0, 0)),
+        out_shape=jax.ShapeDtypeStruct((2, lows, cols, TILE), F32),
+        scratch_shapes=[pltpu.VMEM((2 * (TILE // BR) // BC * lanes, BC), F32)],
         name="column",
-    )(data, first, twist, *((image,) if alias else ()))
+    )(data, first, cos, sin)
 
 
 def work_lists(tile_of, cell_of, me, out_dev, cells):
@@ -455,17 +490,12 @@
     return jnp.sum(number, axis=2), lists
 
 
-def row_chunks(groups):
-    return (1,) * groups
-
-
 def pair_plan(voltages, tile_of, cell_of):
     n_gx = lax.axis_size("gx")
     _, st_dev, pols, spectra, _, fine = voltages.shape
     inputs = st_dev * pols
     out_dev = fine // (n_gx * AVG)
     cells = (TILE // n_gx // BR) * (TILE // BC)
-    cols = TILE // BC
     me = lax.axis_index("grp")
     counts, lists = work_lists(tile_of, cell_of, me, out_dev, cells)
     swap = jnp.where(me == 0, jnp.arange(2), jnp.arange(2)[::-1])
@@ -474,33 +504,39 @@
     volts = voltages.reshape(inputs, 2, FRADIX, FRADIX).transpose(0, 2, 1, 3)
     volts = volts.reshape(inputs, 2 * FRADIX, FRADIX)
     factor = 1.0 / math.sqrt(spectra * AVG)
-    high, low, spec = spectra_first_call(volts, n_gx, out_dev)
-    grid = None
-    for o in range(out_dev):
-        if o:
-            spec = spectra_second_call(high, low, n_gx, out_dev, o)
-        mine = lax.all_to_all(spec, "gx", split_axis=0, concat_axis=0, tiled=True)
-        mine = mine.reshape(n_gx * inputs, 2 * AVG)
-        number, list_of = counts[0, o : o + 1], lists[0, o : o + 1]
-        if o:
-            number = jnp.concatenate([number, counts[1, o - 1 : o]])
-            list_of = jnp.concatenate([list_of, lists[1, o - 1 : o]])
-        streams = (mine, other) if o else (mine,)
-        grid = gram_call(number, list_of, streams, grid, cells, factor)
-        other = lax.ppermute(mine, "grp", [(0, 1), (1, 0)])
+    tables = spectra_tables(n_gx, out_dev)
+    front, middle, last = 0, out_dev // 2, out_dev - 1
+
+    def exchange(spec):
+        return lax.all_to_all(spec, "gx", split_axis=0, concat_axis=0, tiled=True)
+
+    def swap_groups(data):
+        return lax.ppermute(data, "grp", [(0, 1), (1, 0)])
+
+    def work(grid, *items):
+        number = jnp.concatenate([counts[g, start:stop] for g, start, stop, _ in items])
+        list_of = jnp.concatenate([lists[g, start:stop] for g, start, stop, _ in items])
+        streams = [data for _, _, _, data in items]
+        return gram_call(number, list_of, streams, grid, cells, factor)
+
+    high, low, spec_a = spectra_call(volts, None, tables, n_gx, out_dev, front, middle)
+    turned = (high, low)
+    mine_a = exchange(spec_a)
+    spec_c = spectra_call(None, turned, tables, n_gx, out_dev, last, out_dev)
+    other_c = swap_groups(spec_c)
+    spec_b = spectra_call(None, turned, tables, n_gx, out_dev, middle, last)
+    other_a = swap_groups(mine_a)
+    mine_b = exchange(spec_b)
+    grid = work(None, (0, front, middle, mine_a))
+    other_b = swap_groups(mine_b)
+    both_c = exchange(jnp.concatenate([spec_c, other_c], axis=1))
+    grid = work(grid, (0, middle, last, mine_b), (1, front, middle, other_a))
+    grid = work(grid, (1, middle, last, other_b))
     twist, second = row_tables()
-    last = out_dev - 1
-    mixed = gram_row_call(counts[1, last:], lists[1, last:], other, grid, cells, factor, twist)
-    first, turned = column_tables(n_gx)
-    image = None
-    start = 0
-    groups = cols // SUB
-    for size in row_chunks(groups):
-        rows = row_second_call(mixed, second, n_gx, start, size)
-        data = lax.all_to_all(rows, "gx", split_axis=0, concat_axis=0, tiled=True)
-        for part in range(size):
-            image = column_call(data, first, turned, image, part, start + part, groups)
-        start += size
+    rows = rows_call(counts[:, last], lists[:, last], both_c, grid, cells, factor, twist, second, n_gx)
+    data = exchange(rows)
+    cos, sin = column_twist()
+    image = column_call(data, column_tables(n_gx), cos, sin)
     return image.reshape(1, 2, TILE // n_gx, TILE)
 
 
@@ -578,6 +614,8 @@
         and (st_dev * pols) % PACK == 0
         and fine % (gx_count * AVG) == 0
         and TILE // gx_count // BR == PACK
+        and fine // (gx_count * AVG) >= 4
+        and gx_count % 4 == 0
     )
 
 

time: 346 us -> 320 us (0.925)
  Pallas kernels: 127 us -> 95 us
  blocking collectives: 0 us -> 32 us
  starting transfers between devices: 42.9 us -> 17.6 us
  local copies, waits for them, and re-layouts: 4.9 us -> 8.95 us
  waiting for transfers between devices: 157 us -> 153 us
    all_to_all x8 -> x3, waiting for transfers between devices: 137 us -> 101 us  [exchange(): return lax.all_to_all(spec, 'gx', split_axis=0, concat_axis=0, tiled=True)]
    all_to_all x0 -> x1, blocking collectives: none -> 32 us  [exchange(): return lax.all_to_all(spec, 'gx', split_axis=0, concat_axis=0, tiled=True)]
    pallas_call x17 -> x8, Pallas kernels: 127 us -> 95 us  [the longest x3 41 us: gram_call(): pl.pallas_call(functools.partial(gram_kernel, slots, first_call, factor),...]
    ppermute x4 -> x3, waiting for transfers between devices: 20.1 us -> 51.9 us  [swap_groups(): return lax.ppermute(data, 'grp', [(0, 1), (1, 0)])]
    all_to_all x8 -> x3, starting transfers between devices: 41 us -> 15.9 us  [exchange(): return lax.all_to_all(spec, 'gx', split_axis=0, concat_axis=0, tiled=True)]
    concatenate x6 -> x3, other arithmetic: 7.29 us -> 4.57 us  [the longest x1 2.76 us: pair_plan(): both_c = exchange(jnp.concatenate([spec_c, other_c], axis=1))]
  transfers between devices with their start and end apart: 12 -> 6, of which waited for: 11 -> 5; matrix products, arithmetic and copies ran while one was open for 4% -> 5% of each run, Pallas kernels for 28% -> 15%
where the time goes in v2:
time: 320 us; the launch traced here: 316 us
  waiting for transfers between devices  153 us (48%)
  Pallas kernels  95 us (30%)
  blocking collectives  32 us (10%)
  starting transfers between devices  17.6 us (6%)
  other arithmetic  9.53 us (3%)
  local copies, waits for them, and re-layouts  8.95 us (3%)
    all_to_all x3, waiting for transfers between devices, exchange(): return lax.all_to_all(spec, 'gx', split_axis=0, concat_axis=0, tiled=True)  101 us
    ppermute x3, waiting for transfers between devices, swap_groups(): return lax.ppermute(data, 'grp', [(0, 1), (1, 0)])  51.9 us
    pallas_call x3, Pallas kernels, gram_call(): pl.pallas_call(functools.partial(gram_kernel, slots, first_call, factor),...  41 us
    all_to_all x1, blocking collectives, exchange(): return lax.all_to_all(spec, 'gx', split_axis=0, concat_axis=0, tiled=True)  32 us
    pallas_call x1, Pallas kernels, rows_call(): pl.pallas_call(functools.partial(rows_kernel, factor), grid=(cols // SUB,...  17.8 us
    all_to_all x3, starting transfers between devices, exchange(): return lax.all_to_all(spec, 'gx', split_axis=0, concat_axis=0, tiled=True)  15.9 us
    pallas_call x2, Pallas kernels, spectra_call(): pl.pallas_call(functools.partial(spectra_second_kernel, n_gx), grid=(inpu...  14.9 us
    pallas_call x1, Pallas kernels, column_call(): pl.pallas_call(column_kernel, grid=(lows,), in_specs=[pl.BlockSpec((n_gx,...  11.7 us
  transfers between devices with their start and end apart: 6, of which 5 were waited for; matrix products, arithmetic and copies ran while one was open for 5% of the time, Pallas kernels for 15%

profile of v2, /device:TPU:13, one launch (start us, length us, event | category | flops | bytes accessed | tf_op | source)
XLA Modules:
  0.0 316.0 jit_solution(8256791892499297727)
XLA Ops:
  0.0 9.6 %spectra_first.1 = (bf16[64,128,256]{2,1,0:T(8,128)(2,1)}, bf16[64,128,256]{2,1,0:T(8,128)(2,1)}, bf16[16,2,64,512]{3,2,1,0:T(8,128)(2,1)}) custom-call(bf16[64,256,128]{2,1,0:T(8,128)(2,1)} %bitcast.25, bf16[256,512]{1,0:T(8,128)(2,1)} %constant.60.clone.first_ref, f32[2,128,128]{2,1,0:T(8,128)} %constant.61.clone.twist_ref, ...), custom_call_target="tpu_custom_call" | custom-call | tf_op jit(solution)/shard_map/spectra_first/pallas_call | solution.py:196
  9.6 7.5 %spectra_second.3 = bf16[16,1,64,512]{3,2,1,0:T(8,128)(2,1)} custom-call(bf16[64,128,256]{2,1,0:T(8,128)(2,1)} %get-tuple-element.8.high_ref, bf16[64,128,256]{2,1,0:T(8,128)(2,1)} %get-tuple-element.9.low_ref, bf16[64,768]{1,0:T(8,128)(2,1)} %constant.64.clone.second_ref), custom_call_target="tpu_custom_call" | custom-call | tf_op jit(solution)/shard_map/spectra_second/pallas_call | solution.py:210
  17.1 32.0 %all_to_all.20.rest_0_ = bf16[16,1,64,512]{3,2,1,0:T(8,128)(2,1)} all-to-all(bf16[16,1,64,512]{3,2,1,0:T(8,128)(2,1)} %spectra_second.3), channel_id=1, replica_groups=mesh['grp'=2,'gx'=16] {'gx'}, dimensions={0} | all-to-all | bytes 2097152 | tf_op jit(solution)/shard_map/all_to_all | solution.py:511
  49.1 4.4 %all-to-all-start.2 = ((bf16[16,2,64,512]{3,2,1,0:T(8,128)(2,1)}), bf16[16,2,64,512]{3,2,1,0:T(8,128)(2,1)S(1)}, u32[]{:S(2)}, u32[]{:S(2)}) async-start(bf16[16,2,64,512]{3,2,1,0:T(8,128)(2,1)} %get-tuple-element.10), calls=%async_computation.2 | async-start | bytes 4194304 | tf_op jit(solution)/shard_map/all_to_all | solution.py:511
  53.5 7.5 %spectra_second.2 = bf16[16,1,64,512]{3,2,1,0:T(8,128)(2,1)} custom-call(bf16[64,128,256]{2,1,0:T(8,128)(2,1)} %get-tuple-element.8.high_ref, bf16[64,128,256]{2,1,0:T(8,128)(2,1)} %get-tuple-element.9.low_ref, bf16[64,768]{1,0:T(8,128)(2,1)} %constant.63.clone.second_ref), custom_call_target="tpu_custom_call" | custom-call | tf_op jit(solution)/shard_map/spectra_second/pallas_call | solution.py:210
  60.9 0.2 collective-permute-start
  61.1 0.0 copy-done.4
  61.2 2.4 reduce-window.6
  63.6 0.3 slice_reduce_fusion
  63.9 0.4 reduce-window.9
  64.3 0.1 broadcast_add_fusion.1
  64.4 21.1 %collective-permute-done = bf16[16,1,64,512]{3,2,1,0:T(8,128)(2,1)S(1)} collective-permute-done((bf16[16,1,64,512]{3,2,1,0:T(8,128)(2,1)}, bf16[16,1,64,512]{3,2,1,0:T(8,128)(2,1)S(1)}, u32[]{:S(2)}, u32[]{:S(2)}) %collective-permute-start) | collective-permute-done | bytes 1048608 | tf_op jit(solution)/shard_map/ppermute | solution.py:514
  85.5 2.8 pad_maximum_fusion
  88.2 11.3 %all-to-all-done.2.rest_0_ = bf16[16,2,64,512]{3,2,1,0:T(8,128)(2,1)S(1)} async-done(((bf16[16,2,64,512]{3,2,1,0:T(8,128)(2,1)}), bf16[16,2,64,512]{3,2,1,0:T(8,128)(2,1)S(1)}, u32[]{:S(2)}, u32[]{:S(2)}) %all-to-all-start.2) | async-done | bytes 2097184 | tf_op jit(solution)/shard_map/all_to_all | solution.py:511
  99.5 1.3 copy-done.1
  100.8 6.1 %all-to-all-start = ((bf16[16,2,64,512]{3,2,1,0:T(8,128)(2,1)}), bf16[16,2,64,512]{3,2,1,0:T(8,128)(2,1)S(1)}, u32[]{:S(2)}, u32[]{:S(2)}) async-start(bf16[16,2,64,512]{3,2,1,0:T(8,128)(2,1)} %pad_maximum_fusion), calls=%async_computation | async-start | bytes 4194304 | tf_op jit(solution)/shard_map/all_to_all | solution.py:511
  107.0 0.0 copy-done.3
  107.1 0.1 rev.3
  107.2 0.1 fusion
  107.3 0.6 gather_fusion
  107.9 1.1 select_reduce_fusion
  109.0 0.6 gather_fusion.1
  109.5 0.3 collective-permute-start.2
  109.8 0.1 copy_select_fusion
  109.9 0.1 broadcast_select_fusion
  110.0 0.8 slice_reduce_fusion.1.count_ref
  110.8 0.6 fusion.5
  111.4 0.6 slice_bitcast_fusion.1
  112.0 0.6 pad_add_fusion.list_ref
  112.6 0.6 slice_bitcast_fusion.3
  113.1 0.6 slice_bitcast_fusion.list_ref
  113.7 1.2 collective-permute-start.1
  115.0 1.2 pad_add_fusion.1.count_ref
  116.2 0.6 copy.24
  116.8 13.8 %gram.3.rest_2_ = f32[2,512,16,128]{3,2,1,0:T(8,128)} custom-call(s32[2]{0:T(128)} %get-tuple-element.21.count_ref, s32[2,512]{1,0:T(2,128)} %bitcast.28, bf16[16,2,64,512]{3,2,1,0:T(8,128)(2,1)} %copy-done.1), custom_call_target="tpu_custom_call" | custom-call | flops 4294967296 | bytes 16777216 | tf_op jit(solution)/shard_map/gram/pallas_call | solution.py:314
  130.5 26.2 %collective-permute-done.2.rest_1_ = bf16[16,2,64,512]{3,2,1,0:T(8,128)(2,1)} collective-permute-done((bf16[16,2,64,512]{3,2,1,0:T(8,128)(2,1)}, bf16[16,2,64,512]{3,2,1,0:T(8,128)(2,1)}, u32[]{:S(2)}, u32[]{:S(2)}) %collective-permute-start.2) | collective-permute-done | bytes 2097184 | tf_op jit(solution)/shard_map/ppermute | solution.py:514
  156.7 17.8 %gram.4.rest_1_ = f32[2,512,16,128]{3,2,1,0:T(8,128)} custom-call(s32[3]{0:T(128)} %pad_add_fusion.1.count_ref, s32[3,512]{1,0:T(4,128)} %pad_add_fusion.list_ref, bf16[16,1,64,512]{3,2,1,0:T(8,128)(2,1)} %all_to_all.20.rest_0_, bf16[16,2,64,512]{3,2,1,0:T(8,128)(2,1)} %collective-permute-done.2.rest_1_, ...), custom_call_target="tpu_custom_call", output_to_operand_aliasing={{}: (4, {})} | custom-call | flops 6442450944 | bytes 16777216 | tf_op jit(solution)/shard_map/gram/pallas_call | solution.py:314
  174.5 4.6 %collective-permute-done.1.rest_0_ = bf16[16,1,64,512]{3,2,1,0:T(8,128)(2,1)S(1)} collective-permute-done((bf16[16,1,64,512]{3,2,1,0:T(8,128)(2,1)}, bf16[16,1,64,512]{3,2,1,0:T(8,128)(2,1)S(1)}, u32[]{:S(2)}, u32[]{:S(2)}) %collective-permute-start.1) | collective-permute-done | bytes 1048608 | tf_op jit(solution)/shard_map/ppermute | solution.py:514
  179.1 1.0 copy-done.2
  180.1 9.5 %gram.5.grid_ref = f32[2,512,16,128]{3,2,1,0:T(8,128)} custom-call(s32[1]{0:T(128)} %bitcast.4.count_ref, s32[1,512]{1,0:T(1,128)} %get-tuple-element.18.list_ref, bf16[16,1,64,512]{3,2,1,0:T(8,128)(2,1)} %copy-done.2, f32[2,512,16,128]{3,2,1,0:T(8,128)} %gram.4.rest_1_), custom_call_target="tpu_custom_call", output_to_operand_aliasing={{}: (3, {})} | custom-call | flops 2147483648 | bytes 16777216 | tf_op jit(solution)/shard_map/gram/pallas_call | solution.py:314
  189.6 0.0 all-to-all-done.x_ref
  189.6 0.0 copy-start
  189.6 1.3 copy-done
  190.9 17.8 %rows.1 = bf16[16,8,32,512]{3,2,1,0:T(8,128)(2,1)} custom-call(s32[2]{0:T(128)} %slice_reduce_fusion.1.count_ref, s32[2,512]{1,0:T(2,128)} %slice_bitcast_fusion.list_ref, bf16[16,2,64,512]{3,2,1,0:T(8,128)(2,1)} %copy-done, f32[2,512,16,128]{3,2,1,0:T(8,128)} %gram.5.grid_ref, f32[2,32,128]{2,1,0:T(8,128)} %constant.65.clone.twist_ref, ...), custom_call_target="tpu_custom_call" | custom-call | tf_op jit(solution)/shard_map/rows/pallas_call | solution.py:411
  208.7 5.4 %all-to-all-start.3 = ((bf16[16,8,32,512]{3,2,1,0:T(8,128)(2,1)}), bf16[16,8,32,512]{3,2,1,0:T(8,128)(2,1)}, u32[]{:S(2)}, u32[]{:S(2)}) async-start(bf16[16,8,32,512]{3,2,1,0:T(8,128)(2,1)} %rows.1), calls=%async_computation.3 | async-start | bytes 8388608 | tf_op jit(solution)/shard_map/all_to_all | solution.py:511
  214.1 0.7 fusion.1
  214.8 89.5 %all-to-all-done.3.data_ref = bf16[16,8,32,512]{3,2,1,0:T(8,128)(2,1)} async-done(((bf16[16,8,32,512]{3,2,1,0:T(8,128)(2,1)}), bf16[16,8,32,512]{3,2,1,0:T(8,128)(2,1)}, u32[]{:S(2)}, u32[]{:S(2)}) %all-to-all-start.3) | async-done | bytes 4194336 | tf_op jit(solution)/shard_map/all_to_all | solution.py:511
  304.4 11.7 %column.1 = f32[2,8,32,4096]{3,2,1,0:T(8,128)} custom-call(bf16[16,8,32,512]{3,2,1,0:T(8,128)(2,1)} %all-to-all-done.3.data_ref, bf16[512,512]{1,0:T(8,128)(2,1)} %constant.67.clone.first_ref, f32[16,256]{1,0:T(8,128)} %get-tuple-element.27.cos_ref, f32[16,256]{1,0:T(8,128)} %get-tuple-element.26.sin_ref), custom_call_target="tpu_custom_call" | custom-call | tf_op jit(solution)/shard_map/column/pallas_call | solution.py:464
  (15 shorter events, 0.1 us)
Async XLA Ops:
  49.1 50.4 %all-to-all-start.2 = ((bf16[16,2,64,512]{3,2,1,0:T(8,128)(2,1)}), bf16[16,2,64,512]{3,2,1,0:T(8,128)(2,1)S(1)}, u32[]{:S(2)}, u32[]{:S(2)}) async-start(bf16[16,2,64,512]{3,2,1,0:T(8,128)(2,1)} %get-tuple-element.10), calls=%async_computation.2 | async-start | bytes 4194304 | tf_op jit(solution)/shard_map/all_to_all | solution.py:511
  53.5 7.7 %copy-start.4 = (s32[2,2048]{1,0:T(2,128)S(1)}, s32[2,2048]{1,0:T(2,128)}, u32[]{:S(2)}) copy-start(s32[2,2048]{1,0:T(2,128)} %param.12) | copy-start | bytes 49156
  60.9 24.5 %collective-permute-start = (bf16[16,1,64,512]{3,2,1,0:T(8,128)(2,1)}, bf16[16,1,64,512]{3,2,1,0:T(8,128)(2,1)S(1)}, u32[]{:S(2)}, u32[]{:S(2)}) collective-permute-start(bf16[16,1,64,512]{3,2,1,0:T(8,128)(2,1)} %spectra_second.2), channel_id=1, source_target_pairs={{0,16},{16,0},{1,17},{17,1},{2,18},{18,2},{3,19},{19,3},{4,20},{20... | collective-permute-start | bytes 3145736 | tf_op jit(solution)/shard_map/ppermute | solution.py:514
  64.4 42.6 %copy-start.3 = (s32[2,2048]{1,0:T(2,128)S(1)}, s32[2,2048]{1,0:T(2,128)}, u32[]{:S(2)}) copy-start(s32[2,2048]{1,0:T(2,128)} %param.13) | copy-start | bytes 49156
  99.5 1.3 copy-start.1
  100.8 88.7 %all-to-all-start = ((bf16[16,2,64,512]{3,2,1,0:T(8,128)(2,1)}), bf16[16,2,64,512]{3,2,1,0:T(8,128)(2,1)S(1)}, u32[]{:S(2)}, u32[]{:S(2)}) async-start(bf16[16,2,64,512]{3,2,1,0:T(8,128)(2,1)} %pad_maximum_fusion), calls=%async_computation | async-start | bytes 4194304 | tf_op jit(solution)/shard_map/all_to_all | solution.py:511
  109.5 47.2 %collective-permute-start.2 = (bf16[16,2,64,512]{3,2,1,0:T(8,128)(2,1)}, bf16[16,2,64,512]{3,2,1,0:T(8,128)(2,1)}, u32[]{:S(2)}, u32[]{:S(2)}) collective-permute-start(bf16[16,2,64,512]{3,2,1,0:T(8,128)(2,1)} %copy-done.1), channel_id=1, source_target_pairs={{0,16},{16,0},{1,17},{17,1},{2,18},{18,2},{3,19},{19,3},{4,20},{20... | collective-permute-start | bytes 6291464 | tf_op jit(solution)/shard_map/ppermute | solution.py:514
  113.7 65.3 %collective-permute-start.1 = (bf16[16,1,64,512]{3,2,1,0:T(8,128)(2,1)}, bf16[16,1,64,512]{3,2,1,0:T(8,128)(2,1)S(1)}, u32[]{:S(2)}, u32[]{:S(2)}) collective-permute-start(bf16[16,1,64,512]{3,2,1,0:T(8,128)(2,1)} %all_to_all.20.rest_0_), channel_id=1, source_target_pairs={{0,16},{16,0},{1,17},{17,1},{2,18},{18,2},{3,19},{19,3},{4,20},{20... | collective-permute-start | bytes 3145736 | tf_op jit(solution)/shard_map/ppermute | solution.py:514
  179.1 1.0 copy-start.2
  189.6 1.3 copy-start
  208.7 95.6 %all-to-all-start.3 = ((bf16[16,8,32,512]{3,2,1,0:T(8,128)(2,1)}), bf16[16,8,32,512]{3,2,1,0:T(8,128)(2,1)}, u32[]{:S(2)}, u32[]{:S(2)}) async-start(bf16[16,8,32,512]{3,2,1,0:T(8,128)(2,1)} %rows.1), calls=%async_computation.3 | async-start | bytes 8388608 | tf_op jit(solution)/shard_map/all_to_all | solution.py:511

commit v3 on v2

--- a/solution.py
+++ b/solution.py
@@ -142,36 +142,40 @@
                 out_ref[d, o, :, t * FRADIX : (t + 1) * FRADIX] = piece.astype(BF16)
 
 
-def second_stage(pair, high_ref, low_ref, second_ref, scratch):
+PIECES = 4
+LEAD = 4
+
+
+def spectra_kernel(n_gx, *refs):
+    v_refs, (first_ref, twist_ref, second_ref, out_ref, high, low, scratch) = refs[:PIECES], refs[PIECES:]
     rows = second_ref.shape[0]
     stride = scratch.shape[0] // PACK
     two = 2 * FRADIX
-    high = high_ref[2 * pair : 2 * pair + 2].reshape(two, two)
-    low = low_ref[2 * pair : 2 * pair + 2].reshape(two, two)
-    z = dot_nt(second_ref[...], jnp.concatenate([high, high, low], axis=1))
-    scratch[2 * pair * stride : 2 * pair * stride + rows, :] = z[:, :FRADIX]
-    scratch[(2 * pair + 1) * stride : (2 * pair + 1) * stride + rows, :] = z[:, FRADIX:]
-
-
-def spectra_first_kernel(n_gx, v_ref, first_ref, twist_ref, second_ref, high_ref, low_ref, out_ref, scratch):
-    for pair in range(PACK // 2):
-        v = jnp.concatenate([v_ref[2 * pair], v_ref[2 * pair + 1]], axis=1)
+    share = PACK // PIECES
+
+    def turn_pair(pair):
+        v_ref, at = v_refs[2 * pair // share], 2 * pair % share
+        v = jnp.concatenate([v_ref[at], v_ref[at + 1]], axis=1)
         y = jnp.dot(first_ref[...], jnp.concatenate([v, v], axis=0), preferred_element_type=F32)
         for u in range(2):
             lane = slice(u * FRADIX, (u + 1) * FRADIX)
-            re, im = times((y[:FRADIX, lane], y[FRADIX:, lane]), (twist_ref[0], twist_ref[1]))
-            for part, value in enumerate((re, im)):
-                high, low = split_value(value)
-                high_ref[2 * pair + u, :, part * FRADIX : (part + 1) * FRADIX] = high
-                low_ref[2 * pair + u, :, part * FRADIX : (part + 1) * FRADIX] = low
+            value = times((y[:FRADIX, lane], y[FRADIX:, lane]), (twist_ref[0], twist_ref[1]))
+            at_rows = slice((2 * pair + u) * FRADIX, (2 * pair + u + 1) * FRADIX)
+            for part in range(2):
+                at_lane = slice(part * FRADIX, (part + 1) * FRADIX)
+                high[at_rows, at_lane], low[at_rows, at_lane] = split_value(value[part])
+
+    for pair in range(LEAD):
+        turn_pair(pair)
     for pair in range(PACK // 2):
-        second_stage(pair, high_ref, low_ref, second_ref, scratch)
-    channel_rows(n_gx, scratch, out_ref)
-
-
-def spectra_second_kernel(n_gx, high_ref, low_ref, second_ref, out_ref, scratch):
-    for pair in range(PACK // 2):
-        second_stage(pair, high_ref, low_ref, second_ref, scratch)
+        if pair + LEAD < PACK // 2:
+            turn_pair(pair + LEAD)
+        at_rows = slice(pair * two, (pair + 1) * two)
+        h, l = high[at_rows], low[at_rows]
+        z = dot_nt(second_ref[...], jnp.concatenate([h, h, l], axis=1))
+        for u in range(2):
+            at = (2 * pair + u) * stride
+            scratch[at : at + rows, :] = z[:, u * FRADIX : (u + 1) * FRADIX]
     channel_rows(n_gx, scratch, out_ref)
 
 
@@ -179,46 +183,33 @@
     return pl.BlockSpec(x.shape, lambda *i: (0,) * x.ndim)
 
 
-def spectra_call(volts, turned, tables, n_gx, out_dev, start, stop):
+def spectra_call(volts, tables, n_gx, out_dev, start, stop):
     first, twist, second = tables
     per = 2 * FRADIX // out_dev
     second = second[start * per : stop * per]
     depth = 2 * AVG
     channels = stop - start
-    lead = volts if turned is None else turned[0]
-    inputs = lead.shape[0]
-    turned_shape = jax.ShapeDtypeStruct((inputs, FRADIX, 2 * FRADIX), BF16)
-    turned_spec = pl.BlockSpec((PACK, FRADIX, 2 * FRADIX), lambda i: (i, 0, 0))
-    out_spec = pl.BlockSpec((n_gx, channels, PACK, depth), lambda i: (0, 0, i, 0))
-    out_shape = jax.ShapeDtypeStruct((n_gx, channels, inputs, depth), BF16)
-    scratch = [pltpu.VMEM((PACK * (channels * per + SUB), FRADIX), F32)]
-    if turned is None:
-        return pl.pallas_call(
-            functools.partial(spectra_first_kernel, n_gx),
-            grid=(inputs // PACK,),
-            in_specs=[
-                pl.BlockSpec((PACK, 2 * FRADIX, FRADIX), lambda i: (i, 0, 0)),
-                whole(first),
-                whole(twist),
-                whole(second),
-            ],
-            out_specs=[turned_spec, turned_spec, out_spec],
-            out_shape=[turned_shape, turned_shape, out_shape],
-            scratch_shapes=scratch,
-            name="spectra_first",
-        )(volts, first, twist, second)
+    inputs = volts.shape[0]
     return pl.pallas_call(
-        functools.partial(spectra_second_kernel, n_gx),
+        functools.partial(spectra_kernel, n_gx),
         grid=(inputs // PACK,),
-        in_specs=[turned_spec, turned_spec, whole(second)],
-        out_specs=out_spec,
-        out_shape=out_shape,
-        scratch_shapes=scratch,
-        name="spectra_second",
-    )(*turned, second)
-
-
-def correlate(x_ref, slot, vis, factor):
+        in_specs=[
+            pl.BlockSpec((PACK // PIECES, 2 * FRADIX, FRADIX), lambda i, p=p: (i * PIECES + p, 0, 0))
+            for p in range(PIECES)
+        ]
+        + [whole(first), whole(twist), whole(second)],
+        out_specs=pl.BlockSpec((n_gx, channels, PACK, depth), lambda i: (0, 0, i, 0)),
+        out_shape=jax.ShapeDtypeStruct((n_gx, channels, inputs, depth), BF16),
+        scratch_shapes=[
+            pltpu.VMEM((PACK * FRADIX, 2 * FRADIX), BF16),
+            pltpu.VMEM((PACK * FRADIX, 2 * FRADIX), BF16),
+            pltpu.VMEM((PACK * (channels * per + SUB), FRADIX), F32),
+        ],
+        name="spectra",
+    )(*[volts] * PIECES, first, twist, second)
+
+
+def correlate(x_ref, slot, vis, factor, unroll):
     sources, _, inputs, depth = x_ref.shape
     nin = sources * inputs
     half = depth // 2
@@ -237,7 +228,7 @@
             vis[1, e, pl.ds(base, panel), :] = gram[panel:, e * BC : (e + 1) * BC]
         return carry
 
-    lax.fori_loop(0, sources // group, one, 0)
+    lax.fori_loop(0, sources // group, one, 0, unroll=unroll)
 
 
 def place_blocks(which, count_ref, list_ref, vis, grid):
@@ -287,7 +278,7 @@
     which = 0
     for x_ref, many in zip(x_refs, slots):
         for slot in range(many):
-            correlate(x_ref, slot, vis, factor)
+            correlate(x_ref, slot, vis, factor, False)
             if which == 0 and not first_call:
                 for load in loads:
                     load.wait()
@@ -357,8 +348,26 @@
                 turned[block, at, part * BC : (part + 1) * BC] = both.astype(BF16)
 
 
+SENDS = 4
+
+
 def rows_kernel(
-    factor, count_ref, list_ref, x_ref, grid_ref, twist_ref, second_ref, out_ref, vis, grid, stage, turned, scratch, sems
+    factor,
+    count_ref,
+    list_ref,
+    x_ref,
+    grid_ref,
+    twist_ref,
+    second_ref,
+    out_ref,
+    vis,
+    grid,
+    stage,
+    turned,
+    scratch,
+    ready,
+    sems,
+    out_sems,
 ):
     blocks = turned.shape[0]
     lanes = SUB * BR
@@ -371,7 +380,7 @@
         for load in loads:
             load.start()
         for slot in range(x_ref.shape[1]):
-            correlate(x_ref, slot, vis, factor)
+            correlate(x_ref, slot, vis, factor, True)
             if slot == 0:
                 for load in loads:
                     load.wait()
@@ -392,12 +401,40 @@
             at = (2 * b + u) * stride
             scratch[at : at + rows, :] = z[:, u * lanes : (u + 1) * lanes]
     n_gx, lows, _, _ = out_ref.shape
+    share = n_gx // SENDS
+
+    def sends(at_step):
+        slot = lax.rem(at_step, 2)
+        at_out = pl.ds(pl.multiple_of(at_step * lanes, lanes), lanes)
+        copies = []
+        for i in range(SENDS):
+            at = pl.ds(i * share, share)
+            copies.append(pltpu.make_async_copy(ready.at[slot, at], out_ref.at[at, :, :, at_out], out_sems.at[slot, i]))
+        return copies
+
+    steps = pl.num_programs(0)
+    slot = lax.rem(step, 2)
+
+    @pl.when(step >= 2)
+    def _():
+        for copy in sends(step - 2):
+            copy.wait()
+
+    mine = sends(step)
     for d in range(n_gx):
         for k in range(lows):
             for part in range(2):
                 row = (d * lows + k) * 2 + part
                 piece = scratch[pl.ds(row, blocks, stride=stride), :]
-                out_ref[d, k, part * blocks : (part + 1) * blocks, :] = piece.astype(BF16)
+                ready[slot, d, k, part * blocks : (part + 1) * blocks, :] = piece.astype(BF16)
+        if d % share == share - 1:
+            mine[d // share].start()
+
+    @pl.when(step == steps - 1)
+    def _():
+        for at_step in (steps - 2, steps - 1):
+            for copy in sends(at_step):
+                copy.wait()
 
 
 def rows_call(counts, lists, stream, grid, cells, factor, twist, second, n_gx):
@@ -414,12 +451,12 @@
         in_specs=[
             smem,
             smem,
-            whole(stream),
-            pl.BlockSpec(memory_space=pl.ANY),
+            pl.BlockSpec(memory_space=pltpu.VMEM),
+            pl.BlockSpec(memory_space=pltpu.HBM),
             whole(twist),
             whole(second),
         ],
-        out_specs=pl.BlockSpec((n_gx, lows, 2 * blocks, lanes), lambda i: (0, 0, 0, i)),
+        out_specs=pl.BlockSpec(memory_space=pltpu.HBM),
         out_shape=jax.ShapeDtypeStruct((n_gx, lows, 2 * blocks, cols * BR), BF16),
         scratch_shapes=[
             pltpu.VMEM((2, nin // BC, nin, BC), BF16),
@@ -427,35 +464,74 @@
             pltpu.VMEM((BR // SUB, 2, cols, SUB, BC), F32),
             pltpu.VMEM((blocks, cols * BR, 2 * BC), BF16),
             pltpu.VMEM((blocks * (2 * BC + SUB), lanes), F32),
+            pltpu.VMEM((2, n_gx, lows, 2 * blocks, lanes), BF16),
             pltpu.SemaphoreType.DMA((LOADS,)),
+            pltpu.SemaphoreType.DMA((2, SENDS)),
         ],
+        compiler_params=pltpu.CompilerParams(vmem_limit_bytes=48 * 2**20),
         name="rows",
     )(counts, lists, stream, grid, twist, second)
 
 
-def column_kernel(data_ref, first_ref, cos_ref, sin_ref, out_ref, scratch):
+def column_kernel(data_ref, first_ref, cos_ref, sin_ref, out_ref, scratch, ready, out_sems):
     n_gx, _, rows, lanes = data_ref.shape
     count = TILE // BR
-    mixed = dot_tn(data_ref[:, 0].reshape(n_gx * rows, lanes), first_ref[...])
-    for b in range(2 * count // BC):
-        scratch[b * lanes : (b + 1) * lanes, :] = mixed[:, b * BC : (b + 1) * BC]
-    for g in range(lanes // (SUB * BR)):
+    span = SUB * BR
+
+    def mix(g):
+        data = data_ref[:, 0, :, g * span : (g + 1) * span].reshape(n_gx * rows, span)
+        mixed = dot_tn(data, first_ref[...])
+        for b in range(2 * count // BC):
+            scratch[g, b * span : (b + 1) * span, :] = mixed[:, b * BC : (b + 1) * BC]
+
+    step = pl.program_id(0)
+    steps = pl.num_programs(0)
+    slot = lax.rem(step, 2)
+    groups = lanes // (SUB * BR)
+
+    def sends(at_step):
+        at_slot = lax.rem(at_step, 2)
+        copies = []
+        for g in range(groups):
+            at = pl.ds(g * SUB, SUB)
+            for part in range(2):
+                source, target = ready.at[at_slot, part, at], out_ref.at[part, at_step, at]
+                copies.append(pltpu.make_async_copy(source, target, out_sems.at[at_slot, 2 * g + part]))
+        return copies
+
+    @pl.when(step >= 2)
+    def _():
+        for copy in sends(step - 2):
+            copy.wait()
+
+    mine = sends(step)
+    mix(0)
+    for g in range(groups):
+        if g + 1 < groups:
+            mix(g + 1)
         for b in range(count // BC):
             lane = slice(b * BC, (b + 1) * BC)
             values = []
             for r in range(BR):
-                at = g * SUB * BR + r
                 value = (
-                    scratch[pl.ds(b * lanes + at, SUB, stride=BR), :],
-                    scratch[pl.ds((count // BC + b) * lanes + at, SUB, stride=BR), :],
+                    scratch[g, pl.ds(b * span + r, SUB, stride=BR), :],
+                    scratch[g, pl.ds((count // BC + b) * span + r, SUB, stride=BR), :],
                 )
                 factor = (cos_ref[r : r + 1, lane], sin_ref[r : r + 1, lane])
                 values.append(times(value, factor) if r else value)
             values = butterflies(values, 1.0)
             for k in range(BR):
                 at = slice(k * count + b * BC, k * count + (b + 1) * BC)
-                out_ref[0, 0, g * SUB : (g + 1) * SUB, at] = values[k][0]
-                out_ref[1, 0, g * SUB : (g + 1) * SUB, at] = values[k][1]
+                for part in range(2):
+                    ready[slot, part, g * SUB : (g + 1) * SUB, at] = values[k][part]
+        mine[2 * g].start()
+        mine[2 * g + 1].start()
+
+    @pl.when(step == steps - 1)
+    def _():
+        for at_step in (steps - 2, steps - 1):
+            for copy in sends(at_step):
+                copy.wait()
 
 
 def column_call(data, first, cos, sin):
@@ -470,9 +546,13 @@
             whole(cos),
             whole(sin),
         ],
-        out_specs=pl.BlockSpec((2, 1, cols, TILE), lambda i: (0, i, 0, 0)),
+        out_specs=pl.BlockSpec(memory_space=pl.ANY),
         out_shape=jax.ShapeDtypeStruct((2, lows, cols, TILE), F32),
-        scratch_shapes=[pltpu.VMEM((2 * (TILE // BR) // BC * lanes, BC), F32)],
+        scratch_shapes=[
+            pltpu.VMEM((cols // SUB, 2 * (TILE // BR) // BC * SUB * BR, BC), F32),
+            pltpu.VMEM((2, 2, cols, TILE), F32),
+            pltpu.SemaphoreType.DMA((2, 2 * cols // SUB)),
+        ],
         name="column",
     )(data, first, cos, sin)
 
@@ -519,12 +599,11 @@
         streams = [data for _, _, _, data in items]
         return gram_call(number, list_of, streams, grid, cells, factor)
 
-    high, low, spec_a = spectra_call(volts, None, tables, n_gx, out_dev, front, middle)
-    turned = (high, low)
+    spec_a = spectra_call(volts, tables, n_gx, out_dev, front, middle)
     mine_a = exchange(spec_a)
-    spec_c = spectra_call(None, turned, tables, n_gx, out_dev, last, out_dev)
+    spec_c = spectra_call(volts, tables, n_gx, out_dev, last, out_dev)
     other_c = swap_groups(spec_c)
-    spec_b = spectra_call(None, turned, tables, n_gx, out_dev, middle, last)
+    spec_b = spectra_call(volts, tables, n_gx, out_dev, middle, last)
     other_a = swap_groups(mine_a)
     mine_b = exchange(spec_b)
     grid = work(None, (0, front, middle, mine_a))

time: 320 us -> 308 us (0.963)
  blocking collectives: 32 us -> 0 us
  waiting for transfers between devices: 153 us -> 167 us
  starting transfers between devices: 17.6 us -> 24.6 us
    all_to_all x1 -> x0, blocking collectives: 32 us -> none  [exchange(): return lax.all_to_all(spec, 'gx', split_axis=0, concat_axis=0, tiled=True)]
    all_to_all x3 -> x4, waiting for transfers between devices: 101 us -> 114 us  [exchange(): return lax.all_to_all(spec, 'gx', split_axis=0, concat_axis=0, tiled=True)]
    all_to_all x3 -> x4, starting transfers between devices: 15.9 us -> 22.8 us  [exchange(): return lax.all_to_all(spec, 'gx', split_axis=0, concat_axis=0, tiled=True)]
    pallas_call x3, Pallas kernels: 24.5 us -> 28.4 us  [spectra_call(): pl.pallas_call(functools.partial(spectra_kernel, n_gx), grid=(inputs // P...]
  transfers between devices with their start and end apart: 6 -> 7, of which waited for: 5 -> 6; matrix products, arithmetic and copies ran while one was open for 5% -> 5% of each run, Pallas kernels for 15% -> 20%
where the time goes in v3:
time: 308 us; the launch traced here: 304 us
  waiting for transfers between devices  167 us (54%)
  Pallas kernels  95.9 us (31%)
  starting transfers between devices  24.6 us (8%)
  other arithmetic  9.63 us (3%)
  local copies, waits for them, and re-layouts  7.46 us (2%)
    all_to_all x4, waiting for transfers between devices, exchange(): return lax.all_to_all(spec, 'gx', split_axis=0, concat_axis=0, tiled=True)  114 us
    ppermute x3, waiting for transfers between devices, swap_groups(): return lax.ppermute(data, 'grp', [(0, 1), (1, 0)])  52.4 us
    pallas_call x3, Pallas kernels, gram_call(): pl.pallas_call(functools.partial(gram_kernel, slots, first_call, factor),...  41.2 us
    pallas_call x3, Pallas kernels, spectra_call(): pl.pallas_call(functools.partial(spectra_kernel, n_gx), grid=(inputs // P...  28.4 us
    all_to_all x4, starting transfers between devices, exchange(): return lax.all_to_all(spec, 'gx', split_axis=0, concat_axis=0, tiled=True)  22.8 us
    pallas_call x1, Pallas kernels, rows_call(): pl.pallas_call(functools.partial(rows_kernel, factor), grid=(cols // SUB,...  15.9 us
    pallas_call x1, Pallas kernels, column_call(): pl.pallas_call(column_kernel, grid=(lows,), in_specs=[pl.BlockSpec((n_gx,...  10.4 us
  transfers between devices with their start and end apart: 7, of which 6 were waited for; matrix products, arithmetic and copies ran while one was open for 5% of the time, Pallas kernels for 20%

profile of v3, /device:TPU:13, one launch (start us, length us, event | category | flops | bytes accessed | tf_op | source)
XLA Modules:
  0.0 304.4 jit_solution(11820327496680213393)
XLA Ops:
  0.0 9.3 %spectra.4 = bf16[16,1,64,512]{3,2,1,0:T(8,128)(2,1)} custom-call(bf16[64,256,128]{2,1,0:T(8,128)(2,1)} %bitcast.25, bf16[64,256,128]{2,1,0:T(8,128)(2,1)} %bitcast.26, bf16[64,256,128]{2,1,0:T(8,128)(2,1)} %bitcast.27, bf16[64,256,128]{2,1,0:T(8,128)(2,1)} %bitcast.28, bf16[256,512]{1,0:T(8,128)(2,1)} %constant.60.clone.refs_4_, ...), custom_call_target="tpu_custom_call" | custom-call | tf_op jit(solution)/shard_map/spectra/pallas_call | solution.py:193
  9.3 6.5 %all-to-all-start.1 = ((bf16[16,1,64,512]{3,2,1,0:T(8,128)(2,1)}), bf16[16,1,64,512]{3,2,1,0:T(8,128)(2,1)S(1)}, u32[]{:S(2)}, u32[]{:S(2)}) async-start(bf16[16,1,64,512]{3,2,1,0:T(8,128)(2,1)} %spectra.4), calls=%async_computation.1 | async-start | bytes 2097152 | tf_op jit(solution)/shard_map/all_to_all | solution.py:591
  15.9 9.8 %spectra.5 = bf16[16,2,64,512]{3,2,1,0:T(8,128)(2,1)} custom-call(bf16[64,256,128]{2,1,0:T(8,128)(2,1)} %bitcast.29, bf16[64,256,128]{2,1,0:T(8,128)(2,1)} %bitcast.30, bf16[64,256,128]{2,1,0:T(8,128)(2,1)} %bitcast.31, bf16[64,256,128]{2,1,0:T(8,128)(2,1)} %bitcast.32, bf16[256,512]{1,0:T(8,128)(2,1)} %constant.60.clone.refs_4_, ...), custom_call_target="tpu_custom_call" | custom-call | tf_op jit(solution)/shard_map/spectra/pallas_call | solution.py:193
  25.6 15.1 %all-to-all-done.1.rest_0_ = bf16[16,1,64,512]{3,2,1,0:T(8,128)(2,1)S(1)} async-done(((bf16[16,1,64,512]{3,2,1,0:T(8,128)(2,1)}), bf16[16,1,64,512]{3,2,1,0:T(8,128)(2,1)S(1)}, u32[]{:S(2)}, u32[]{:S(2)}) %all-to-all-start.1) | async-done | bytes 1048608 | tf_op jit(solution)/shard_map/all_to_all | solution.py:591
  40.8 1.0 copy-done.4
  41.8 4.8 %all-to-all-start.2 = ((bf16[16,2,64,512]{3,2,1,0:T(8,128)(2,1)}), bf16[16,2,64,512]{3,2,1,0:T(8,128)(2,1)S(1)}, u32[]{:S(2)}, u32[]{:S(2)}) async-start(bf16[16,2,64,512]{3,2,1,0:T(8,128)(2,1)} %spectra.5), calls=%async_computation.2 | async-start | bytes 4194304 | tf_op jit(solution)/shard_map/all_to_all | solution.py:591
  46.5 9.3 %spectra.3 = bf16[16,1,64,512]{3,2,1,0:T(8,128)(2,1)} custom-call(bf16[64,256,128]{2,1,0:T(8,128)(2,1)} %bitcast.33, bf16[64,256,128]{2,1,0:T(8,128)(2,1)} %bitcast.34, bf16[64,256,128]{2,1,0:T(8,128)(2,1)} %bitcast.35, bf16[64,256,128]{2,1,0:T(8,128)(2,1)} %bitcast.36, bf16[256,512]{1,0:T(8,128)(2,1)} %constant.60.clone.refs_4_, ...), custom_call_target="tpu_custom_call" | custom-call | tf_op jit(solution)/shard_map/spectra/pallas_call | solution.py:193
  55.9 0.2 collective-permute-start
  56.1 0.0 copy-done.6
  56.1 2.4 reduce-window.6
  58.6 0.3 slice_reduce_fusion
  58.9 0.4 reduce-window.9
  59.2 0.1 broadcast_add_fusion.1
  59.3 21.1 %collective-permute-done = bf16[16,1,64,512]{3,2,1,0:T(8,128)(2,1)S(1)} collective-permute-done((bf16[16,1,64,512]{3,2,1,0:T(8,128)(2,1)}, bf16[16,1,64,512]{3,2,1,0:T(8,128)(2,1)S(1)}, u32[]{:S(2)}, u32[]{:S(2)}) %collective-permute-start) | collective-permute-done | bytes 1048608 | tf_op jit(solution)/shard_map/ppermute | solution.py:594
  80.4 2.8 pad_maximum_fusion
  83.2 9.5 %all-to-all-done.2.rest_0_ = bf16[16,2,64,512]{3,2,1,0:T(8,128)(2,1)S(1)} async-done(((bf16[16,2,64,512]{3,2,1,0:T(8,128)(2,1)}), bf16[16,2,64,512]{3,2,1,0:T(8,128)(2,1)S(1)}, u32[]{:S(2)}, u32[]{:S(2)}) %all-to-all-start.2) | async-done | bytes 2097184 | tf_op jit(solution)/shard_map/all_to_all | solution.py:591
  92.6 1.3 copy-done.2
  93.9 6.1 %all-to-all-start = ((bf16[16,2,64,512]{3,2,1,0:T(8,128)(2,1)}), bf16[16,2,64,512]{3,2,1,0:T(8,128)(2,1)S(1)}, u32[]{:S(2)}, u32[]{:S(2)}) async-start(bf16[16,2,64,512]{3,2,1,0:T(8,128)(2,1)} %pad_maximum_fusion), calls=%async_computation | async-start | bytes 4194304 | tf_op jit(solution)/shard_map/all_to_all | solution.py:591
  100.1 0.1 rev.3
  100.3 0.1 fusion
  100.4 1.1 select_reduce_fusion
  101.5 0.6 gather_fusion.1
  102.1 0.3 collective-permute-start.2
  102.4 0.1 copy_select_fusion
  102.5 0.6 gather_fusion
  103.0 0.1 broadcast_select_fusion
  103.1 0.2 slice_reduce_fusion.1.count_ref
  103.3 0.6 fusion.5
  103.9 0.6 slice_bitcast_fusion.1
  104.4 0.6 pad_add_fusion.list_ref
  105.0 0.6 slice_bitcast_fusion.3
  105.6 1.2 collective-permute-start.1
  106.9 1.3 pad_add_fusion.1.count_ref
  108.2 0.6 copy.24
  108.8 13.8 %gram.3.rest_2_ = f32[2,512,16,128]{3,2,1,0:T(8,128)} custom-call(s32[2]{0:T(128)} %get-tuple-element.15.count_ref, s32[2,512]{1,0:T(2,128)} %bitcast.39, bf16[16,2,64,512]{3,2,1,0:T(8,128)(2,1)} %copy-done.2), custom_call_target="tpu_custom_call" | custom-call | flops 4294967296 | bytes 16777216 | tf_op jit(solution)/shard_map/gram/pallas_call | solution.py:305
  122.5 26.7 %collective-permute-done.2.rest_1_ = bf16[16,2,64,512]{3,2,1,0:T(8,128)(2,1)} collective-permute-done((bf16[16,2,64,512]{3,2,1,0:T(8,128)(2,1)}, bf16[16,2,64,512]{3,2,1,0:T(8,128)(2,1)}, u32[]{:S(2)}, u32[]{:S(2)}) %collective-permute-start.2) | collective-permute-done | bytes 2097184 | tf_op jit(solution)/shard_map/ppermute | solution.py:594
  149.2 17.8 %gram.4.rest_1_ = f32[2,512,16,128]{3,2,1,0:T(8,128)} custom-call(s32[3]{0:T(128)} %pad_add_fusion.1.count_ref, s32[3,512]{1,0:T(4,128)} %pad_add_fusion.list_ref, bf16[16,1,64,512]{3,2,1,0:T(8,128)(2,1)} %copy-done.4, bf16[16,2,64,512]{3,2,1,0:T(8,128)(2,1)} %collective-permute-done.2.rest_1_, ...), custom_call_target="tpu_custom_call", output_to_operand_aliasing={{}: (4, {})} | custom-call | flops 6442450944 | bytes 16777216 | tf_op jit(solution)/shard_map/gram/pallas_call | solution.py:305
  167.0 4.6 %collective-permute-done.1.rest_0_ = bf16[16,1,64,512]{3,2,1,0:T(8,128)(2,1)S(1)} collective-permute-done((bf16[16,1,64,512]{3,2,1,0:T(8,128)(2,1)}, bf16[16,1,64,512]{3,2,1,0:T(8,128)(2,1)S(1)}, u32[]{:S(2)}, u32[]{:S(2)}) %collective-permute-start.1) | collective-permute-done | bytes 1048608 | tf_op jit(solution)/shard_map/ppermute | solution.py:594
  171.6 1.0 copy-done.3
  172.6 9.7 %gram.5.grid_ref = f32[2,512,16,128]{3,2,1,0:T(8,128)} custom-call(s32[1]{0:T(128)} %bitcast.4.count_ref, s32[1,512]{1,0:T(1,128)} %get-tuple-element.12.list_ref, bf16[16,1,64,512]{3,2,1,0:T(8,128)(2,1)} %copy-done.3, f32[2,512,16,128]{3,2,1,0:T(8,128)} %gram.4.rest_1_), custom_call_target="tpu_custom_call", output_to_operand_aliasing={{}: (3, {})} | custom-call | flops 2147483648 | bytes 16777216 | tf_op jit(solution)/shard_map/gram/pallas_call | solution.py:305
  182.3 0.0 all-to-all-done.x_ref
  182.3 0.0 copy-done
  182.3 0.0 copy-done.1
  182.3 15.9 %rows.1 = bf16[16,8,32,512]{3,2,1,0:T(8,128)(2,1)} custom-call(s32[2]{0:T(128)S(1)} %slice_reduce_fusion.1.count_ref, s32[2,512]{1,0:T(2,128)S(1)} %slice_bitcast_fusion.list_ref, bf16[16,2,64,512]{3,2,1,0:T(8,128)(2,1)S(1)} %all-to-all-done.x_ref, f32[2,512,16,128]{3,2,1,0:T(8,128)} %gram.5.grid_ref, f32[2,32,128]{2,1,0:T(8,128)S(1)} %copy-done.1, ...), custom_call_target="tpu_custom_call" | custom-call | tf_op jit(solution)/shard_map/rows/pallas_call | solution.py:448
  198.2 5.4 %all-to-all-start.3 = ((bf16[16,8,32,512]{3,2,1,0:T(8,128)(2,1)}), bf16[16,8,32,512]{3,2,1,0:T(8,128)(2,1)}, u32[]{:S(2)}, u32[]{:S(2)}) async-start(bf16[16,8,32,512]{3,2,1,0:T(8,128)(2,1)} %rows.1), calls=%async_computation.3 | async-start | bytes 8388608 | tf_op jit(solution)/shard_map/all_to_all | solution.py:591
  203.6 0.7 fusion.1
  204.3 89.5 %all-to-all-done.3.data_ref = bf16[16,8,32,512]{3,2,1,0:T(8,128)(2,1)} async-done(((bf16[16,8,32,512]{3,2,1,0:T(8,128)(2,1)}), bf16[16,8,32,512]{3,2,1,0:T(8,128)(2,1)}, u32[]{:S(2)}, u32[]{:S(2)}) %all-to-all-start.3) | async-done | bytes 4194336 | tf_op jit(solution)/shard_map/all_to_all | solution.py:591
  293.9 10.4 %column.1 = f32[2,8,32,4096]{3,2,1,0:T(8,128)} custom-call(bf16[16,8,32,512]{3,2,1,0:T(8,128)(2,1)} %all-to-all-done.3.data_ref, bf16[512,512]{1,0:T(8,128)(2,1)} %constant.67.clone.first_ref, f32[16,256]{1,0:T(8,128)} %get-tuple-element.21.cos_ref, f32[16,256]{1,0:T(8,128)} %get-tuple-element.20.sin_ref), custom_call_target="tpu_custom_call" | custom-call | tf_op jit(solution)/shard_map/column/pallas_call | solution.py:540
  (20 shorter events, 0.2 us)
Async XLA Ops:
  9.3 31.5 %all-to-all-start.1 = ((bf16[16,1,64,512]{3,2,1,0:T(8,128)(2,1)}), bf16[16,1,64,512]{3,2,1,0:T(8,128)(2,1)S(1)}, u32[]{:S(2)}, u32[]{:S(2)}) async-start(bf16[16,1,64,512]{3,2,1,0:T(8,128)(2,1)} %spectra.4), calls=%async_computation.1 | async-start | bytes 2097152 | tf_op jit(solution)/shard_map/all_to_all | solution.py:591
  40.8 1.0 copy-start.4
  41.8 50.8 %all-to-all-start.2 = ((bf16[16,2,64,512]{3,2,1,0:T(8,128)(2,1)}), bf16[16,2,64,512]{3,2,1,0:T(8,128)(2,1)S(1)}, u32[]{:S(2)}, u32[]{:S(2)}) async-start(bf16[16,2,64,512]{3,2,1,0:T(8,128)(2,1)} %spectra.5), calls=%async_computation.2 | async-start | bytes 4194304 | tf_op jit(solution)/shard_map/all_to_all | solution.py:591
  46.5 9.6 %copy-start.6 = (s32[2,2048]{1,0:T(2,128)S(1)}, s32[2,2048]{1,0:T(2,128)}, u32[]{:S(2)}) copy-start(s32[2,2048]{1,0:T(2,128)} %param.12) | copy-start | bytes 49156
  55.9 24.5 %collective-permute-start = (bf16[16,1,64,512]{3,2,1,0:T(8,128)(2,1)}, bf16[16,1,64,512]{3,2,1,0:T(8,128)(2,1)S(1)}, u32[]{:S(2)}, u32[]{:S(2)}) collective-permute-start(bf16[16,1,64,512]{3,2,1,0:T(8,128)(2,1)} %spectra.3), channel_id=1, source_target_pairs={{0,16},{16,0},{1,17},{17,1},{2,18},{18,2},{3,19},{19,3},{4,20},{20... | collective-permute-start | bytes 3145736 | tf_op jit(solution)/shard_map/ppermute | solution.py:594
  59.3 40.8 %copy-start.5 = (s32[2,2048]{1,0:T(2,128)S(1)}, s32[2,2048]{1,0:T(2,128)}, u32[]{:S(2)}) copy-start(s32[2,2048]{1,0:T(2,128)} %param.13) | copy-start | bytes 49156
  92.6 1.3 copy-start.2
  93.9 88.3 %all-to-all-start = ((bf16[16,2,64,512]{3,2,1,0:T(8,128)(2,1)}), bf16[16,2,64,512]{3,2,1,0:T(8,128)(2,1)S(1)}, u32[]{:S(2)}, u32[]{:S(2)}) async-start(bf16[16,2,64,512]{3,2,1,0:T(8,128)(2,1)} %pad_maximum_fusion), calls=%async_computation | async-start | bytes 4194304 | tf_op jit(solution)/shard_map/all_to_all | solution.py:591
  102.1 47.2 %collective-permute-start.2 = (bf16[16,2,64,512]{3,2,1,0:T(8,128)(2,1)}, bf16[16,2,64,512]{3,2,1,0:T(8,128)(2,1)}, u32[]{:S(2)}, u32[]{:S(2)}) collective-permute-start(bf16[16,2,64,512]{3,2,1,0:T(8,128)(2,1)} %copy-done.2), channel_id=1, source_target_pairs={{0,16},{16,0},{1,17},{17,1},{2,18},{18,2},{3,19},{19,3},{4,20},{20... | collective-permute-start | bytes 6291464 | tf_op jit(solution)/shard_map/ppermute | solution.py:594
  105.6 66.0 %collective-permute-start.1 = (bf16[16,1,64,512]{3,2,1,0:T(8,128)(2,1)}, bf16[16,1,64,512]{3,2,1,0:T(8,128)(2,1)S(1)}, u32[]{:S(2)}, u32[]{:S(2)}) collective-permute-start(bf16[16,1,64,512]{3,2,1,0:T(8,128)(2,1)} %copy-done.4), channel_id=1, source_target_pairs={{0,16},{16,0},{1,17},{17,1},{2,18},{18,2},{3,19},{19,3},{4,20},{20... | collective-permute-start | bytes 3145736 | tf_op jit(solution)/shard_map/ppermute | solution.py:594
  171.6 1.0 copy-start.3
  172.6 9.7 %copy-start = (bf16[256,256]{1,0:T(8,128)(2,1)S(1)}, bf16[256,256]{1,0:T(8,128)(2,1)}, u32[]{:S(2)}) copy-start(bf16[256,256]{1,0:T(8,128)(2,1)} %constant.66.clone.second_ref) | copy-start | bytes 393220
  172.6 9.7 %copy-start.1 = (f32[2,32,128]{2,1,0:T(8,128)S(1)}, f32[2,32,128]{2,1,0:T(8,128)}, u32[]{:S(2)}) copy-start(f32[2,32,128]{2,1,0:T(8,128)} %constant.65.clone.twist_ref) | copy-start | bytes 98308
  198.2 95.6 %all-to-all-start.3 = ((bf16[16,8,32,512]{3,2,1,0:T(8,128)(2,1)}), bf16[16,8,32,512]{3,2,1,0:T(8,128)(2,1)}, u32[]{:S(2)}, u32[]{:S(2)}) async-start(bf16[16,8,32,512]{3,2,1,0:T(8,128)(2,1)} %rows.1), calls=%async_computation.3 | async-start | bytes 8388608 | tf_op jit(solution)/shard_map/all_to_all | solution.py:591

commit v4 on v3

--- a/solution.py
+++ b/solution.py
@@ -132,7 +132,7 @@
 
 
 def channel_rows(n_gx, scratch, out_ref):
-    stride = scratch.shape[0] // PACK
+    stride = scratch.shape[0] // (PACK + 1)
     channels = out_ref.shape[1]
     per = out_ref.shape[3] // FRADIX
     for o in range(channels):
@@ -149,7 +149,7 @@
 def spectra_kernel(n_gx, *refs):
     v_refs, (first_ref, twist_ref, second_ref, out_ref, high, low, scratch) = refs[:PIECES], refs[PIECES:]
     rows = second_ref.shape[0]
-    stride = scratch.shape[0] // PACK
+    stride = scratch.shape[0] // (PACK + 1)
     two = 2 * FRADIX
     share = PACK // PIECES
 
@@ -203,7 +203,7 @@
         scratch_shapes=[
             pltpu.VMEM((PACK * FRADIX, 2 * FRADIX), BF16),
             pltpu.VMEM((PACK * FRADIX, 2 * FRADIX), BF16),
-            pltpu.VMEM((PACK * (channels * per + SUB), FRADIX), F32),
+            pltpu.VMEM(((PACK + 1) * (channels * per + SUB), FRADIX), F32),
         ],
         name="spectra",
     )(*[volts] * PIECES, first, twist, second)
@@ -392,7 +392,7 @@
 
         lax.fori_loop(0, blocks, one, 0)
 
-    stride = scratch.shape[0] // blocks
+    stride = scratch.shape[0] // (blocks + 1)
     at_lane = pl.ds(pl.multiple_of(step * lanes, lanes), lanes)
     for b in range(blocks // 2):
         data = turned[2 * b : 2 * b + 2, at_lane].reshape(2 * lanes, rows)
@@ -463,7 +463,7 @@
             pltpu.VMEM((2, cells, BR, BC), F32),
             pltpu.VMEM((BR // SUB, 2, cols, SUB, BC), F32),
             pltpu.VMEM((blocks, cols * BR, 2 * BC), BF16),
-            pltpu.VMEM((blocks * (2 * BC + SUB), lanes), F32),
+            pltpu.VMEM(((blocks + 1) * (2 * BC + SUB), lanes), F32),
             pltpu.VMEM((2, n_gx, lows, 2 * blocks, lanes), BF16),
             pltpu.SemaphoreType.DMA((LOADS,)),
             pltpu.SemaphoreType.DMA((2, SENDS)),
@@ -549,7 +549,7 @@
         out_specs=pl.BlockSpec(memory_space=pl.ANY),
         out_shape=jax.ShapeDtypeStruct((2, lows, cols, TILE), F32),
         scratch_shapes=[
-            pltpu.VMEM((cols // SUB, 2 * (TILE // BR) // BC * SUB * BR, BC), F32),
+            pltpu.VMEM((cols // SUB, (2 * (TILE // BR) // BC + 1) * SUB * BR, BC), F32),
             pltpu.VMEM((2, 2, cols, TILE), F32),
             pltpu.SemaphoreType.DMA((2, 2 * cols // SUB)),
         ],

time: 308 us -> 308 us (level)
  no operation moved by 1% of the time
where the time goes in v4:
time: 308 us; the launch traced here: 304 us
  waiting for transfers between devices  167 us (54%)
  Pallas kernels  95.9 us (31%)
  starting transfers between devices  24.6 us (8%)
  other arithmetic  9.63 us (3%)
  local copies, waits for them, and re-layouts  7.46 us (2%)
    all_to_all x4, waiting for transfers between devices, exchange(): return lax.all_to_all(spec, 'gx', split_axis=0, concat_axis=0, tiled=True)  114 us
    ppermute x3, waiting for transfers between devices, swap_groups(): return lax.ppermute(data, 'grp', [(0, 1), (1, 0)])  52.4 us
    pallas_call x3, Pallas kernels, gram_call(): pl.pallas_call(functools.partial(gram_kernel, slots, first_call, factor),...  41.2 us
    pallas_call x3, Pallas kernels, spectra_call(): pl.pallas_call(functools.partial(spectra_kernel, n_gx), grid=(inputs // P...  28.4 us
    all_to_all x4, starting transfers between devices, exchange(): return lax.all_to_all(spec, 'gx', split_axis=0, concat_axis=0, tiled=True)  22.8 us
    pallas_call x1, Pallas kernels, rows_call(): pl.pallas_call(functools.partial(rows_kernel, factor), grid=(cols // SUB,...  15.9 us
    pallas_call x1, Pallas kernels, column_call(): pl.pallas_call(column_kernel, grid=(lows,), in_specs=[pl.BlockSpec((n_gx,...  10.4 us
  transfers between devices with their start and end apart: 7, of which 6 were waited for; matrix products, arithmetic and copies ran while one was open for 5% of the time, Pallas kernels for 20%

profile of v4, /device:TPU:13, one launch (start us, length us, event | category | flops | bytes accessed | tf_op | source)
XLA Modules:
  0.0 304.4 jit_solution(7166192505352728289)
XLA Ops:
  0.0 9.3 %spectra.4 = bf16[16,1,64,512]{3,2,1,0:T(8,128)(2,1)} custom-call(bf16[64,256,128]{2,1,0:T(8,128)(2,1)} %bitcast.25, bf16[64,256,128]{2,1,0:T(8,128)(2,1)} %bitcast.26, bf16[64,256,128]{2,1,0:T(8,128)(2,1)} %bitcast.27, bf16[64,256,128]{2,1,0:T(8,128)(2,1)} %bitcast.28, bf16[256,512]{1,0:T(8,128)(2,1)} %constant.60.clone.refs_4_, ...), custom_call_target="tpu_custom_call" | custom-call | tf_op jit(solution)/shard_map/spectra/pallas_call | solution.py:193
  9.3 6.5 %all-to-all-start.1 = ((bf16[16,1,64,512]{3,2,1,0:T(8,128)(2,1)}), bf16[16,1,64,512]{3,2,1,0:T(8,128)(2,1)S(1)}, u32[]{:S(2)}, u32[]{:S(2)}) async-start(bf16[16,1,64,512]{3,2,1,0:T(8,128)(2,1)} %spectra.4), calls=%async_computation.1 | async-start | bytes 2097152 | tf_op jit(solution)/shard_map/all_to_all | solution.py:591
  15.9 9.8 %spectra.5 = bf16[16,2,64,512]{3,2,1,0:T(8,128)(2,1)} custom-call(bf16[64,256,128]{2,1,0:T(8,128)(2,1)} %bitcast.29, bf16[64,256,128]{2,1,0:T(8,128)(2,1)} %bitcast.30, bf16[64,256,128]{2,1,0:T(8,128)(2,1)} %bitcast.31, bf16[64,256,128]{2,1,0:T(8,128)(2,1)} %bitcast.32, bf16[256,512]{1,0:T(8,128)(2,1)} %constant.60.clone.refs_4_, ...), custom_call_target="tpu_custom_call" | custom-call | tf_op jit(solution)/shard_map/spectra/pallas_call | solution.py:193
  25.7 15.1 %all-to-all-done.1.rest_0_ = bf16[16,1,64,512]{3,2,1,0:T(8,128)(2,1)S(1)} async-done(((bf16[16,1,64,512]{3,2,1,0:T(8,128)(2,1)}), bf16[16,1,64,512]{3,2,1,0:T(8,128)(2,1)S(1)}, u32[]{:S(2)}, u32[]{:S(2)}) %all-to-all-start.1) | async-done | bytes 1048608 | tf_op jit(solution)/shard_map/all_to_all | solution.py:591
  40.8 1.0 copy-done.4
  41.8 4.8 %all-to-all-start.2 = ((bf16[16,2,64,512]{3,2,1,0:T(8,128)(2,1)}), bf16[16,2,64,512]{3,2,1,0:T(8,128)(2,1)S(1)}, u32[]{:S(2)}, u32[]{:S(2)}) async-start(bf16[16,2,64,512]{3,2,1,0:T(8,128)(2,1)} %spectra.5), calls=%async_computation.2 | async-start | bytes 4194304 | tf_op jit(solution)/shard_map/all_to_all | solution.py:591
  46.5 9.3 %spectra.3 = bf16[16,1,64,512]{3,2,1,0:T(8,128)(2,1)} custom-call(bf16[64,256,128]{2,1,0:T(8,128)(2,1)} %bitcast.33, bf16[64,256,128]{2,1,0:T(8,128)(2,1)} %bitcast.34, bf16[64,256,128]{2,1,0:T(8,128)(2,1)} %bitcast.35, bf16[64,256,128]{2,1,0:T(8,128)(2,1)} %bitcast.36, bf16[256,512]{1,0:T(8,128)(2,1)} %constant.60.clone.refs_4_, ...), custom_call_target="tpu_custom_call" | custom-call | tf_op jit(solution)/shard_map/spectra/pallas_call | solution.py:193
  55.9 0.2 collective-permute-start
  56.1 0.0 copy-done.6
  56.1 2.4 reduce-window.6
  58.6 0.3 slice_reduce_fusion
  58.9 0.4 reduce-window.9
  59.2 0.1 broadcast_add_fusion.1
  59.3 21.1 %collective-permute-done = bf16[16,1,64,512]{3,2,1,0:T(8,128)(2,1)S(1)} collective-permute-done((bf16[16,1,64,512]{3,2,1,0:T(8,128)(2,1)}, bf16[16,1,64,512]{3,2,1,0:T(8,128)(2,1)S(1)}, u32[]{:S(2)}, u32[]{:S(2)}) %collective-permute-start) | collective-permute-done | bytes 1048608 | tf_op jit(solution)/shard_map/ppermute | solution.py:594
  80.4 2.8 pad_maximum_fusion
  83.2 9.5 %all-to-all-done.2.rest_0_ = bf16[16,2,64,512]{3,2,1,0:T(8,128)(2,1)S(1)} async-done(((bf16[16,2,64,512]{3,2,1,0:T(8,128)(2,1)}), bf16[16,2,64,512]{3,2,1,0:T(8,128)(2,1)S(1)}, u32[]{:S(2)}, u32[]{:S(2)}) %all-to-all-start.2) | async-done | bytes 2097184 | tf_op jit(solution)/shard_map/all_to_all | solution.py:591
  92.6 1.3 copy-done.2
  93.9 6.1 %all-to-all-start = ((bf16[16,2,64,512]{3,2,1,0:T(8,128)(2,1)}), bf16[16,2,64,512]{3,2,1,0:T(8,128)(2,1)S(1)}, u32[]{:S(2)}, u32[]{:S(2)}) async-start(bf16[16,2,64,512]{3,2,1,0:T(8,128)(2,1)} %pad_maximum_fusion), calls=%async_computation | async-start | bytes 4194304 | tf_op jit(solution)/shard_map/all_to_all | solution.py:591
  100.1 0.1 rev.3
  100.3 0.1 fusion
  100.4 1.1 select_reduce_fusion
  101.5 0.6 gather_fusion.1
  102.1 0.3 collective-permute-start.2
  102.4 0.1 copy_select_fusion
  102.5 0.6 gather_fusion
  103.0 0.1 broadcast_select_fusion
  103.1 0.2 slice_reduce_fusion.1.count_ref
  103.3 0.6 fusion.5
  103.9 0.6 slice_bitcast_fusion.1
  104.4 0.6 pad_add_fusion.list_ref
  105.0 0.6 slice_bitcast_fusion.3
  105.6 1.2 collective-permute-start.1
  106.9 1.3 pad_add_fusion.1.count_ref
  108.2 0.6 copy.24
  108.8 13.8 %gram.3.rest_2_ = f32[2,512,16,128]{3,2,1,0:T(8,128)} custom-call(s32[2]{0:T(128)} %get-tuple-element.15.count_ref, s32[2,512]{1,0:T(2,128)} %bitcast.39, bf16[16,2,64,512]{3,2,1,0:T(8,128)(2,1)} %copy-done.2), custom_call_target="tpu_custom_call" | custom-call | flops 4294967296 | bytes 16777216 | tf_op jit(solution)/shard_map/gram/pallas_call | solution.py:305
  122.5 26.7 %collective-permute-done.2.rest_1_ = bf16[16,2,64,512]{3,2,1,0:T(8,128)(2,1)} collective-permute-done((bf16[16,2,64,512]{3,2,1,0:T(8,128)(2,1)}, bf16[16,2,64,512]{3,2,1,0:T(8,128)(2,1)}, u32[]{:S(2)}, u32[]{:S(2)}) %collective-permute-start.2) | collective-permute-done | bytes 2097184 | tf_op jit(solution)/shard_map/ppermute | solution.py:594
  149.2 17.7 %gram.4.rest_1_ = f32[2,512,16,128]{3,2,1,0:T(8,128)} custom-call(s32[3]{0:T(128)} %pad_add_fusion.1.count_ref, s32[3,512]{1,0:T(4,128)} %pad_add_fusion.list_ref, bf16[16,1,64,512]{3,2,1,0:T(8,128)(2,1)} %copy-done.4, bf16[16,2,64,512]{3,2,1,0:T(8,128)(2,1)} %collective-permute-done.2.rest_1_, ...), custom_call_target="tpu_custom_call", output_to_operand_aliasing={{}: (4, {})} | custom-call | flops 6442450944 | bytes 16777216 | tf_op jit(solution)/shard_map/gram/pallas_call | solution.py:305
  167.0 4.6 %collective-permute-done.1.rest_0_ = bf16[16,1,64,512]{3,2,1,0:T(8,128)(2,1)S(1)} collective-permute-done((bf16[16,1,64,512]{3,2,1,0:T(8,128)(2,1)}, bf16[16,1,64,512]{3,2,1,0:T(8,128)(2,1)S(1)}, u32[]{:S(2)}, u32[]{:S(2)}) %collective-permute-start.1) | collective-permute-done | bytes 1048608 | tf_op jit(solution)/shard_map/ppermute | solution.py:594
  171.6 1.0 copy-done.3
  172.6 9.7 %gram.5.grid_ref = f32[2,512,16,128]{3,2,1,0:T(8,128)} custom-call(s32[1]{0:T(128)} %bitcast.4.count_ref, s32[1,512]{1,0:T(1,128)} %get-tuple-element.12.list_ref, bf16[16,1,64,512]{3,2,1,0:T(8,128)(2,1)} %copy-done.3, f32[2,512,16,128]{3,2,1,0:T(8,128)} %gram.4.rest_1_), custom_call_target="tpu_custom_call", output_to_operand_aliasing={{}: (3, {})} | custom-call | flops 2147483648 | bytes 16777216 | tf_op jit(solution)/shard_map/gram/pallas_call | solution.py:305
  182.3 0.0 all-to-all-done.x_ref
  182.3 0.0 copy-done
  182.3 0.0 copy-done.1
  182.3 15.9 %rows.1 = bf16[16,8,32,512]{3,2,1,0:T(8,128)(2,1)} custom-call(s32[2]{0:T(128)S(1)} %slice_reduce_fusion.1.count_ref, s32[2,512]{1,0:T(2,128)S(1)} %slice_bitcast_fusion.list_ref, bf16[16,2,64,512]{3,2,1,0:T(8,128)(2,1)S(1)} %all-to-all-done.x_ref, f32[2,512,16,128]{3,2,1,0:T(8,128)} %gram.5.grid_ref, f32[2,32,128]{2,1,0:T(8,128)S(1)} %copy-done.1, ...), custom_call_target="tpu_custom_call" | custom-call | tf_op jit(solution)/shard_map/rows/pallas_call | solution.py:448
  198.2 5.4 %all-to-all-start.3 = ((bf16[16,8,32,512]{3,2,1,0:T(8,128)(2,1)}), bf16[16,8,32,512]{3,2,1,0:T(8,128)(2,1)}, u32[]{:S(2)}, u32[]{:S(2)}) async-start(bf16[16,8,32,512]{3,2,1,0:T(8,128)(2,1)} %rows.1), calls=%async_computation.3 | async-start | bytes 8388608 | tf_op jit(solution)/shard_map/all_to_all | solution.py:591
  203.6 0.7 fusion.1
  204.3 89.5 %all-to-all-done.3.data_ref = bf16[16,8,32,512]{3,2,1,0:T(8,128)(2,1)} async-done(((bf16[16,8,32,512]{3,2,1,0:T(8,128)(2,1)}), bf16[16,8,32,512]{3,2,1,0:T(8,128)(2,1)}, u32[]{:S(2)}, u32[]{:S(2)}) %all-to-all-start.3) | async-done | bytes 4194336 | tf_op jit(solution)/shard_map/all_to_all | solution.py:591
  293.8 10.4 %column.1 = f32[2,8,32,4096]{3,2,1,0:T(8,128)} custom-call(bf16[16,8,32,512]{3,2,1,0:T(8,128)(2,1)} %all-to-all-done.3.data_ref, bf16[512,512]{1,0:T(8,128)(2,1)} %constant.67.clone.first_ref, f32[16,256]{1,0:T(8,128)} %get-tuple-element.21.cos_ref, f32[16,256]{1,0:T(8,128)} %get-tuple-element.20.sin_ref), custom_call_target="tpu_custom_call" | custom-call | tf_op jit(solution)/shard_map/column/pallas_call | solution.py:540
  (20 shorter events, 0.2 us)
Async XLA Ops:
  9.3 31.5 %all-to-all-start.1 = ((bf16[16,1,64,512]{3,2,1,0:T(8,128)(2,1)}), bf16[16,1,64,512]{3,2,1,0:T(8,128)(2,1)S(1)}, u32[]{:S(2)}, u32[]{:S(2)}) async-start(bf16[16,1,64,512]{3,2,1,0:T(8,128)(2,1)} %spectra.4), calls=%async_computation.1 | async-start | bytes 2097152 | tf_op jit(solution)/shard_map/all_to_all | solution.py:591
  40.8 1.0 copy-start.4
  41.8 50.8 %all-to-all-start.2 = ((bf16[16,2,64,512]{3,2,1,0:T(8,128)(2,1)}), bf16[16,2,64,512]{3,2,1,0:T(8,128)(2,1)S(1)}, u32[]{:S(2)}, u32[]{:S(2)}) async-start(bf16[16,2,64,512]{3,2,1,0:T(8,128)(2,1)} %spectra.5), calls=%async_computation.2 | async-start | bytes 4194304 | tf_op jit(solution)/shard_map/all_to_all | solution.py:591
  46.5 9.6 %copy-start.6 = (s32[2,2048]{1,0:T(2,128)S(1)}, s32[2,2048]{1,0:T(2,128)}, u32[]{:S(2)}) copy-start(s32[2,2048]{1,0:T(2,128)} %param.12) | copy-start | bytes 49156
  55.9 24.5 %collective-permute-start = (bf16[16,1,64,512]{3,2,1,0:T(8,128)(2,1)}, bf16[16,1,64,512]{3,2,1,0:T(8,128)(2,1)S(1)}, u32[]{:S(2)}, u32[]{:S(2)}) collective-permute-start(bf16[16,1,64,512]{3,2,1,0:T(8,128)(2,1)} %spectra.3), channel_id=1, source_target_pairs={{0,16},{16,0},{1,17},{17,1},{2,18},{18,2},{3,19},{19,3},{4,20},{20... | collective-permute-start | bytes 3145736 | tf_op jit(solution)/shard_map/ppermute | solution.py:594
  59.3 40.8 %copy-start.5 = (s32[2,2048]{1,0:T(2,128)S(1)}, s32[2,2048]{1,0:T(2,128)}, u32[]{:S(2)}) copy-start(s32[2,2048]{1,0:T(2,128)} %param.13) | copy-start | bytes 49156
  92.6 1.3 copy-start.2
  93.9 88.3 %all-to-all-start = ((bf16[16,2,64,512]{3,2,1,0:T(8,128)(2,1)}), bf16[16,2,64,512]{3,2,1,0:T(8,128)(2,1)S(1)}, u32[]{:S(2)}, u32[]{:S(2)}) async-start(bf16[16,2,64,512]{3,2,1,0:T(8,128)(2,1)} %pad_maximum_fusion), calls=%async_computation | async-start | bytes 4194304 | tf_op jit(solution)/shard_map/all_to_all | solution.py:591
  102.1 47.2 %collective-permute-start.2 = (bf16[16,2,64,512]{3,2,1,0:T(8,128)(2,1)}, bf16[16,2,64,512]{3,2,1,0:T(8,128)(2,1)}, u32[]{:S(2)}, u32[]{:S(2)}) collective-permute-start(bf16[16,2,64,512]{3,2,1,0:T(8,128)(2,1)} %copy-done.2), channel_id=1, source_target_pairs={{0,16},{16,0},{1,17},{17,1},{2,18},{18,2},{3,19},{19,3},{4,20},{20... | collective-permute-start | bytes 6291464 | tf_op jit(solution)/shard_map/ppermute | solution.py:594
  105.6 66.0 %collective-permute-start.1 = (bf16[16,1,64,512]{3,2,1,0:T(8,128)(2,1)}, bf16[16,1,64,512]{3,2,1,0:T(8,128)(2,1)S(1)}, u32[]{:S(2)}, u32[]{:S(2)}) collective-permute-start(bf16[16,1,64,512]{3,2,1,0:T(8,128)(2,1)} %copy-done.4), channel_id=1, source_target_pairs={{0,16},{16,0},{1,17},{17,1},{2,18},{18,2},{3,19},{19,3},{4,20},{20... | collective-permute-start | bytes 3145736 | tf_op jit(solution)/shard_map/ppermute | solution.py:594
  171.6 1.0 copy-start.3
  172.6 9.7 %copy-start = (bf16[256,256]{1,0:T(8,128)(2,1)S(1)}, bf16[256,256]{1,0:T(8,128)(2,1)}, u32[]{:S(2)}) copy-start(bf16[256,256]{1,0:T(8,128)(2,1)} %constant.66.clone.second_ref) | copy-start | bytes 393220
  172.6 9.7 %copy-start.1 = (f32[2,32,128]{2,1,0:T(8,128)S(1)}, f32[2,32,128]{2,1,0:T(8,128)}, u32[]{:S(2)}) copy-start(f32[2,32,128]{2,1,0:T(8,128)} %constant.65.clone.twist_ref) | copy-start | bytes 98308
  198.2 95.6 %all-to-all-start.3 = ((bf16[16,8,32,512]{3,2,1,0:T(8,128)(2,1)}), bf16[16,8,32,512]{3,2,1,0:T(8,128)(2,1)}, u32[]{:S(2)}, u32[]{:S(2)}) async-start(bf16[16,8,32,512]{3,2,1,0:T(8,128)(2,1)} %rows.1), calls=%async_computation.3 | async-start | bytes 8388608 | tf_op jit(solution)/shard_map/all_to_all | solution.py:591

commit v5 on v4

--- a/solution.py
+++ b/solution.py
@@ -231,16 +231,21 @@
     lax.fori_loop(0, sources // group, one, 0, unroll=unroll)
 
 
+def parts_of(number, size):
+    if size & (size - 1):
+        return lax.div(number, size), lax.rem(number, size)
+    return lax.shift_right_logical(number, size.bit_length() - 1), number & (size - 1)
+
+
 def place_blocks(which, count_ref, list_ref, vis, grid):
     cells = grid.shape[1]
     wide = vis.shape[1]
 
     def place(s, carry):
         code = list_ref[which, s]
-        cell = lax.rem(code, cells)
-        block = lax.div(code, cells)
-        e = lax.rem(block, wide)
-        row = pl.multiple_of(lax.div(block, wide) * BR, BR)
+        block, cell = parts_of(code, cells)
+        high, e = parts_of(block, wide)
+        row = pl.multiple_of(high * BR, BR)
         for part in range(2):
             grid[part, cell] += vis[part, e, pl.ds(row, BR), :].astype(F32)
         return carry
@@ -473,13 +478,15 @@
     )(counts, lists, stream, grid, twist, second)
 
 
-def column_kernel(data_ref, first_ref, cos_ref, sin_ref, out_ref, scratch, ready, out_sems):
-    n_gx, _, rows, lanes = data_ref.shape
+def column_kernel(data_a, data_b, data_c, data_d, first_ref, cos_ref, sin_ref, out_ref, scratch, ready, out_sems):
+    pieces = (data_a, data_b, data_c, data_d)
+    share, _, rows, lanes = data_a.shape
     count = TILE // BR
     span = SUB * BR
 
     def mix(g):
-        data = data_ref[:, 0, :, g * span : (g + 1) * span].reshape(n_gx * rows, span)
+        at = slice(g * span, (g + 1) * span)
+        data = jnp.concatenate([x[:, 0, :, at].reshape(share * rows, span) for x in pieces], axis=0)
         mixed = dot_tn(data, first_ref[...])
         for b in range(2 * count // BC):
             scratch[g, b * span : (b + 1) * span, :] = mixed[:, b * BC : (b + 1) * BC]
@@ -541,7 +548,7 @@
         column_kernel,
         grid=(lows,),
         in_specs=[
-            pl.BlockSpec((n_gx, 1, rows, lanes), lambda i: (0, i, 0, 0)),
+            *[pl.BlockSpec((n_gx // 4, 1, rows, lanes), lambda i, p=p: (p, i, 0, 0)) for p in range(4)],
             whole(first),
             whole(cos),
             whole(sin),
@@ -554,7 +561,7 @@
             pltpu.SemaphoreType.DMA((2, 2 * cols // SUB)),
         ],
         name="column",
-    )(data, first, cos, sin)
+    )(data, data, data, data, first, cos, sin)
 
 
 def work_lists(tile_of, cell_of, me, out_dev, cells):

time: 308 us -> 308 us (level)
  transfers between devices with their start and end apart: 7 -> 7, of which waited for: 6 -> 6; matrix products, arithmetic and copies ran while one was open for 5% -> 5% of each run, Pallas kernels for 20% -> 19%
where the time goes in v5:
time: 308 us; the launch traced here: 304 us
  waiting for transfers between devices  168 us (55%)
  Pallas kernels  94 us (31%)
  starting transfers between devices  25 us (8%)
  other arithmetic  9.63 us (3%)
  local copies, waits for them, and re-layouts  7.46 us (2%)
    all_to_all x4, waiting for transfers between devices, exchange(): return lax.all_to_all(spec, 'gx', split_axis=0, concat_axis=0, tiled=True)  114 us
    ppermute x3, waiting for transfers between devices, swap_groups(): return lax.ppermute(data, 'grp', [(0, 1), (1, 0)])  53.8 us
    pallas_call x3, Pallas kernels, gram_call(): pl.pallas_call(functools.partial(gram_kernel, slots, first_call, factor),...  39.5 us
    pallas_call x3, Pallas kernels, spectra_call(): pl.pallas_call(functools.partial(spectra_kernel, n_gx), grid=(inputs // P...  28.4 us
    all_to_all x4, starting transfers between devices, exchange(): return lax.all_to_all(spec, 'gx', split_axis=0, concat_axis=0, tiled=True)  23.2 us
    pallas_call x1, Pallas kernels, rows_call(): pl.pallas_call(functools.partial(rows_kernel, factor), grid=(cols // SUB,...  15.4 us
    pallas_call x1, Pallas kernels, column_call(): pl.pallas_call(column_kernel, grid=(lows,), in_specs=[*[pl.BlockSpec((n_g...  10.6 us
  transfers between devices with their start and end apart: 7, of which 6 were waited for; matrix products, arithmetic and copies ran while one was open for 5% of the time, Pallas kernels for 19%

profile of v5, /device:TPU:13, one launch (start us, length us, event | category | flops | bytes accessed | tf_op | source)
XLA Modules:
  0.0 304.2 jit_solution(12024729586854165928)
XLA Ops:
  0.0 9.3 %spectra.4 = bf16[16,1,64,512]{3,2,1,0:T(8,128)(2,1)} custom-call(bf16[64,256,128]{2,1,0:T(8,128)(2,1)} %bitcast.25, bf16[64,256,128]{2,1,0:T(8,128)(2,1)} %bitcast.26, bf16[64,256,128]{2,1,0:T(8,128)(2,1)} %bitcast.27, bf16[64,256,128]{2,1,0:T(8,128)(2,1)} %bitcast.28, bf16[256,512]{1,0:T(8,128)(2,1)} %constant.60.clone.refs_4_, ...), custom_call_target="tpu_custom_call" | custom-call | tf_op jit(solution)/shard_map/spectra/pallas_call | solution.py:193
  9.3 6.5 %all-to-all-start.1 = ((bf16[16,1,64,512]{3,2,1,0:T(8,128)(2,1)}), bf16[16,1,64,512]{3,2,1,0:T(8,128)(2,1)S(1)}, u32[]{:S(2)}, u32[]{:S(2)}) async-start(bf16[16,1,64,512]{3,2,1,0:T(8,128)(2,1)} %spectra.4), calls=%async_computation.1 | async-start | bytes 2097152 | tf_op jit(solution)/shard_map/all_to_all | solution.py:598
  15.9 9.8 %spectra.5 = bf16[16,2,64,512]{3,2,1,0:T(8,128)(2,1)} custom-call(bf16[64,256,128]{2,1,0:T(8,128)(2,1)} %bitcast.29, bf16[64,256,128]{2,1,0:T(8,128)(2,1)} %bitcast.30, bf16[64,256,128]{2,1,0:T(8,128)(2,1)} %bitcast.31, bf16[64,256,128]{2,1,0:T(8,128)(2,1)} %bitcast.32, bf16[256,512]{1,0:T(8,128)(2,1)} %constant.60.clone.refs_4_, ...), custom_call_target="tpu_custom_call" | custom-call | tf_op jit(solution)/shard_map/spectra/pallas_call | solution.py:193
  25.7 15.1 %all-to-all-done.1.rest_0_ = bf16[16,1,64,512]{3,2,1,0:T(8,128)(2,1)S(1)} async-done(((bf16[16,1,64,512]{3,2,1,0:T(8,128)(2,1)}), bf16[16,1,64,512]{3,2,1,0:T(8,128)(2,1)S(1)}, u32[]{:S(2)}, u32[]{:S(2)}) %all-to-all-start.1) | async-done | bytes 1048608 | tf_op jit(solution)/shard_map/all_to_all | solution.py:598
  40.8 1.0 copy-done.4
  41.8 4.8 %all-to-all-start.2 = ((bf16[16,2,64,512]{3,2,1,0:T(8,128)(2,1)}), bf16[16,2,64,512]{3,2,1,0:T(8,128)(2,1)S(1)}, u32[]{:S(2)}, u32[]{:S(2)}) async-start(bf16[16,2,64,512]{3,2,1,0:T(8,128)(2,1)} %spectra.5), calls=%async_computation.2 | async-start | bytes 4194304 | tf_op jit(solution)/shard_map/all_to_all | solution.py:598
  46.5 9.3 %spectra.3 = bf16[16,1,64,512]{3,2,1,0:T(8,128)(2,1)} custom-call(bf16[64,256,128]{2,1,0:T(8,128)(2,1)} %bitcast.33, bf16[64,256,128]{2,1,0:T(8,128)(2,1)} %bitcast.34, bf16[64,256,128]{2,1,0:T(8,128)(2,1)} %bitcast.35, bf16[64,256,128]{2,1,0:T(8,128)(2,1)} %bitcast.36, bf16[256,512]{1,0:T(8,128)(2,1)} %constant.60.clone.refs_4_, ...), custom_call_target="tpu_custom_call" | custom-call | tf_op jit(solution)/shard_map/spectra/pallas_call | solution.py:193
  55.9 0.2 collective-permute-start
  56.1 0.0 copy-done.6
  56.1 2.4 reduce-window.6
  58.6 0.3 slice_reduce_fusion
  58.9 0.4 reduce-window.9
  59.2 0.1 broadcast_add_fusion.1
  59.3 21.1 %collective-permute-done = bf16[16,1,64,512]{3,2,1,0:T(8,128)(2,1)S(1)} collective-permute-done((bf16[16,1,64,512]{3,2,1,0:T(8,128)(2,1)}, bf16[16,1,64,512]{3,2,1,0:T(8,128)(2,1)S(1)}, u32[]{:S(2)}, u32[]{:S(2)}) %collective-permute-start) | collective-permute-done | bytes 1048608 | tf_op jit(solution)/shard_map/ppermute | solution.py:601
  80.4 2.8 pad_maximum_fusion
  83.2 9.5 %all-to-all-done.2.rest_0_ = bf16[16,2,64,512]{3,2,1,0:T(8,128)(2,1)S(1)} async-done(((bf16[16,2,64,512]{3,2,1,0:T(8,128)(2,1)}), bf16[16,2,64,512]{3,2,1,0:T(8,128)(2,1)S(1)}, u32[]{:S(2)}, u32[]{:S(2)}) %all-to-all-start.2) | async-done | bytes 2097184 | tf_op jit(solution)/shard_map/all_to_all | solution.py:598
  92.6 1.3 copy-done.2
  93.9 6.1 %all-to-all-start = ((bf16[16,2,64,512]{3,2,1,0:T(8,128)(2,1)}), bf16[16,2,64,512]{3,2,1,0:T(8,128)(2,1)S(1)}, u32[]{:S(2)}, u32[]{:S(2)}) async-start(bf16[16,2,64,512]{3,2,1,0:T(8,128)(2,1)} %pad_maximum_fusion), calls=%async_computation | async-start | bytes 4194304 | tf_op jit(solution)/shard_map/all_to_all | solution.py:598
  100.1 0.0 copy-done.5
  100.1 0.1 rev.3
  100.3 0.1 fusion
  100.4 1.1 select_reduce_fusion
  101.5 0.6 gather_fusion.1
  102.1 0.3 collective-permute-start.2
  102.4 0.1 copy_select_fusion
  102.5 0.6 gather_fusion
  103.0 0.1 broadcast_select_fusion
  103.1 0.2 slice_reduce_fusion.1.count_ref
  103.3 0.6 fusion.5
  103.9 0.6 slice_bitcast_fusion.1
  104.4 0.6 pad_add_fusion.list_ref
  105.0 0.6 slice_bitcast_fusion.3
  105.6 1.2 collective-permute-start.1
  106.9 1.3 pad_add_fusion.1.count_ref
  108.2 0.6 copy.24
  108.8 13.2 %gram.3.rest_2_ = f32[2,512,16,128]{3,2,1,0:T(8,128)} custom-call(s32[2]{0:T(128)} %get-tuple-element.15.count_ref, s32[2,512]{1,0:T(2,128)} %bitcast.39, bf16[16,2,64,512]{3,2,1,0:T(8,128)(2,1)} %copy-done.2), custom_call_target="tpu_custom_call" | custom-call | flops 4294967296 | bytes 16777216 | tf_op jit(solution)/shard_map/gram/pallas_call | solution.py:310
  122.0 27.3 %collective-permute-done.2.rest_1_ = bf16[16,2,64,512]{3,2,1,0:T(8,128)(2,1)} collective-permute-done((bf16[16,2,64,512]{3,2,1,0:T(8,128)(2,1)}, bf16[16,2,64,512]{3,2,1,0:T(8,128)(2,1)}, u32[]{:S(2)}, u32[]{:S(2)}) %collective-permute-start.2) | collective-permute-done | bytes 2097184 | tf_op jit(solution)/shard_map/ppermute | solution.py:601
  149.2 16.9 %gram.4.rest_1_ = f32[2,512,16,128]{3,2,1,0:T(8,128)} custom-call(s32[3]{0:T(128)} %pad_add_fusion.1.count_ref, s32[3,512]{1,0:T(4,128)} %pad_add_fusion.list_ref, bf16[16,1,64,512]{3,2,1,0:T(8,128)(2,1)} %copy-done.4, bf16[16,2,64,512]{3,2,1,0:T(8,128)(2,1)} %collective-permute-done.2.rest_1_, ...), custom_call_target="tpu_custom_call", output_to_operand_aliasing={{}: (4, {})} | custom-call | flops 6442450944 | bytes 16777216 | tf_op jit(solution)/shard_map/gram/pallas_call | solution.py:310
  166.2 5.4 %collective-permute-done.1.rest_0_ = bf16[16,1,64,512]{3,2,1,0:T(8,128)(2,1)S(1)} collective-permute-done((bf16[16,1,64,512]{3,2,1,0:T(8,128)(2,1)}, bf16[16,1,64,512]{3,2,1,0:T(8,128)(2,1)S(1)}, u32[]{:S(2)}, u32[]{:S(2)}) %collective-permute-start.1) | collective-permute-done | bytes 1048608 | tf_op jit(solution)/shard_map/ppermute | solution.py:601
  171.6 1.0 copy-done.3
  172.6 9.4 %gram.5.grid_ref = f32[2,512,16,128]{3,2,1,0:T(8,128)} custom-call(s32[1]{0:T(128)} %bitcast.4.count_ref, s32[1,512]{1,0:T(1,128)} %get-tuple-element.12.list_ref, bf16[16,1,64,512]{3,2,1,0:T(8,128)(2,1)} %copy-done.3, f32[2,512,16,128]{3,2,1,0:T(8,128)} %gram.4.rest_1_), custom_call_target="tpu_custom_call", output_to_operand_aliasing={{}: (3, {})} | custom-call | flops 2147483648 | bytes 16777216 | tf_op jit(solution)/shard_map/gram/pallas_call | solution.py:310
  182.0 0.0 all-to-all-done.x_ref
  182.0 0.0 copy-done
  182.0 15.4 %rows.1 = bf16[16,8,32,512]{3,2,1,0:T(8,128)(2,1)} custom-call(s32[2]{0:T(128)S(1)} %slice_reduce_fusion.1.count_ref, s32[2,512]{1,0:T(2,128)S(1)} %slice_bitcast_fusion.list_ref, bf16[16,2,64,512]{3,2,1,0:T(8,128)(2,1)S(1)} %all-to-all-done.x_ref, f32[2,512,16,128]{3,2,1,0:T(8,128)} %gram.5.grid_ref, f32[2,32,128]{2,1,0:T(8,128)S(1)} %copy-done.1, ...), custom_call_target="tpu_custom_call" | custom-call | tf_op jit(solution)/shard_map/rows/pallas_call | solution.py:453
  197.5 5.8 %all-to-all-start.3 = ((bf16[16,8,32,512]{3,2,1,0:T(8,128)(2,1)}), bf16[16,8,32,512]{3,2,1,0:T(8,128)(2,1)}, u32[]{:S(2)}, u32[]{:S(2)}) async-start(bf16[16,8,32,512]{3,2,1,0:T(8,128)(2,1)} %rows.1), calls=%async_computation.3 | async-start | bytes 8388608 | tf_op jit(solution)/shard_map/all_to_all | solution.py:598
  203.3 0.7 fusion.1
  203.9 89.5 %all-to-all-done.3.data_a.data_b.data_c.data_d = bf16[16,8,32,512]{3,2,1,0:T(8,128)(2,1)} async-done(((bf16[16,8,32,512]{3,2,1,0:T(8,128)(2,1)}), bf16[16,8,32,512]{3,2,1,0:T(8,128)(2,1)}, u32[]{:S(2)}, u32[]{:S(2)}) %all-to-all-start.3) | async-done | bytes 4194336 | tf_op jit(solution)/shard_map/all_to_all | solution.py:598
  293.5 10.6 %column.1 = f32[2,8,32,4096]{3,2,1,0:T(8,128)} custom-call(bf16[16,8,32,512]{3,2,1,0:T(8,128)(2,1)} %all-to-all-done.3.data_a.data_b.data_c.data_d, bf16[16,8,32,512]{3,2,1,0:T(8,128)(2,1)} %all-to-all-done.3.data_a.data_b.data_c.data_d, bf16[16,8,32,512]{3,2,1,0:T(8,128)(2,1)} %all-to-all-done.3.data_a.data_b.data_c.data_d, ...), custom_call_target="tpu_custom_call" | custom-call | tf_op jit(solution)/shard_map/column/pallas_call | solution.py:547
  (20 shorter events, 0.2 us)
Async XLA Ops:
  9.3 31.5 %all-to-all-start.1 = ((bf16[16,1,64,512]{3,2,1,0:T(8,128)(2,1)}), bf16[16,1,64,512]{3,2,1,0:T(8,128)(2,1)S(1)}, u32[]{:S(2)}, u32[]{:S(2)}) async-start(bf16[16,1,64,512]{3,2,1,0:T(8,128)(2,1)} %spectra.4), calls=%async_computation.1 | async-start | bytes 2097152 | tf_op jit(solution)/shard_map/all_to_all | solution.py:598
  40.8 1.0 copy-start.4
  41.8 50.8 %all-to-all-start.2 = ((bf16[16,2,64,512]{3,2,1,0:T(8,128)(2,1)}), bf16[16,2,64,512]{3,2,1,0:T(8,128)(2,1)S(1)}, u32[]{:S(2)}, u32[]{:S(2)}) async-start(bf16[16,2,64,512]{3,2,1,0:T(8,128)(2,1)} %spectra.5), calls=%async_computation.2 | async-start | bytes 4194304 | tf_op jit(solution)/shard_map/all_to_all | solution.py:598
  46.5 9.6 %copy-start.6 = (s32[2,2048]{1,0:T(2,128)S(1)}, s32[2,2048]{1,0:T(2,128)}, u32[]{:S(2)}) copy-start(s32[2,2048]{1,0:T(2,128)} %param.12) | copy-start | bytes 49156
  55.9 24.5 %collective-permute-start = (bf16[16,1,64,512]{3,2,1,0:T(8,128)(2,1)}, bf16[16,1,64,512]{3,2,1,0:T(8,128)(2,1)S(1)}, u32[]{:S(2)}, u32[]{:S(2)}) collective-permute-start(bf16[16,1,64,512]{3,2,1,0:T(8,128)(2,1)} %spectra.3), channel_id=1, source_target_pairs={{0,16},{16,0},{1,17},{17,1},{2,18},{18,2},{3,19},{19,3},{4,20},{20... | collective-permute-start | bytes 3145736 | tf_op jit(solution)/shard_map/ppermute | solution.py:601
  59.3 40.8 %copy-start.5 = (s32[2,2048]{1,0:T(2,128)S(1)}, s32[2,2048]{1,0:T(2,128)}, u32[]{:S(2)}) copy-start(s32[2,2048]{1,0:T(2,128)} %param.13) | copy-start | bytes 49156
  92.6 1.3 copy-start.2
  93.9 88.1 %all-to-all-start = ((bf16[16,2,64,512]{3,2,1,0:T(8,128)(2,1)}), bf16[16,2,64,512]{3,2,1,0:T(8,128)(2,1)S(1)}, u32[]{:S(2)}, u32[]{:S(2)}) async-start(bf16[16,2,64,512]{3,2,1,0:T(8,128)(2,1)} %pad_maximum_fusion), calls=%async_computation | async-start | bytes 4194304 | tf_op jit(solution)/shard_map/all_to_all | solution.py:598
  102.1 47.2 %collective-permute-start.2 = (bf16[16,2,64,512]{3,2,1,0:T(8,128)(2,1)}, bf16[16,2,64,512]{3,2,1,0:T(8,128)(2,1)}, u32[]{:S(2)}, u32[]{:S(2)}) collective-permute-start(bf16[16,2,64,512]{3,2,1,0:T(8,128)(2,1)} %copy-done.2), channel_id=1, source_target_pairs={{0,16},{16,0},{1,17},{17,1},{2,18},{18,2},{3,19},{19,3},{4,20},{20... | collective-permute-start | bytes 6291464 | tf_op jit(solution)/shard_map/ppermute | solution.py:601
  105.6 66.0 %collective-permute-start.1 = (bf16[16,1,64,512]{3,2,1,0:T(8,128)(2,1)}, bf16[16,1,64,512]{3,2,1,0:T(8,128)(2,1)S(1)}, u32[]{:S(2)}, u32[]{:S(2)}) collective-permute-start(bf16[16,1,64,512]{3,2,1,0:T(8,128)(2,1)} %copy-done.4), channel_id=1, source_target_pairs={{0,16},{16,0},{1,17},{17,1},{2,18},{18,2},{3,19},{19,3},{4,20},{20... | collective-permute-start | bytes 3145736 | tf_op jit(solution)/shard_map/ppermute | solution.py:601
  171.6 1.0 copy-start.3
  172.6 9.4 %copy-start = (bf16[256,256]{1,0:T(8,128)(2,1)S(1)}, bf16[256,256]{1,0:T(8,128)(2,1)}, u32[]{:S(2)}) copy-start(bf16[256,256]{1,0:T(8,128)(2,1)} %constant.66.clone.second_ref) | copy-start | bytes 393220
  172.6 9.4 %copy-start.1 = (f32[2,32,128]{2,1,0:T(8,128)S(1)}, f32[2,32,128]{2,1,0:T(8,128)}, u32[]{:S(2)}) copy-start(f32[2,32,128]{2,1,0:T(8,128)} %constant.65.clone.twist_ref) | copy-start | bytes 98308
  197.5 96.0 %all-to-all-start.3 = ((bf16[16,8,32,512]{3,2,1,0:T(8,128)(2,1)}), bf16[16,8,32,512]{3,2,1,0:T(8,128)(2,1)}, u32[]{:S(2)}, u32[]{:S(2)}) async-start(bf16[16,8,32,512]{3,2,1,0:T(8,128)(2,1)} %rows.1), calls=%async_computation.3 | async-start | bytes 8388608 | tf_op jit(solution)/shard_map/all_to_all | solution.py:598
